TPU v7x, 512 devices: a whole 4x8x8 slice. The times are simulated.
512 devices in a mesh: slab: 16 (over z, x_hi), blk: 32 (over y, x_lo, core).
Axes of the slice: x: 4 (x_hi: 2, x_lo: 2; x = x_hi * 2 + x_lo), y: 8, z: 8, core: 2. Of those that a mesh axis runs over, the one named last changes fastest.
Arguments:
- fixed_image: bfloat16 [1024, 512, 128], P('blk', 'slab'), may hold values from -6 to 6
- moving_image: bfloat16 [1024, 512, 128], P('blk', 'slab'), may hold values from -6 to 6
- fetch_owner: int32 [32, 16, 4, 4], P('blk', 'slab'), may hold values from 0 to 31, as said below
- fetch_block: int32 [32, 16, 4, 4], P('blk', 'slab'), may hold values from 0 to 3
- fetch_count: int32 [32, 16, 4], P('blk', 'slab'), may hold values from 1 to 4, as said below
- interp_level: int32 [32, 16, 4, 3, 4], P('blk', 'slab'), may hold values from 0 to 7
- block_mask: int32 [32, 16, 4], P('blk', 'slab'), may hold values 0 or 1
Outputs:
- update: float32 [3, 1024, 512, 128], P(None, 'blk', 'slab')
Inputs may be any that keep to these rules, and one draw needn't show every extreme that they name: `fetch_owner`: entries k < fetch_count of one device's lists name any one owner at most 2 times in all; in every draw some owner is named exactly 2 times by every device of its slab. Entries k >= fetch_count are not read. `fetch_count`: every device has a block whose list holds 4 entries.
All inputs are finite; a program needn't handle non-finite values. No bound on the sum of `block_mask` on one device may be relied on, other than what follows from the above.
Results may differ from a plain program's by a relative error of at most 0.006.
Values may be sent and summed in bfloat16 or wider, within the bound.
No kernel may reach another device: no remote copies, remote signals or barrier semaphores. Data moves between devices by JAX's collectives and lax.ppermute only.
A program may use at most 64 MiB of HBM per device.

v0:
```python
import math

import jax
import jax.numpy as jnp
from jax import lax
from jax.sharding import PartitionSpec as P

LEVELS = 8
BOX_RADIUS = 2
SMOOTH_RADIUS = 3
RIM = BOX_RADIUS + SMOOTH_RADIUS

sigma_smooth = 1.5
step_length = 2.0
var_eps = 1e-05
peak_eps = 1e-06


def smooth_weights(radius):
    raw = [math.exp(-(t * t) / (2.0 * sigma_smooth * sigma_smooth)) for t in range(-radius, radius + 1)]
    total = sum(raw)
    return [one / total for one in raw]


def window_sum(volume, axis_pos, length, weights):
    result = weights[0] * lax.slice_in_dim(volume, 0, length, axis=axis_pos)
    for offset in range(1, len(weights)):
        result = result + weights[offset] * lax.slice_in_dim(volume, offset, offset + length, axis=axis_pos)
    return result


def shift_up(axis):
    n = lax.axis_size(axis)
    return [(i, i + 1) for i in range(n - 1)]


def shift_down(axis):
    n = lax.axis_size(axis)
    return [(i + 1, i) for i in range(n - 1)]


def next_along(a, axis):
    size = a.shape[axis]
    return jnp.concatenate(
        [lax.slice_in_dim(a, 1, size, axis=axis), lax.slice_in_dim(a, size - 1, size, axis=axis)], axis=axis
    )


def request_row(fetch_owner, fetch_block, fetch_count, interp_level):
    blocks, slots = fetch_owner.shape
    in_list = jnp.arange(slots)[None, :] < fetch_count[:, None]
    ids = jnp.where(in_list, fetch_owner * blocks + fetch_block, -1)
    row = jnp.concatenate([ids.reshape(-1), interp_level.reshape(-1), fetch_count.reshape(-1)])
    return jnp.pad(row, (0, 128 - row.shape[0])).astype(jnp.bfloat16)


def coefficients(rows, blocks, slots):
    n = rows.shape[0]
    rows = rows.astype(jnp.float32)
    e = blocks * slots
    ids = rows[:, :e].reshape(n, blocks, slots)
    lev = rows[:, e : 4 * e].reshape(n, blocks, 3, slots)
    count = rows[:, 4 * e : 4 * e + blocks]
    hit = (ids[..., None] == jnp.arange(n * blocks).astype(jnp.float32)).astype(jnp.float32)
    pair = jnp.stack([LEVELS - lev, lev], axis=3)
    wx, wz, wy = pair[:, :, 0], pair[:, :, 1], pair[:, :, 2]
    prod = wz[:, :, :, None, None, :] * wx[:, :, None, :, None, :] * wy[:, :, None, None, :, :]
    c = jnp.sum(prod[..., None] * hit[:, :, None, None, None], axis=5)
    c = c.reshape(n * blocks, 8 * n * blocks)
    hi = jnp.floor(c / 16.0) * 16.0
    both = jnp.concatenate([hi, c - hi], axis=0).astype(jnp.bfloat16)
    return both, (1.0 / count).reshape(n * blocks, 1) / float(LEVELS**3)


def warp(moving_t, row):
    side, _, width = moving_t.shape
    owners = lax.axis_size("blk")
    blocks = width // side
    payload = jnp.concatenate(
        [moving_t, next_along(moving_t, 0), jnp.broadcast_to(row[None, None, :], (side, 2, width))], axis=1
    )
    got = lax.all_to_all(payload, "blk", split_axis=0, concat_axis=0, tiled=True)
    c, scale = coefficients(got[:, 2 * side, :], blocks, 4)
    src = got[:, : 2 * side].reshape(owners, 2, side, blocks, side).transpose(1, 0, 3, 2, 4)
    corners = []
    for dz in range(2):
        for dx in range(2):
            one = src[dz]
            if dx:
                one = next_along(one, 2)
            for dy in range(2):
                corners.append(next_along(one, 3) if dy else one)
    s = jnp.stack(corners).reshape(8 * owners * blocks, side * side)
    acc = jnp.dot(c, s, preferred_element_type=jnp.float32)
    m = owners * blocks
    w = ((acc[:m] + acc[m:]) * scale).astype(jnp.bfloat16)
    w = w.reshape(owners, blocks, side, side).transpose(0, 2, 1, 3).reshape(owners, side, width)
    zero = jnp.zeros((1, RIM, width), jnp.bfloat16)
    before = jnp.concatenate([zero, w[:-1, side - RIM :]], axis=0)
    after = jnp.concatenate([w[1:, :RIM], zero], axis=0)
    w = jnp.concatenate([before, w, after], axis=1)
    return lax.all_to_all(w, "blk", split_axis=0, concat_axis=0, tiled=True)


def per_device(fixed_image, moving_image, fetch_owner, fetch_block, fetch_count, interp_level, block_mask):
    side = fixed_image.shape[0]
    width = fixed_image.shape[2]
    blocks = fetch_count.shape[2]
    ext = side + 2 * RIM
    mid = side + 2 * SMOOTH_RADIUS
    row = request_row(fetch_owner[0, 0], fetch_block[0, 0], fetch_count[0, 0], interp_level[0, 0])
    warped = warp(moving_image.transpose(1, 0, 2), row)

    mask_row = jnp.repeat(block_mask.reshape(blocks), side).astype(jnp.bfloat16)
    fixed_t = fixed_image.transpose(1, 0, 2)
    tail = jnp.concatenate([fixed_t[side - RIM :].reshape(-1, width), mask_row[None]], axis=0)
    head = jnp.concatenate([fixed_t[:RIM].reshape(-1, width), mask_row[None]], axis=0)
    below = lax.ppermute(tail, "slab", shift_up("slab"))
    above = lax.ppermute(head, "slab", shift_down("slab"))
    fixed_z = jnp.concatenate(
        [below[:-1].reshape(RIM, side, width), fixed_t, above[:-1].reshape(RIM, side, width)], axis=0
    )
    masks = jnp.stack([below[-1], mask_row, above[-1]])
    tail = jnp.concatenate([fixed_z[:, side - RIM :].reshape(-1, width), masks], axis=0)
    head = jnp.concatenate([fixed_z[:, :RIM].reshape(-1, width), masks], axis=0)
    left = lax.ppermute(tail, "blk", shift_up("blk"))
    right = lax.ppermute(head, "blk", shift_down("blk"))
    fixed = jnp.concatenate(
        [left[:-3].reshape(ext, RIM, width), fixed_z, right[:-3].reshape(ext, RIM, width)], axis=1
    ).astype(jnp.float32)
    masks = jnp.stack([left[-3:], masks, right[-3:]], axis=1).astype(jnp.float32)
    mask = jnp.repeat(jnp.repeat(masks, jnp.array([SMOOTH_RADIUS, side, SMOOTH_RADIUS]), axis=0, total_repeat_length=mid),
                      jnp.array([SMOOTH_RADIUS, side, SMOOTH_RADIUS]), axis=1, total_repeat_length=mid)

    below = lax.ppermute(warped[side - RIM :], "slab", shift_up("slab"))
    above = lax.ppermute(warped[:RIM], "slab", shift_down("slab"))
    moving = jnp.concatenate([below, warped, above], axis=0).astype(jnp.float32)

    ones = [1.0] * (2 * BOX_RADIUS + 1)
    n = float(len(ones) ** 3)

    def box(a):
        a = window_sum(a, 0, mid, ones)
        a = window_sum(a, 1, mid, ones)
        a = jnp.pad(a, ((0, 0), (0, 0), (BOX_RADIUS, BOX_RADIUS)))
        return window_sum(a, 2, width, ones)

    mean_f = box(fixed) / n
    mean_m = box(moving) / n
    var_f = box(fixed * fixed) / n - mean_f * mean_f + var_eps
    var_m = box(moving * moving) / n - mean_m * mean_m + var_eps
    cov = box(fixed * moving) / n - mean_f * mean_m
    r = BOX_RADIUS
    here = (slice(r, r + mid), slice(r, r + mid))
    grad_z = (moving[r + 1 : r + 1 + mid, here[1]] - moving[r - 1 : r - 1 + mid, here[1]]) * 0.5
    grad_x = (moving[here[0], r + 1 : r + 1 + mid] - moving[here[0], r - 1 : r - 1 + mid]) * 0.5
    padded = jnp.pad(moving[here], ((0, 0), (0, 0), (1, 1)))
    grad_y = (padded[:, :, 2:] - padded[:, :, :-2]) * 0.5
    term = mask * 2.0 * cov / (var_f * var_m) * (fixed[here] - mean_f - cov / var_m * (moving[here] - mean_m))
    force = jnp.stack([term * grad_x, term * grad_z, term * grad_y]).astype(jnp.bfloat16).astype(jnp.float32)
    taps = smooth_weights(SMOOTH_RADIUS)
    s = window_sum(force, 2, side, taps)
    s = window_sum(s, 1, side, taps)
    s = window_sum(jnp.pad(s, ((0, 0), (0, 0), (0, 0), (SMOOTH_RADIUS, SMOOTH_RADIUS))), 3, width, taps)
    peak = jnp.max(jnp.sqrt(s[0] * s[0] + s[1] * s[1] + s[2] * s[2]))
    for axis in ("blk", "slab"):
        tile = jnp.broadcast_to(peak, (lax.axis_size(axis), 1, 128))
        peak = jnp.max(lax.all_to_all(tile, axis, split_axis=0, concat_axis=0, tiled=True))
    return (step_length * s / (peak + peak_eps)).transpose(0, 2, 1, 3)


def solution(mesh):
    in_specs = (
        P("blk", "slab", None),
        P("blk", "slab", None),
        P("blk", "slab", None, None),
        P("blk", "slab", None, None),
        P("blk", "slab", None),
        P("blk", "slab", None, None, None),
        P("blk", "slab", None),
    )
    return jax.shard_map(
        per_device, mesh=mesh, in_specs=in_specs, out_specs=P(None, "blk", "slab", None), check_vma=False
    )
```

profile of v0, /device:TPU:1, one launch (start us, length us, event | category | flops | bytes accessed | tf_op | source)
XLA Modules:
  0.0 181.3 jit_solution(16113411672295632893)
XLA Ops:
  5.2 10.4 %all-to-all-start = ((bf16[32,66,128]{2,1,0:T(8,128)(2,1)}), bf16[32,66,128]{2,1,0:T(8,128)(2,1)S(1)}, u32[]{:S(2)}, u32[]{:S(2)}) async-start(bf16[32,66,128]{2,1,0:T(8,128)(2,1)} %pad_maximum_fusion.2), calls=%async_computation | async-start | bytes 1179648 | tf_op jit(solution)/shard_map/all_to_all | solution.py:82
  15.9 3.6 %collective-permute-start = (bf16[161,128]{1,0:T(8,128)(2,1)S(1)}, bf16[161,128]{1,0:T(8,128)(2,1)S(1)}, u32[]{:S(2)}, u32[]{:S(2)}) collective-permute-start(bf16[161,128]{1,0:T(8,128)(2,1)S(1)} %get-tuple-element.54), channel_id=1, source_target_pairs={{0,32},{32,64},{64,96},{96,128},{128,160},{160,192},{192,224},{224... | collective-permute-start | bytes 123656 | tf_op jit(solution)/shard_map/ppermute | solution.py:118
  22.3 4.1 %collective-permute-done.1 = bf16[161,128]{1,0:T(8,128)(2,1)S(1)} collective-permute-done((bf16[161,128]{1,0:T(8,128)(2,1)S(1)}, bf16[161,128]{1,0:T(8,128)(2,1)S(1)}, u32[]{:S(2)}, u32[]{:S(2)}) %collective-permute-start.1) | collective-permute-done | bytes 41248 | tf_op jit(solution)/shard_map/ppermute | solution.py:119
  26.7 3.9 %collective-permute-start.2 = (bf16[213,128]{1,0:T(8,128)(2,1)S(1)}, bf16[213,128]{1,0:T(8,128)(2,1)S(1)}, u32[]{:S(2)}, u32[]{:S(2)}) collective-permute-start(bf16[213,128]{1,0:T(8,128)(2,1)S(1)} %get-tuple-element.52), channel_id=1, source_target_pairs={{0,1},{1,2},{2,3},{3,4},{4,5},{5,6},{6,7},{7,8},{8,9},{9,10},{10,1... | collective-permute-start | bytes 163592 | tf_op jit(solution)/shard_map/ppermute | solution.py:126
  30.6 1.9 %collective-permute-start.3 = (bf16[213,128]{1,0:T(8,128)(2,1)S(1)}, bf16[213,128]{1,0:T(8,128)(2,1)S(1)}, u32[]{:S(2)}, u32[]{:S(2)}) collective-permute-start(bf16[213,128]{1,0:T(8,128)(2,1)S(1)} %get-tuple-element.53), channel_id=1, source_target_pairs={{1,0},{2,1},{3,2},{4,3},{5,4},{6,5},{7,6},{8,7},{9,8},{10,9},{11,1... | collective-permute-start | bytes 163592 | tf_op jit(solution)/shard_map/ppermute | solution.py:127
  33.8 2.3 %collective-permute-done.3 = bf16[213,128]{1,0:T(8,128)(2,1)S(1)} collective-permute-done((bf16[213,128]{1,0:T(8,128)(2,1)S(1)}, bf16[213,128]{1,0:T(8,128)(2,1)S(1)}, u32[]{:S(2)}, u32[]{:S(2)}) %collective-permute-start.3) | collective-permute-done | bytes 54560 | tf_op jit(solution)/shard_map/ppermute | solution.py:127
  40.2 1.8 %slice_bitcast_fusion = (bf16[32,4,32,32]{3,2,1,0:T(8,128)(2,1)S(1)}, bf16[8,32,4,32,32]{4,3,2,1,0:T(8,128)(2,1)}, bf16[32,4,32,32]{3,2,1,0:T(8,128)(2,1)S(1)}) fusion(bf16[2,32,4,32,32]{4,3,2,1,0:T(8,128)(2,1)S(1)} %bitcast.81), kind=kLoop, calls=%fused_computation.95 | loop fusion | bytes 2097152 | tf_op jit(solution)/shard_map/squeeze | solution.py:88
  45.5 1.5 fusion.30
  47.0 1.5 fusion.31
  52.5 1.5 fusion.27
  57.0 3.1 %fusion.32 = bf16[8,32,4,32,32]{4,3,2,1,0:T(8,128)(2,1)} fusion(bf16[8,32,4,32,32]{4,3,2,1,0:T(8,128)(2,1)} %get-tuple-element.32, bf16[32,4,32,1]{3,2,1,0:T(8,128)(2,1)} %slice.648, bf16[32,4,32,31]{3,2,1,0:T(8,128)(2,1)} %slice.647), kind=kLoop, calls=%fused_computation.87 | loop fusion | flops 524288 | bytes 3145728
  62.1 1.6 fusion.33
  65.7 1.6 fusion.34
  68.6 1.7 fusion.35
  70.3 11.5 %reshape.274 = bf16[1024,1024]{1,0:T(8,128)(2,1)S(1)} reshape(bf16[8,32,4,32,32]{4,3,2,1,0:T(8,128)(2,1)} %fusion.35) | data formatting | bytes 4194304 | tf_op jit(solution)/shard_map/reshape | solution.py:93
  87.5 10.5 %all-to-all-start.1 = ((bf16[32,42,128]{2,1,0:T(8,128)(2,1)}), bf16[32,42,128]{2,1,0:T(8,128)(2,1)S(1)}, u32[]{:S(2)}, u32[]{:S(2)}) async-start(bf16[32,42,128]{2,1,0:T(8,128)(2,1)} %fusion.93), calls=%async_computation.1 | async-start | bytes 786432 | tf_op jit(solution)/shard_map/all_to_all | solution.py:102
  98.6 13.1 %all-to-all-done.1 = bf16[32,42,128]{2,1,0:T(8,128)(2,1)S(1)} async-done(((bf16[32,42,128]{2,1,0:T(8,128)(2,1)}), bf16[32,42,128]{2,1,0:T(8,128)(2,1)S(1)}, u32[]{:S(2)}, u32[]{:S(2)}) %all-to-all-start.1) | async-done | bytes 344096 | tf_op jit(solution)/shard_map/all_to_all | solution.py:102
  112.5 5.0 %collective-permute-start.4 = (bf16[5,42,128]{2,0,1:T(8,128)(2,1)}, bf16[5,42,128]{2,0,1:T(8,128)(2,1)}, u32[]{:S(2)}, u32[]{:S(2)}) collective-permute-start(bf16[5,42,128]{2,0,1:T(8,128)(2,1)} %get-tuple-element.43), channel_id=1, source_target_pairs={{0,32},{32,64},{64,96},{96,128},{128,160},{160,192},{192,224},{224... | collective-permute-start | bytes 161288 | tf_op jit(solution)/shard_map/ppermute | solution.py:135
  120.3 4.2 %collective-permute-done.5 = bf16[5,42,128]{2,0,1:T(8,128)(2,1)} collective-permute-done((bf16[5,42,128]{2,0,1:T(8,128)(2,1)}, bf16[5,42,128]{2,0,1:T(8,128)(2,1)}, u32[]{:S(2)}, u32[]{:S(2)}) %collective-permute-start.5) | collective-permute-done | bytes 53792 | tf_op jit(solution)/shard_map/ppermute | solution.py:136
  128.9 4.4 %fusion.95 = (bf16[1,38,38,128]{3,1,2,0:T(8,128)(2,1)S(1)}, f32[38,38,128]{2,0,1:T(8,128)S(1)}) fusion(f32[42,42,128]{2,0,1:T(8,128)S(1)} %maximum_convert_fusion.2, f32[42,42,128]{2,0,1:T(8,128)S(1)} %maximum_convert_fusion.1, f32[38,38,128]{2,0,1:T(8,128)S(1)} %slice_add_fusion.20, f32[38,38,128]{2,0,1:T(8,128)S(1)} %slice_add_fusion.24, ...), kind=kLoop, calls=%fused_computation.212 | loop fusion | flops 8687104 | bytes 8502272 | tf_op jit(solution)/shard_map/stack | solution.py:160
  136.2 2.5 %fusion.12 = f32[3,32,32,128]{3,1,2,0:T(8,128)S(1)} fusion(f32[3,32,32,128]{3,1,2,0:T(8,128)S(1)} %fusion.18), kind=kLoop, calls=%fused_computation.57 | loop fusion | flops 5111808 | bytes 3145728 | tf_op jit(solution)/shard_map/add | solution.py:28
  140.2 13.8 %all_to_all.20 = f32[32,1,128]{2,1,0:T(1,128)S(1)} all-to-all(f32[32,1,128]{2,1,0:T(1,128)S(1)} %broadcast_in_dim.55), channel_id=1, replica_groups=mesh['slab'=16,'blk'=32] {'blk'}, dimensions={0} | all-to-all | bytes 32768 | tf_op jit(solution)/shard_map/all_to_all | solution.py:168
  155.3 21.1 %all_to_all.21 = f32[16,1,128]{2,1,0:T(1,128)S(1)} all-to-all(f32[16,1,128]{2,1,0:T(1,128)S(1)} %broadcast_in_dim.56), channel_id=1, replica_groups=mesh['slab'=16,'blk'=32] {'slab'}, dimensions={0} | all-to-all | bytes 16384 | tf_op jit(solution)/shard_map/all_to_all | solution.py:168
  177.6 3.6 %divide_bitcast_fusion = f32[3,32,32,128]{3,2,1,0:T(8,128)} fusion(f32[]{:T(128)S(6)} %add.472, f32[3,32,32,128]{3,1,2,0:T(8,128)S(1)} %fusion.18), kind=kLoop, calls=%fused_computation.76 | loop fusion | flops 5898240 | bytes 3145732 | tf_op jit(solution)/shard_map/transpose | solution.py:169
  (165 shorter events, 49.5 us)
Async XLA Ops:
  1.1 14.5 %copy-start.7 = (bf16[32,32,128]{2,1,0:T(8,128)(2,1)S(1)}, bf16[32,32,128]{2,1,0:T(8,128)(2,1)}, u32[]{:S(2)}) copy-start(bf16[32,32,128]{2,1,0:T(8,128)(2,1)} %param.13) | copy-start | bytes 786436
  1.1 14.6 %copy-start.22 = (s32[1,1,4]{2,1,0:T(1,128)S(1)}, s32[1,1,4]{2,1,0:T(1,128)}, u32[]{:S(2)}) copy-start(s32[1,1,4]{2,1,0:T(1,128)} %param.19) | copy-start | bytes 52
  1.1 19.7 %copy-start.21 = (s32[38]{0:T(128)S(1)}, s32[38]{0:T(128)}, u32[]{:S(2)}) copy-start(s32[38]{0:T(128)} %constant.197) | copy-start | bytes 460
  5.2 32.7 %all-to-all-start = ((bf16[32,66,128]{2,1,0:T(8,128)(2,1)}), bf16[32,66,128]{2,1,0:T(8,128)(2,1)S(1)}, u32[]{:S(2)}, u32[]{:S(2)}) async-start(bf16[32,66,128]{2,1,0:T(8,128)(2,1)} %pad_maximum_fusion.2), calls=%async_computation | async-start | bytes 1179648 | tf_op jit(solution)/shard_map/all_to_all | solution.py:82
  15.9 6.4 %collective-permute-start = (bf16[161,128]{1,0:T(8,128)(2,1)S(1)}, bf16[161,128]{1,0:T(8,128)(2,1)S(1)}, u32[]{:S(2)}, u32[]{:S(2)}) collective-permute-start(bf16[161,128]{1,0:T(8,128)(2,1)S(1)} %get-tuple-element.54), channel_id=1, source_target_pairs={{0,32},{32,64},{64,96},{96,128},{128,160},{160,192},{192,224},{224... | collective-permute-start | bytes 123656 | tf_op jit(solution)/shard_map/ppermute | solution.py:118
  19.5 6.9 %collective-permute-start.1 = (bf16[161,128]{1,0:T(8,128)(2,1)S(1)}, bf16[161,128]{1,0:T(8,128)(2,1)S(1)}, u32[]{:S(2)}, u32[]{:S(2)}) collective-permute-start(bf16[161,128]{1,0:T(8,128)(2,1)S(1)} %get-tuple-element.55), channel_id=1, source_target_pairs={{32,0},{64,32},{96,64},{128,96},{160,128},{192,160},{224,192},{256... | collective-permute-start | bytes 123656 | tf_op jit(solution)/shard_map/ppermute | solution.py:119
  26.7 6.5 %collective-permute-start.2 = (bf16[213,128]{1,0:T(8,128)(2,1)S(1)}, bf16[213,128]{1,0:T(8,128)(2,1)S(1)}, u32[]{:S(2)}, u32[]{:S(2)}) collective-permute-start(bf16[213,128]{1,0:T(8,128)(2,1)S(1)} %get-tuple-element.52), channel_id=1, source_target_pairs={{0,1},{1,2},{2,3},{3,4},{4,5},{5,6},{6,7},{7,8},{8,9},{9,10},{10,1... | collective-permute-start | bytes 163592 | tf_op jit(solution)/shard_map/ppermute | solution.py:126
  30.6 5.5 %collective-permute-start.3 = (bf16[213,128]{1,0:T(8,128)(2,1)S(1)}, bf16[213,128]{1,0:T(8,128)(2,1)S(1)}, u32[]{:S(2)}, u32[]{:S(2)}) collective-permute-start(bf16[213,128]{1,0:T(8,128)(2,1)S(1)} %get-tuple-element.53), channel_id=1, source_target_pairs={{1,0},{2,1},{3,2},{4,3},{5,4},{6,5},{7,6},{8,7},{9,8},{10,9},{11,1... | collective-permute-start | bytes 163592 | tf_op jit(solution)/shard_map/ppermute | solution.py:127
  45.5 3.1 %copy-start.11 = (bf16[32,4,1,32]{3,2,1,0:T(2,128)(2,1)}, bf16[32,4,1,32]{3,2,1,0:T(2,128)(2,1)S(1)}, u32[]{:S(2)}) copy-start(bf16[32,4,1,32]{3,2,1,0:T(2,128)(2,1)S(1)} %slice.650) | copy-start | bytes 24580
  52.0 2.1 %copy-start.9 = (bf16[32,4,1,32]{3,2,1,0:T(2,128)(2,1)}, bf16[32,4,1,32]{3,2,1,0:T(2,128)(2,1)S(1)}, u32[]{:S(2)}) copy-start(bf16[32,4,1,32]{3,2,1,0:T(2,128)(2,1)S(1)} %slice.659) | copy-start | bytes 24580
  57.0 3.1 %copy-start.12 = (bf16[32,4,1,32]{3,2,1,0:T(2,128)(2,1)S(1)}, bf16[32,4,1,32]{3,2,1,0:T(2,128)(2,1)}, u32[]{:S(2)}) copy-start(bf16[32,4,1,32]{3,2,1,0:T(2,128)(2,1)} %copy-done.11) | copy-start | bytes 24580
  60.2 1.9 %copy-start.6 = (bf16[32,4,32,1]{3,2,1,0:T(8,128)(2,1)S(1)}, bf16[32,4,32,1]{3,2,1,0:T(8,128)(2,1)}, u32[]{:S(2)}) copy-start(bf16[32,4,32,1]{3,2,1,0:T(8,128)(2,1)} %fusion.31) | copy-start | bytes 24580
  63.7 1.9 %copy-start.4 = (bf16[32,4,32,1]{3,2,1,0:T(8,128)(2,1)S(1)}, bf16[32,4,32,1]{3,2,1,0:T(8,128)(2,1)}, u32[]{:S(2)}) copy-start(bf16[32,4,32,1]{3,2,1,0:T(8,128)(2,1)} %slice.657) | copy-start | bytes 24580
  70.3 11.5 %copy-start.15 = (f32[32,48]{0,1:T(8,128)S(1)}, f32[32,48]{0,1:T(8,128)}, u32[]{:S(2)}) copy-start(f32[32,48]{0,1:T(8,128)} %slice.639) | copy-start | bytes 18436
  70.3 11.6 %slice-start = ((f32[32,128]{0,1:T(8,128)}), f32[32,16]{0,1:T(8,128)S(1)}, s32[]{:S(2)}) async-start(f32[32,128]{0,1:T(8,128)} %copy-done.16), calls=%async_computation.4 | async-start | bytes 16384 | tf_op jit(solution)/shard_map/slice | solution.py:61
  70.3 11.7 %copy-start.20 = (f32[128]{0:T(128)S(1)}, f32[128]{0:T(128)}, u32[]{:S(2)}) copy-start(f32[128]{0:T(128)} %iota_convert_fusion) | copy-start | bytes 1540
  86.0 12.0 %copy-start.13 = (bf16[42,5,128]{2,0,1:T(8,128)(2,1)S(1)}, bf16[42,5,128]{2,0,1:T(8,128)(2,1)}, u32[]{:S(2)}) copy-start(bf16[42,5,128]{2,0,1:T(8,128)(2,1)} %copy.155) | copy-start | bytes 161284
  86.0 12.0 %copy-start.14 = (bf16[42,5,128]{2,0,1:T(8,128)(2,1)S(1)}, bf16[42,5,128]{2,0,1:T(8,128)(2,1)}, u32[]{:S(2)}) copy-start(bf16[42,5,128]{2,0,1:T(8,128)(2,1)} %copy.156) | copy-start | bytes 161284
  87.5 24.2 %all-to-all-start.1 = ((bf16[32,42,128]{2,1,0:T(8,128)(2,1)}), bf16[32,42,128]{2,1,0:T(8,128)(2,1)S(1)}, u32[]{:S(2)}, u32[]{:S(2)}) async-start(bf16[32,42,128]{2,1,0:T(8,128)(2,1)} %fusion.93), calls=%async_computation.1 | async-start | bytes 786432 | tf_op jit(solution)/shard_map/all_to_all | solution.py:102
  98.5 20.3 %copy-start.17 = (bf16[3,1,128]{2,1,0:T(2,128)(2,1)S(1)}, bf16[3,1,128]{2,1,0:T(2,128)(2,1)}, u32[]{:S(2)}) copy-start(bf16[3,1,128]{2,1,0:T(2,128)(2,1)} %copy.152) | copy-start | bytes 2308
  98.5 20.3 %copy-start.18 = (bf16[3,1,128]{2,1,0:T(2,128)(2,1)S(1)}, bf16[3,1,128]{2,1,0:T(2,128)(2,1)}, u32[]{:S(2)}) copy-start(bf16[3,1,128]{2,1,0:T(2,128)(2,1)} %copy.151) | copy-start | bytes 2308
  98.5 20.3 %copy-start.19 = (bf16[3,1,128]{2,1,0:T(2,128)(2,1)S(1)}, bf16[3,1,128]{2,1,0:T(2,128)(2,1)}, u32[]{:S(2)}) copy-start(bf16[3,1,128]{2,1,0:T(2,128)(2,1)} %copy.153) | copy-start | bytes 2308
  112.5 7.8 %collective-permute-start.4 = (bf16[5,42,128]{2,0,1:T(8,128)(2,1)}, bf16[5,42,128]{2,0,1:T(8,128)(2,1)}, u32[]{:S(2)}, u32[]{:S(2)}) collective-permute-start(bf16[5,42,128]{2,0,1:T(8,128)(2,1)} %get-tuple-element.43), channel_id=1, source_target_pairs={{0,32},{32,64},{64,96},{96,128},{128,160},{160,192},{192,224},{224... | collective-permute-start | bytes 161288 | tf_op jit(solution)/shard_map/ppermute | solution.py:135
  117.5 7.0 %collective-permute-start.5 = (bf16[5,42,128]{2,0,1:T(8,128)(2,1)}, bf16[5,42,128]{2,0,1:T(8,128)(2,1)}, u32[]{:S(2)}, u32[]{:S(2)}) collective-permute-start(bf16[5,42,128]{2,0,1:T(8,128)(2,1)} %get-tuple-element.44), channel_id=1, source_target_pairs={{32,0},{64,32},{96,64},{128,96},{160,128},{192,160},{224,192},{256... | collective-permute-start | bytes 161288 | tf_op jit(solution)/shard_map/ppermute | solution.py:136
  (8 other events, 10.9 us)
where the time goes:
time: 182 us; the launch traced here: 181 us
  other arithmetic  44 us (24%)
  local copies, waits for them, and re-layouts  38.4 us (21%)
  starting transfers between devices  37.9 us (21%)
  blocking collectives  34.9 us (19%)
  waiting for transfers between devices  24 us (13%)
    all_to_all x2, blocking collectives, per_device(): lax.all_to_all(tile, axis, split_axis=0, concat_axis=0, tiled=True)  34.9 us
    all_to_all x1, waiting for transfers between devices, warp(): return lax.all_to_all(w, 'blk', split_axis=0, concat_axis=0, tiled=True)  13.1 us
    reshape x1, local copies, waits for them, and re-layouts, warp(): s = jnp.stack(corners).reshape(8 * owners * blocks, side * side)  11.5 us
    all_to_all x1, starting transfers between devices, warp(): return lax.all_to_all(w, 'blk', split_axis=0, concat_axis=0, tiled=True)  10.5 us
    all_to_all x1, starting transfers between devices, warp(): lax.all_to_all(payload, 'blk', split_axis=0, concat_axis=0, tiled=True)  10.4 us
    unnamed x5, other arithmetic  9.1 us
    add x11, other arithmetic, window_sum(): result + weights[offset] * lax.slice_in_dim(volume, offset, offset + leng...  6.69 us
    another operation x3, other arithmetic, per_device(): jnp.stack([term * grad_x, term * grad_z, term * grad_y])  5.16 us
  transfers between devices with their start and end apart: 8, of which 5 were waited for; matrix products, arithmetic and copies ran while one was open for 4% of the time, Pallas kernels for 0%

commit v1 on v0

--- a/solution.py
+++ b/solution.py
@@ -3,6 +3,8 @@
 import jax
 import jax.numpy as jnp
 from jax import lax
+from jax.experimental import pallas as pl
+from jax.experimental.pallas import tpu as pltpu
 from jax.sharding import PartitionSpec as P
 
 LEVELS = 8
@@ -39,67 +41,172 @@
     return [(i + 1, i) for i in range(n - 1)]
 
 
-def next_along(a, axis):
-    size = a.shape[axis]
-    return jnp.concatenate(
-        [lax.slice_in_dim(a, 1, size, axis=axis), lax.slice_in_dim(a, size - 1, size, axis=axis)], axis=axis
-    )
-
-
-def request_row(fetch_owner, fetch_block, fetch_count, interp_level):
-    blocks, slots = fetch_owner.shape
-    in_list = jnp.arange(slots)[None, :] < fetch_count[:, None]
-    ids = jnp.where(in_list, fetch_owner * blocks + fetch_block, -1)
-    row = jnp.concatenate([ids.reshape(-1), interp_level.reshape(-1), fetch_count.reshape(-1)])
-    return jnp.pad(row, (0, 128 - row.shape[0])).astype(jnp.bfloat16)
-
-
-def coefficients(rows, blocks, slots):
-    n = rows.shape[0]
-    rows = rows.astype(jnp.float32)
-    e = blocks * slots
-    ids = rows[:, :e].reshape(n, blocks, slots)
-    lev = rows[:, e : 4 * e].reshape(n, blocks, 3, slots)
-    count = rows[:, 4 * e : 4 * e + blocks]
-    hit = (ids[..., None] == jnp.arange(n * blocks).astype(jnp.float32)).astype(jnp.float32)
-    pair = jnp.stack([LEVELS - lev, lev], axis=3)
-    wx, wz, wy = pair[:, :, 0], pair[:, :, 1], pair[:, :, 2]
-    prod = wz[:, :, :, None, None, :] * wx[:, :, None, :, None, :] * wy[:, :, None, None, :, :]
-    c = jnp.sum(prod[..., None] * hit[:, :, None, None, None], axis=5)
-    c = c.reshape(n * blocks, 8 * n * blocks)
-    hi = jnp.floor(c / 16.0) * 16.0
-    both = jnp.concatenate([hi, c - hi], axis=0).astype(jnp.bfloat16)
-    return both, (1.0 / count).reshape(n * blocks, 1) / float(LEVELS**3)
-
-
-def warp(moving_t, row):
-    side, _, width = moving_t.shape
-    owners = lax.axis_size("blk")
-    blocks = width // side
-    payload = jnp.concatenate(
-        [moving_t, next_along(moving_t, 0), jnp.broadcast_to(row[None, None, :], (side, 2, width))], axis=1
-    )
-    got = lax.all_to_all(payload, "blk", split_axis=0, concat_axis=0, tiled=True)
-    c, scale = coefficients(got[:, 2 * side, :], blocks, 4)
-    src = got[:, : 2 * side].reshape(owners, 2, side, blocks, side).transpose(1, 0, 3, 2, 4)
-    corners = []
+SIDE = 32
+WIDTH = 128
+BLOCKS = WIDTH // SIDE
+SLOTS = 4
+OWNERS = 32
+SENT = 2 * SIDE + 2
+PITCH = 72
+EXT = SIDE + 2 * RIM
+OUT_PITCH = 48
+
+
+def in_vmem():
+    return pl.BlockSpec(memory_space=pltpu.VMEM)
+
+
+def in_smem():
+    return pl.BlockSpec(memory_space=pltpu.SMEM)
+
+
+def pack_kernel(owner_ref, block_ref, count_ref, level_ref, moving_ref, out_ref, wide):
+    lane = lax.broadcasted_iota(jnp.int32, (2, WIDTH), 1)
+    row = jnp.zeros((2, WIDTH), jnp.int32)
+    e = BLOCKS * SLOTS
+    for g in range(BLOCKS):
+        count = count_ref[0, 0, g]
+        row = jnp.where(lane == 4 * e + g, count, row)
+        for k in range(SLOTS):
+            name = block_ref[0, 0, g, k] * OWNERS + owner_ref[0, 0, g, k]
+            row = jnp.where(lane == g * SLOTS + k, jnp.where(k < count, name, -1), row)
+            for axis in range(3):
+                at = e + (g * 3 + axis) * SLOTS + k
+                row = jnp.where(lane == at, level_ref[0, 0, g, axis, k], row)
+    row = row.astype(jnp.float32).astype(jnp.bfloat16)
+    for x in range(SIDE):
+        wide[pl.ds(x * SIDE, SIDE), :] = moving_ref[x].astype(jnp.float32)
+    for z in range(SIDE):
+        plane = wide[pl.ds(z, SIDE, stride=SIDE), :].astype(jnp.bfloat16)
+        out_ref[z, 0:SIDE, :] = plane
+        if z > 0:
+            out_ref[z - 1, SIDE : 2 * SIDE, :] = plane
+        if z == SIDE - 1:
+            out_ref[z, SIDE : 2 * SIDE, :] = plane
+        out_ref[z, 2 * SIDE : SENT, :] = row
+
+
+def pack(owner, block, count, level, moving):
+    return pl.pallas_call(
+        pack_kernel,
+        out_shape=jax.ShapeDtypeStruct((OWNERS, SENT, WIDTH), jnp.bfloat16),
+        in_specs=[in_smem()] * 4 + [in_vmem()],
+        out_specs=in_vmem(),
+        scratch_shapes=[pltpu.VMEM((SIDE * SIDE, WIDTH), jnp.float32)],
+        name="pack",
+    )(owner, block, count, level, moving)
+
+
+def exchange_groups(parts, lane):
+    turned = [[p] + [pltpu.roll(p, SIDE * s, 1) for s in range(1, BLOCKS)] for p in parts]
+    out = []
+    for b in range(BLOCKS):
+        pick = [turned[a][(a - b) % BLOCKS] for a in range(BLOCKS)]
+        out.append(
+            jnp.where(
+                lane < 2 * SIDE,
+                jnp.where(lane < SIDE, pick[0], pick[1]),
+                jnp.where(lane < 3 * SIDE, pick[2], pick[3]),
+            )
+        )
+    return out
+
+
+def hold_kernel(got_ref, out_ref, wide, source, coef, mixed, spread):
+    strip = SIDE // BLOCKS
+    rows = OWNERS * BLOCKS
+    lane = lax.broadcasted_iota(jnp.int32, (OWNERS, WIDTH), 1)
+    last_y = lane % SIDE == SIDE - 1
+    for o in range(OWNERS):
+        wide[pl.ds(o * PITCH, SENT), :] = got_ref[o].astype(jnp.float32)
+
+    lists = wide[pl.ds(2 * SIDE, OWNERS, stride=PITCH), :]
+    where_k = lane.astype(jnp.float32)
+    e = BLOCKS * SLOTS
+    top = float(LEVELS)
+    scales = []
+    for g in range(BLOCKS):
+        total = {}
+        for k in range(SLOTS):
+            at = g * SLOTS + k
+            name = lists[:, at : at + 1]
+            base = e + g * 3 * SLOTS + k
+            lx, lz, ly = (lists[:, base + a * SLOTS : base + a * SLOTS + 1] for a in range(3))
+            hit = jnp.where(where_k == name, 1.0, 0.0)
+            for dx in range(2):
+                ax = hit * (lx if dx else top - lx)
+                for dz in range(2):
+                    az = ax * (lz if dz else top - lz)
+                    for dy in range(2):
+                        ay = az * (ly if dy else top - ly)
+                        key = (dx, dz, dy)
+                        total[key] = ay if k == 0 else total[key] + ay
+        for (dx, dz, dy), c in total.items():
+            hi = jnp.floor(c * (1.0 / 16.0)) * 16.0
+            col = pl.ds((dz * 2 + dy) * WIDTH, WIDTH)
+            coef[dx, pl.ds(g * OWNERS, OWNERS), col] = hi.astype(jnp.bfloat16)
+            coef[dx, pl.ds(rows + g * OWNERS, OWNERS), col] = (c - hi).astype(jnp.bfloat16)
+        count = lists[:, 4 * e + g : 4 * e + g + 1]
+        scales.append((1.0 / count) * (1.0 / LEVELS**3))
+
     for dz in range(2):
-        for dx in range(2):
-            one = src[dz]
-            if dx:
-                one = next_along(one, 2)
-            for dy in range(2):
-                corners.append(next_along(one, 3) if dy else one)
-    s = jnp.stack(corners).reshape(8 * owners * blocks, side * side)
-    acc = jnp.dot(c, s, preferred_element_type=jnp.float32)
-    m = owners * blocks
-    w = ((acc[:m] + acc[m:]) * scale).astype(jnp.bfloat16)
-    w = w.reshape(owners, blocks, side, side).transpose(0, 2, 1, 3).reshape(owners, side, width)
-    zero = jnp.zeros((1, RIM, width), jnp.bfloat16)
-    before = jnp.concatenate([zero, w[:-1, side - RIM :]], axis=0)
-    after = jnp.concatenate([w[1:, :RIM], zero], axis=0)
-    w = jnp.concatenate([before, w, after], axis=1)
-    return lax.all_to_all(w, "blk", split_axis=0, concat_axis=0, tiled=True)
+        for t in range(strip):
+            parts = [
+                wide[pl.ds(dz * SIDE + strip * q + t, OWNERS, stride=PITCH), :] for q in range(BLOCKS)
+            ]
+            for g, u in enumerate(exchange_groups(parts, lane)):
+                v = jnp.where(last_y, u, pltpu.roll(u, WIDTH - 1, 1))
+                for dy, a in enumerate((u, v)):
+                    r0 = (dz * 2 + dy) * rows + g * OWNERS
+                    source[pl.ds(r0, OWNERS), pl.ds(t * WIDTH, WIDTH)] = a.astype(jnp.bfloat16)
+    tall = lax.broadcasted_iota(jnp.int32, (rows, WIDTH), 1)
+    for i in range(4):
+        first = source[pl.ds(i * rows, rows), 0:WIDTH].astype(jnp.float32)
+        final = source[pl.ds(i * rows, rows), pl.ds((strip - 1) * WIDTH, WIDTH)].astype(jnp.float32)
+        after = jnp.where(tall >= WIDTH - SIDE, final, pltpu.roll(first, WIDTH - SIDE, 1))
+        source[pl.ds(i * rows, rows), pl.ds(strip * WIDTH, WIDTH)] = after.astype(jnp.bfloat16)
+
+    piece = 2 * WIDTH
+    for n in range(strip * WIDTH // piece):
+        acc = jnp.dot(coef[0], source[:, pl.ds(n * piece, piece)], preferred_element_type=jnp.float32)
+        acc += jnp.dot(coef[1], source[:, pl.ds(n * piece + WIDTH, piece)], preferred_element_type=jnp.float32)
+        for g in range(BLOCKS):
+            lo = rows + g * OWNERS
+            part = acc[g * OWNERS : (g + 1) * OWNERS] + acc[lo : lo + OWNERS]
+            mixed[pl.ds(g * OWNERS, OWNERS), pl.ds(n * piece, piece)] = part * scales[g]
+
+    spread[pl.ds(OUT_PITCH, 8), :] = jnp.zeros((8, WIDTH), jnp.float32)
+    spread[pl.ds(OWNERS * OUT_PITCH + SIDE, 16), :] = jnp.zeros((16, WIDTH), jnp.float32)
+    for t in range(strip):
+        parts = [mixed[pl.ds(g * OWNERS, OWNERS), pl.ds(t * WIDTH, WIDTH)] for g in range(BLOCKS)]
+        for q, w in enumerate(exchange_groups(parts, lane)):
+            x = strip * q + t
+            spread[pl.ds(OUT_PITCH + RIM + x, OWNERS, stride=OUT_PITCH), :] = w
+            if x >= SIDE - RIM:
+                spread[pl.ds(2 * OUT_PITCH + x - SIDE + RIM, OWNERS, stride=OUT_PITCH), :] = w
+            if x < RIM:
+                spread[pl.ds(SIDE + RIM + x, OWNERS, stride=OUT_PITCH), :] = w
+    for r in range(OWNERS):
+        out_ref[r] = spread[pl.ds((r + 1) * OUT_PITCH, EXT), :].astype(jnp.bfloat16)
+
+
+def hold(got):
+    strip = SIDE // BLOCKS
+    rows = OWNERS * BLOCKS
+    return pl.pallas_call(
+        hold_kernel,
+        out_shape=jax.ShapeDtypeStruct((OWNERS, EXT, WIDTH), jnp.bfloat16),
+        in_specs=[in_vmem()],
+        out_specs=in_vmem(),
+        scratch_shapes=[
+            pltpu.VMEM((OWNERS * PITCH, WIDTH), jnp.float32),
+            pltpu.VMEM((4 * rows, (strip + 1) * WIDTH), jnp.bfloat16),
+            pltpu.VMEM((2, 2 * rows, 4 * rows), jnp.bfloat16),
+            pltpu.VMEM((rows, strip * WIDTH), jnp.float32),
+            pltpu.VMEM(((OWNERS + 2) * OUT_PITCH, WIDTH), jnp.float32),
+        ],
+        name="hold",
+    )(got)
 
 
 def per_device(fixed_image, moving_image, fetch_owner, fetch_block, fetch_count, interp_level, block_mask):
@@ -108,8 +215,9 @@
     blocks = fetch_count.shape[2]
     ext = side + 2 * RIM
     mid = side + 2 * SMOOTH_RADIUS
-    row = request_row(fetch_owner[0, 0], fetch_block[0, 0], fetch_count[0, 0], interp_level[0, 0])
-    warped = warp(moving_image.transpose(1, 0, 2), row)
+    sent = pack(fetch_owner, fetch_block, fetch_count, interp_level, moving_image)
+    got = lax.all_to_all(sent, "blk", split_axis=0, concat_axis=0, tiled=True)
+    warped = lax.all_to_all(hold(got), "blk", split_axis=0, concat_axis=0, tiled=True)
 
     mask_row = jnp.repeat(block_mask.reshape(blocks), side).astype(jnp.bfloat16)
     fixed_t = fixed_image.transpose(1, 0, 2)

time: 182 us -> 135 us (0.74)
  local copies, waits for them, and re-layouts: 38.4 us -> 7.83 us
  other arithmetic: 44 us -> 18.8 us
  Pallas kernels: 0 us -> 7.11 us
  waiting for transfers between devices: 24 us -> 26.1 us
    reshape x8 -> x0, local copies, waits for them, and re-layouts: 14.7 us -> none  [the longest x1 11.5 us: warp(): s = jnp.stack(corners).reshape(8 * owners * blocks, side * side)]
    unnamed x5 -> x0, other arithmetic: 9.1 us -> none
    slice x19 -> x0, local copies, waits for them, and re-layouts: 8.42 us -> none  [the longest x5 3.88 us: next_along(): lax.slice_in_dim(a, 1, size, axis=axis)]
    pallas_call x0 -> x2, Pallas kernels: none -> 7.11 us  [the longest x1 4.98 us: hold(): pl.pallas_call(hold_kernel, out_shape=jax.ShapeDtypeStruct((OWNERS, EXT,...]
    concatenate x7 -> x0, other arithmetic: 7.01 us -> none  [the longest x4 5.15 us: next_along(): jnp.concatenate([lax.slice_in_dim(a, 1, size, axis=axis), lax.slice_in_di...]
    another operation x5 -> x0, other arithmetic: 3.17 us -> none  [the longest x1 1.67 us: warp(): s = jnp.stack(corners).reshape(8 * owners * blocks, side * side)]
    unnamed x49 -> x12, local copies, waits for them, and re-layouts: 5.13 us -> 2.26 us
    squeeze x1 -> x0, local copies, waits for them, and re-layouts: 1.84 us -> none  [warp(): one = src[dz]]
  transfers between devices with their start and end apart: 8 -> 8, of which waited for: 5 -> 5; matrix products, arithmetic and copies ran while one was open for 4% -> 2% of each run, Pallas kernels for 0% -> 0%
where the time goes in v1:
time: 135 us; the launch traced here: 134 us
  starting transfers between devices  38 us (28%)
  blocking collectives  34.9 us (26%)
  waiting for transfers between devices  26.1 us (19%)
  other arithmetic  18.8 us (14%)
  local copies, waits for them, and re-layouts  7.83 us (6%)
  Pallas kernels  7.11 us (5%)
    all_to_all x2, blocking collectives, per_device(): lax.all_to_all(tile, axis, split_axis=0, concat_axis=0, tiled=True)  34.9 us
    all_to_all x1, waiting for transfers between devices, per_device(): lax.all_to_all(hold(got), 'blk', split_axis=0, concat_axis=0, tiled=True)  13.1 us
    all_to_all x1, starting transfers between devices, per_device(): lax.all_to_all(hold(got), 'blk', split_axis=0, concat_axis=0, tiled=True)  10.4 us
    all_to_all x1, starting transfers between devices, per_device(): got = lax.all_to_all(sent, 'blk', split_axis=0, concat_axis=0, tiled=True)  10.4 us
    add x11, other arithmetic, window_sum(): result + weights[offset] * lax.slice_in_dim(volume, offset, offset + leng...  6.76 us
    pallas_call x1, Pallas kernels, hold(): pl.pallas_call(hold_kernel, out_shape=jax.ShapeDtypeStruct((OWNERS, EXT,...  4.98 us
    ppermute x1, starting transfers between devices, per_device(): below = lax.ppermute(warped[side - RIM:], 'slab', shift_up('slab'))  4.95 us
    another operation x3, other arithmetic, per_device(): jnp.stack([term * grad_x, term * grad_z, term * grad_y])  4.87 us
  transfers between devices with their start and end apart: 8, of which 5 were waited for; matrix products, arithmetic and copies ran while one was open for 2% of the time, Pallas kernels for 0%

profile of v1, /device:TPU:1, one launch (start us, length us, event | category | flops | bytes accessed | tf_op | source)
XLA Modules:
  0.0 133.8 jit_solution(340215731432906971)
XLA Ops:
  0.0 1.3 copy.48.level_ref
  1.3 2.1 %pack.1 = bf16[32,66,128]{2,1,0:T(8,128)(2,1)} custom-call(s32[1,1,4,4]{3,2,1,0:T(4,128)} %owner_ref.1, s32[1,1,4,4]{3,2,1,0:T(4,128)} %block_ref.1, s32[1,1,4]{2,1,0:T(1,128)} %count_ref.1, s32[1,1,4,3,4]{4,3,2,1,0:T(4,128)} %copy.48.level_ref, bf16[32,32,128]{2,1,0:T(8,128)(2,1)} %moving_ref.1), custom_call_target="tpu_custom_call" | custom-call | tf_op jit(solution)/shard_map/pack/pallas_call | solution.py:90
  3.5 10.4 %all-to-all-start = ((bf16[32,66,128]{2,1,0:T(8,128)(2,1)}), bf16[32,66,128]{2,1,0:T(8,128)(2,1)S(1)}, u32[]{:S(2)}, u32[]{:S(2)}) async-start(bf16[32,66,128]{2,1,0:T(8,128)(2,1)} %pack.1), calls=%async_computation | async-start | bytes 1179648 | tf_op jit(solution)/shard_map/all_to_all | solution.py:219
  14.2 3.6 %collective-permute-start = (bf16[161,128]{1,0:T(8,128)(2,1)S(1)}, bf16[161,128]{1,0:T(8,128)(2,1)S(1)}, u32[]{:S(2)}, u32[]{:S(2)}) collective-permute-start(bf16[161,128]{1,0:T(8,128)(2,1)S(1)} %get-tuple-element.44), channel_id=1, source_target_pairs={{0,32},{32,64},{64,96},{96,128},{128,160},{160,192},{192,224},{224... | collective-permute-start | bytes 123656 | tf_op jit(solution)/shard_map/ppermute | solution.py:226
  17.9 1.3 collective-permute-start.1
  19.2 1.4 %collective-permute-done = bf16[161,128]{1,0:T(8,128)(2,1)S(1)} collective-permute-done((bf16[161,128]{1,0:T(8,128)(2,1)S(1)}, bf16[161,128]{1,0:T(8,128)(2,1)S(1)}, u32[]{:S(2)}, u32[]{:S(2)}) %collective-permute-start) | collective-permute-done | bytes 41248 | tf_op jit(solution)/shard_map/ppermute | solution.py:226
  20.6 4.1 %collective-permute-done.1 = bf16[161,128]{1,0:T(8,128)(2,1)S(1)} collective-permute-done((bf16[161,128]{1,0:T(8,128)(2,1)S(1)}, bf16[161,128]{1,0:T(8,128)(2,1)S(1)}, u32[]{:S(2)}, u32[]{:S(2)}) %collective-permute-start.1) | collective-permute-done | bytes 41248 | tf_op jit(solution)/shard_map/ppermute | solution.py:227
  24.9 4.0 %collective-permute-start.2 = (bf16[213,128]{1,0:T(8,128)(2,1)S(1)}, bf16[213,128]{1,0:T(8,128)(2,1)S(1)}, u32[]{:S(2)}, u32[]{:S(2)}) collective-permute-start(bf16[213,128]{1,0:T(8,128)(2,1)S(1)} %get-tuple-element.42), channel_id=1, source_target_pairs={{0,1},{1,2},{2,3},{3,4},{4,5},{5,6},{6,7},{7,8},{8,9},{9,10},{10,1... | collective-permute-start | bytes 163592 | tf_op jit(solution)/shard_map/ppermute | solution.py:234
  28.9 1.9 %collective-permute-start.3 = (bf16[213,128]{1,0:T(8,128)(2,1)S(1)}, bf16[213,128]{1,0:T(8,128)(2,1)S(1)}, u32[]{:S(2)}, u32[]{:S(2)}) collective-permute-start(bf16[213,128]{1,0:T(8,128)(2,1)S(1)} %get-tuple-element.43), channel_id=1, source_target_pairs={{1,0},{2,1},{3,2},{4,3},{5,4},{6,5},{7,6},{8,7},{9,8},{10,9},{11,1... | collective-permute-start | bytes 163592 | tf_op jit(solution)/shard_map/ppermute | solution.py:235
  30.9 3.5 %collective-permute-done.3 = bf16[213,128]{1,0:T(8,128)(2,1)S(1)} collective-permute-done((bf16[213,128]{1,0:T(8,128)(2,1)S(1)}, bf16[213,128]{1,0:T(8,128)(2,1)S(1)}, u32[]{:S(2)}, u32[]{:S(2)}) %collective-permute-start.3) | collective-permute-done | bytes 54560 | tf_op jit(solution)/shard_map/ppermute | solution.py:235
  35.2 5.0 %hold.1 = bf16[32,42,128]{2,1,0:T(8,128)(2,1)} custom-call(bf16[32,66,128]{2,1,0:T(8,128)(2,1)} %copy-done), custom_call_target="tpu_custom_call" | custom-call | tf_op jit(solution)/shard_map/hold/pallas_call | solution.py:196
  40.2 10.4 %all-to-all-start.1 = ((bf16[32,42,128]{2,1,0:T(8,128)(2,1)}), bf16[32,42,128]{2,1,0:T(8,128)(2,1)S(1)}, u32[]{:S(2)}, u32[]{:S(2)}) async-start(bf16[32,42,128]{2,1,0:T(8,128)(2,1)} %hold.1), calls=%async_computation.1 | async-start | bytes 786432 | tf_op jit(solution)/shard_map/all_to_all | solution.py:220
  51.3 13.1 %all-to-all-done.1 = bf16[32,42,128]{2,1,0:T(8,128)(2,1)S(1)} async-done(((bf16[32,42,128]{2,1,0:T(8,128)(2,1)}), bf16[32,42,128]{2,1,0:T(8,128)(2,1)S(1)}, u32[]{:S(2)}, u32[]{:S(2)}) %all-to-all-start.1) | async-done | bytes 344096 | tf_op jit(solution)/shard_map/all_to_all | solution.py:220
  65.0 5.0 %collective-permute-start.4 = (bf16[5,42,128]{2,1,0:T(8,128)(2,1)}, bf16[5,42,128]{2,1,0:T(8,128)(2,1)}, u32[]{:S(2)}, u32[]{:S(2)}) collective-permute-start(bf16[5,42,128]{2,1,0:T(8,128)(2,1)} %get-tuple-element.36), channel_id=1, source_target_pairs={{0,32},{32,64},{64,96},{96,128},{128,160},{160,192},{192,224},{224... | collective-permute-start | bytes 161288 | tf_op jit(solution)/shard_map/ppermute | solution.py:243
  70.0 1.5 %collective-permute-start.5 = (bf16[5,42,128]{2,1,0:T(8,128)(2,1)}, bf16[5,42,128]{2,1,0:T(8,128)(2,1)}, u32[]{:S(2)}, u32[]{:S(2)}) collective-permute-start(bf16[5,42,128]{2,1,0:T(8,128)(2,1)} %get-tuple-element.37), channel_id=1, source_target_pairs={{32,0},{64,32},{96,64},{128,96},{160,128},{192,160},{224,192},{256... | collective-permute-start | bytes 161288 | tf_op jit(solution)/shard_map/ppermute | solution.py:244
  72.7 4.0 %collective-permute-done.5 = bf16[5,42,128]{2,1,0:T(8,128)(2,1)} collective-permute-done((bf16[5,42,128]{2,1,0:T(8,128)(2,1)}, bf16[5,42,128]{2,1,0:T(8,128)(2,1)}, u32[]{:S(2)}, u32[]{:S(2)}) %collective-permute-start.5) | collective-permute-done | bytes 53792 | tf_op jit(solution)/shard_map/ppermute | solution.py:244
  76.8 1.2 fusion.76
  80.7 4.2 %fusion.72 = (bf16[1,38,38,128]{3,2,1,0:T(8,128)(2,1)S(1)}, f32[38,38,128]{2,1,0:T(8,128)S(1)}) fusion(f32[42,42,128]{2,1,0:T(8,128)S(1)} %maximum_convert_fusion.2, f32[42,42,128]{2,1,0:T(8,128)S(1)} %maximum_convert_fusion.1, f32[38,38,128]{2,1,0:T(8,128)S(1)} %slice_add_fusion.20, f32[38,38,128]{2,1,0:T(8,128)S(1)} %slice_add_fusion.24, ...), kind=kLoop, calls=%fused_computation.168 | loop fusion | flops 8687104 | bytes 8502272 | tf_op jit(solution)/shard_map/stack | solution.py:268
  85.8 1.5 %fusion = f32[3,38,32,128]{3,2,1,0:T(8,128)S(1)} fusion(f32[3,38,38,128]{3,2,1,0:T(8,128)S(1)} %maximum_convert_fusion), kind=kLoop, calls=%fused_computation.29 | loop fusion | flops 6070272 | bytes 14942208 | tf_op jit(solution)/shard_map/add | solution.py:30
  87.9 2.5 %fusion.12 = f32[3,32,32,128]{3,2,1,0:T(8,128)S(1)} fusion(f32[3,32,32,128]{3,2,1,0:T(8,128)S(1)} %fusion.18), kind=kLoop, calls=%fused_computation.49 | loop fusion | flops 5111808 | bytes 3145728 | tf_op jit(solution)/shard_map/add | solution.py:30
  91.9 13.8 %all_to_all.20 = f32[32,1,128]{2,1,0:T(1,128)S(1)} all-to-all(f32[32,1,128]{2,1,0:T(1,128)S(1)} %broadcast_in_dim.38), channel_id=1, replica_groups=mesh['slab'=16,'blk'=32] {'blk'}, dimensions={0} | all-to-all | bytes 32768 | tf_op jit(solution)/shard_map/all_to_all | solution.py:276
  106.9 21.1 %all_to_all.21 = f32[16,1,128]{2,1,0:T(1,128)S(1)} all-to-all(f32[16,1,128]{2,1,0:T(1,128)S(1)} %broadcast_in_dim.39), channel_id=1, replica_groups=mesh['slab'=16,'blk'=32] {'slab'}, dimensions={0} | all-to-all | bytes 16384 | tf_op jit(solution)/shard_map/all_to_all | solution.py:276
  129.3 2.5 %divide_bitcast_fusion = f32[3,32,32,128]{3,1,2,0:T(8,128)S(1)} fusion(f32[]{:T(128)S(6)} %add.453, f32[3,32,32,128]{3,2,1,0:T(8,128)S(1)} %fusion.18), kind=kLoop, calls=%fused_computation.68 | loop fusion | flops 5898240 | bytes 3145732 | tf_op jit(solution)/shard_map/transpose | solution.py:277
  131.8 2.1 %copy.51 = f32[3,32,32,128]{3,2,1,0:T(8,128)} copy(f32[3,32,32,128]{3,1,2,0:T(8,128)S(1)} %divide_bitcast_fusion) | data formatting | bytes 3145728 | tf_op jit(solution)/shard_map/transpose | solution.py:277
  (60 shorter events, 11.3 us)
Async XLA Ops:
  0.0 19.2 %copy-start.3 = (s32[38]{0:T(128)S(1)}, s32[38]{0:T(128)}, u32[]{:S(2)}) copy-start(s32[38]{0:T(128)} %constant.173) | copy-start | bytes 460
  0.0 13.9 %copy-start.2 = (bf16[32,32,128]{2,1,0:T(8,128)(2,1)S(1)}, bf16[32,32,128]{2,1,0:T(8,128)(2,1)}, u32[]{:S(2)}) copy-start(bf16[32,32,128]{2,1,0:T(8,128)(2,1)} %param.13) | copy-start | bytes 786436
  0.0 14.0 %copy-start.4 = (s32[1,1,4]{2,1,0:T(1,128)S(1)}, s32[1,1,4]{2,1,0:T(1,128)}, u32[]{:S(2)}) copy-start(s32[1,1,4]{2,1,0:T(1,128)} %param.19) | copy-start | bytes 52
  3.5 30.9 %all-to-all-start = ((bf16[32,66,128]{2,1,0:T(8,128)(2,1)}), bf16[32,66,128]{2,1,0:T(8,128)(2,1)S(1)}, u32[]{:S(2)}, u32[]{:S(2)}) async-start(bf16[32,66,128]{2,1,0:T(8,128)(2,1)} %pack.1), calls=%async_computation | async-start | bytes 1179648 | tf_op jit(solution)/shard_map/all_to_all | solution.py:219
  14.2 6.4 %collective-permute-start = (bf16[161,128]{1,0:T(8,128)(2,1)S(1)}, bf16[161,128]{1,0:T(8,128)(2,1)S(1)}, u32[]{:S(2)}, u32[]{:S(2)}) collective-permute-start(bf16[161,128]{1,0:T(8,128)(2,1)S(1)} %get-tuple-element.44), channel_id=1, source_target_pairs={{0,32},{32,64},{64,96},{96,128},{128,160},{160,192},{192,224},{224... | collective-permute-start | bytes 123656 | tf_op jit(solution)/shard_map/ppermute | solution.py:226
  17.9 6.9 %collective-permute-start.1 = (bf16[161,128]{1,0:T(8,128)(2,1)S(1)}, bf16[161,128]{1,0:T(8,128)(2,1)S(1)}, u32[]{:S(2)}, u32[]{:S(2)}) collective-permute-start(bf16[161,128]{1,0:T(8,128)(2,1)S(1)} %get-tuple-element.45), channel_id=1, source_target_pairs={{32,0},{64,32},{96,64},{128,96},{160,128},{192,160},{224,192},{256... | collective-permute-start | bytes 123656 | tf_op jit(solution)/shard_map/ppermute | solution.py:227
  24.7 26.1 %copy-start.1 = (bf16[160,128]{1,0:T(8,128)(2,1)}, bf16[160,128]{1,0:T(8,128)(2,1)S(1)}, u32[]{:S(2)}) copy-start(bf16[160,128]{1,0:T(8,128)(2,1)S(1)} %slice.515) | copy-start | bytes 122884
  24.9 5.9 %collective-permute-start.2 = (bf16[213,128]{1,0:T(8,128)(2,1)S(1)}, bf16[213,128]{1,0:T(8,128)(2,1)S(1)}, u32[]{:S(2)}, u32[]{:S(2)}) collective-permute-start(bf16[213,128]{1,0:T(8,128)(2,1)S(1)} %get-tuple-element.42), channel_id=1, source_target_pairs={{0,1},{1,2},{2,3},{3,4},{4,5},{5,6},{6,7},{7,8},{8,9},{9,10},{10,1... | collective-permute-start | bytes 163592 | tf_op jit(solution)/shard_map/ppermute | solution.py:234
  28.9 5.5 %collective-permute-start.3 = (bf16[213,128]{1,0:T(8,128)(2,1)S(1)}, bf16[213,128]{1,0:T(8,128)(2,1)S(1)}, u32[]{:S(2)}, u32[]{:S(2)}) collective-permute-start(bf16[213,128]{1,0:T(8,128)(2,1)S(1)} %get-tuple-element.43), channel_id=1, source_target_pairs={{1,0},{2,1},{3,2},{4,3},{5,4},{6,5},{7,6},{8,7},{9,8},{10,9},{11,1... | collective-permute-start | bytes 163592 | tf_op jit(solution)/shard_map/ppermute | solution.py:235
  34.4 0.8 copy-start
  40.2 24.2 %all-to-all-start.1 = ((bf16[32,42,128]{2,1,0:T(8,128)(2,1)}), bf16[32,42,128]{2,1,0:T(8,128)(2,1)S(1)}, u32[]{:S(2)}, u32[]{:S(2)}) async-start(bf16[32,42,128]{2,1,0:T(8,128)(2,1)} %hold.1), calls=%async_computation.1 | async-start | bytes 786432 | tf_op jit(solution)/shard_map/all_to_all | solution.py:220
  65.0 7.7 %collective-permute-start.4 = (bf16[5,42,128]{2,1,0:T(8,128)(2,1)}, bf16[5,42,128]{2,1,0:T(8,128)(2,1)}, u32[]{:S(2)}, u32[]{:S(2)}) collective-permute-start(bf16[5,42,128]{2,1,0:T(8,128)(2,1)} %get-tuple-element.36), channel_id=1, source_target_pairs={{0,32},{32,64},{64,96},{96,128},{128,160},{160,192},{192,224},{224... | collective-permute-start | bytes 161288 | tf_op jit(solution)/shard_map/ppermute | solution.py:243
  70.0 6.8 %collective-permute-start.5 = (bf16[5,42,128]{2,1,0:T(8,128)(2,1)}, bf16[5,42,128]{2,1,0:T(8,128)(2,1)}, u32[]{:S(2)}, u32[]{:S(2)}) collective-permute-start(bf16[5,42,128]{2,1,0:T(8,128)(2,1)} %get-tuple-element.37), channel_id=1, source_target_pairs={{32,0},{64,32},{96,64},{128,96},{160,128},{192,160},{224,192},{256... | collective-permute-start | bytes 161288 | tf_op jit(solution)/shard_map/ppermute | solution.py:244

commit v2 on v1

--- a/solution.py
+++ b/solution.py
@@ -7,6 +7,7 @@
 from jax.experimental.pallas import tpu as pltpu
 from jax.sharding import PartitionSpec as P
 
+
 LEVELS = 8
 BOX_RADIUS = 2
 SMOOTH_RADIUS = 3
@@ -22,13 +23,6 @@
     raw = [math.exp(-(t * t) / (2.0 * sigma_smooth * sigma_smooth)) for t in range(-radius, radius + 1)]
     total = sum(raw)
     return [one / total for one in raw]
-
-
-def window_sum(volume, axis_pos, length, weights):
-    result = weights[0] * lax.slice_in_dim(volume, 0, length, axis=axis_pos)
-    for offset in range(1, len(weights)):
-        result = result + weights[offset] * lax.slice_in_dim(volume, offset, offset + length, axis=axis_pos)
-    return result
 
 
 def shift_up(axis):
@@ -50,6 +44,21 @@
 PITCH = 72
 EXT = SIDE + 2 * RIM
 OUT_PITCH = 48
+
+
+MID = SIDE + 2 * SMOOTH_RADIUS
+INNER = SIDE - 2 * BOX_RADIUS
+CORE = INNER - 2 * SMOOTH_RADIUS
+ROW = OUT_PITCH
+MIB = 1 << 20
+
+
+def params(mib):
+    return pltpu.CompilerParams(vmem_limit_bytes=mib * MIB)
+
+
+def cost(flops, nbytes):
+    return pl.CostEstimate(flops=flops, bytes_accessed=nbytes, transcendentals=0)
 
 
 def in_vmem():
@@ -93,6 +102,7 @@
         in_specs=[in_smem()] * 4 + [in_vmem()],
         out_specs=in_vmem(),
         scratch_shapes=[pltpu.VMEM((SIDE * SIDE, WIDTH), jnp.float32)],
+        compiler_params=params(8),
         name="pack",
     )(owner, block, count, level, moving)
 
@@ -177,6 +187,8 @@
 
     spread[pl.ds(OUT_PITCH, 8), :] = jnp.zeros((8, WIDTH), jnp.float32)
     spread[pl.ds(OWNERS * OUT_PITCH + SIDE, 16), :] = jnp.zeros((16, WIDTH), jnp.float32)
+    for i in range(EXT, OUT_PITCH):
+        spread[pl.ds(OUT_PITCH + i, OWNERS, stride=OUT_PITCH), :] = jnp.zeros((OWNERS, WIDTH), jnp.float32)
     for t in range(strip):
         parts = [mixed[pl.ds(g * OWNERS, OWNERS), pl.ds(t * WIDTH, WIDTH)] for g in range(BLOCKS)]
         for q, w in enumerate(exchange_groups(parts, lane)):
@@ -187,7 +199,7 @@
             if x < RIM:
                 spread[pl.ds(SIDE + RIM + x, OWNERS, stride=OUT_PITCH), :] = w
     for r in range(OWNERS):
-        out_ref[r] = spread[pl.ds((r + 1) * OUT_PITCH, EXT), :].astype(jnp.bfloat16)
+        out_ref[r] = spread[pl.ds((r + 1) * OUT_PITCH, OUT_PITCH), :].astype(jnp.bfloat16)
 
 
 def hold(got):
@@ -195,7 +207,7 @@
     rows = OWNERS * BLOCKS
     return pl.pallas_call(
         hold_kernel,
-        out_shape=jax.ShapeDtypeStruct((OWNERS, EXT, WIDTH), jnp.bfloat16),
+        out_shape=jax.ShapeDtypeStruct((OWNERS, OUT_PITCH, WIDTH), jnp.bfloat16),
         in_specs=[in_vmem()],
         out_specs=in_vmem(),
         scratch_shapes=[
@@ -205,21 +217,316 @@
             pltpu.VMEM((rows, strip * WIDTH), jnp.float32),
             pltpu.VMEM(((OWNERS + 2) * OUT_PITCH, WIDTH), jnp.float32),
         ],
+        compiler_params=params(16),
         name="hold",
     )(got)
 
 
+def distance():
+    i = lax.broadcasted_iota(jnp.int32, (WIDTH, WIDTH), 0)
+    j = lax.broadcasted_iota(jnp.int32, (WIDTH, WIDTH), 1)
+    return jnp.abs(i - j)
+
+
+def box_band():
+    one = jnp.where(distance() <= BOX_RADIUS, 1.0, 0.0).astype(jnp.bfloat16)
+    return one, jnp.concatenate([one, one], axis=0)
+
+
+def smooth_band():
+    d = distance()
+    taps = smooth_weights(SMOOTH_RADIUS)
+    left = jnp.zeros((WIDTH, WIDTH), jnp.float32)
+    for t in range(SMOOTH_RADIUS + 1):
+        left = jnp.where(d == t, taps[SMOOTH_RADIUS + t], left)
+    parts = []
+    for _ in range(3):
+        part = left.astype(jnp.bfloat16)
+        parts.append(part)
+        left = left - part.astype(jnp.float32)
+    return jnp.concatenate(parts, axis=0)
+
+
+def times(a, band):
+    return jnp.dot(a, band, preferred_element_type=jnp.float32)
+
+
+def halves(product):
+    hi = product.astype(jnp.bfloat16)
+    return jnp.concatenate([hi, (product - hi.astype(jnp.float32)).astype(jnp.bfloat16)], axis=1)
+
+
+def rows_at(i):
+    if isinstance(i, int):
+        return pl.ds(i * ROW, ROW)
+    return pl.ds(pl.multiple_of(i * ROW, ROW), ROW)
+
+
+def along(a, step):
+    return pltpu.roll(a, (-step) % ROW, 0)
+
+
+def box_zx(ref, which, i):
+    r = [ref[which, rows_at(i + t), :] for t in range(2 * BOX_RADIUS + 1)]
+    a = ((r[0] + r[1]) + (r[2] + r[3])) + r[4]
+    two = a + along(a, -1)
+    return ((along(two, -1) + a) + along(two, 2)) * (1.0 / (2 * BOX_RADIUS + 1) ** 3)
+
+
+def fixed_kernel(fixed_ref, mask_ref, mean_ref, away_ref, gain_ref, sums):
+    one, twice = box_band()
+    chunk = 3 * ROW
+
+    def by_y(i, carry):
+        rows = pl.ds(pl.multiple_of(i * chunk, chunk), chunk)
+        f = fixed_ref[rows, :]
+        sums[0, rows, :] = times(f, one)
+        wide = f.astype(jnp.float32)
+        sums[1, rows, :] = times(halves(wide * wide), twice)
+        return carry
+
+    lax.fori_loop(0, EXT // 3, by_y, 0)
+
+    def by_z(i, carry):
+        mean = box_zx(sums, 0, i)
+        var = box_zx(sums, 1, i) - mean * mean + var_eps
+        part = jnp.where(i < SMOOTH_RADIUS, 0, jnp.where(i < SMOOTH_RADIUS + SIDE, 1, 2))
+        mean_ref[rows_at(i), :] = mean
+        away_ref[rows_at(i), :] = fixed_ref[rows_at(i + BOX_RADIUS), :].astype(jnp.float32) - mean
+        gain_ref[rows_at(i), :] = mask_ref[rows_at(part), :] * 2.0 / var
+        return carry
+
+    lax.fori_loop(0, MID, by_z, 0)
+
+
+def fixed_part(fixed, mask):
+    out = jax.ShapeDtypeStruct((MID * ROW, WIDTH), jnp.float32)
+    return pl.pallas_call(
+        fixed_kernel,
+        out_shape=[out] * 3,
+        in_specs=[in_vmem()] * 2,
+        out_specs=[in_vmem()] * 3,
+        scratch_shapes=[pltpu.VMEM((2, EXT * ROW, WIDTH), jnp.float32)],
+        compiler_params=params(12),
+        cost_estimate=cost(5_000_000_000, 4_000_000),
+        name="fixed_part",
+    )(fixed, mask)
+
+
+def sums_by_y(m, f, wide, sums, rows, bands):
+    mw = m.astype(jnp.float32)
+    wide[rows, :] = mw
+    sums[0, rows, :] = times(m, bands[0])
+    sums[1, rows, :] = times(halves(mw * mw), bands[1])
+    sums[2, rows, :] = times(halves(mw * f.astype(jnp.float32)), bands[1])
+
+
+def force_row(wide, sums, i, mean_ref, away_ref, gain_ref, j, force, k):
+    mean = box_zx(sums, 0, i)
+    var = box_zx(sums, 1, i) - mean * mean + var_eps
+    cov = box_zx(sums, 2, i) - mean_ref[rows_at(j), :] * mean
+    q = cov / var
+    m = wide[rows_at(i + BOX_RADIUS), :]
+    term = (0.5 * gain_ref[rows_at(j), :]) * q * (away_ref[rows_at(j), :] - q * (m - mean))
+    lane = lax.broadcasted_iota(jnp.int32, (ROW, WIDTH), 1)
+    up = jnp.where(lane == WIDTH - 1, 0.0, pltpu.roll(m, WIDTH - 1, 1))
+    down = jnp.where(lane == 0, 0.0, pltpu.roll(m, 1, 1))
+    force[0, rows_at(k), :] = (term * (along(m, 1) - along(m, -1))).astype(jnp.bfloat16)
+    z_step = wide[rows_at(i + BOX_RADIUS + 1), :] - wide[rows_at(i + BOX_RADIUS - 1), :]
+    force[1, rows_at(k), :] = (term * z_step).astype(jnp.bfloat16)
+    force[2, rows_at(k), :] = (term * (up - down)).astype(jnp.bfloat16)
+
+
+def smooth_row(smooth_y, i, out_ref, z, peak):
+    taps = smooth_weights(SMOOTH_RADIUS)[SMOOTH_RADIUS:]
+    total = None
+    for c in range(3):
+        g = [smooth_y[c, rows_at(i + t), :] for t in range(2 * SMOOTH_RADIUS + 1)]
+        mid = SMOOTH_RADIUS
+        s = taps[0] * g[mid]
+        for t in range(1, SMOOTH_RADIUS + 1):
+            s += taps[t] * (g[mid - t] + g[mid + t])
+        a = taps[0] * along(s, RIM)
+        for t in range(1, SMOOTH_RADIUS + 1):
+            a += taps[t] * (along(s, RIM - t) + along(s, RIM + t))
+        a = a[:SIDE]
+        at = (c * SIDE + z) * SIDE
+        out_ref[pl.ds(at if isinstance(at, int) else pl.multiple_of(at, SIDE), SIDE), :] = a
+        total = a * a if total is None else total + a * a
+    return jnp.maximum(peak, total)
+
+
+def inner_kernel(warped_ref, fixed_ref, mean_ref, away_ref, gain_ref, out_ref, edge_ref, peak_ref, wide, sums, force, smooth_y):
+    bands = box_band()
+    triple = smooth_band()
+    chunk = 4 * ROW
+
+    def by_y(i, carry):
+        rows = pl.ds(pl.multiple_of(i * chunk, chunk), chunk)
+        f = fixed_ref[pl.ds(pl.multiple_of(i * chunk + RIM * ROW, ROW), chunk), :]
+        sums_by_y(warped_ref[rows, :], f, wide, sums, rows, bands)
+        return carry
+
+    lax.fori_loop(0, SIDE // 4, by_y, 0)
+
+    def by_z(i, carry):
+        force_row(wide, sums, i, mean_ref, away_ref, gain_ref, i + RIM, force, i)
+        return carry
+
+    lax.fori_loop(0, INNER, by_z, 0)
+
+    def smooth(i, carry):
+        rows = pl.ds(pl.multiple_of(i * chunk, chunk), chunk)
+        for c in range(3):
+            f = force[c, rows, :]
+            smooth_y[c, rows, :] = times(jnp.concatenate([f, f, f], axis=1), triple)
+        return carry
+
+    lax.fori_loop(0, INNER // 4, smooth, 0)
+    kept = 2 * SMOOTH_RADIUS * ROW
+    for c in range(3):
+        edge_ref[c, 0:kept, :] = smooth_y[c, 0:kept, :]
+        edge_ref[c, kept : 2 * kept, :] = smooth_y[c, INNER * ROW - kept : INNER * ROW, :]
+    peak_ref[...] = lax.fori_loop(
+        0, CORE, lambda i, peak: smooth_row(smooth_y, i, out_ref, i + RIM, peak), jnp.zeros((SIDE, WIDTH), jnp.float32)
+    )
+
+
+def rim_kernel(below_ref, above_ref, warped_ref, fixed_ref, mean_ref, away_ref, gain_ref, edge_ref, first_ref, out_ref, peak_ref, wide, sums, force, smooth_y):
+    bands = box_band()
+    triple = smooth_band()
+    own = RIM - 1
+    stack = RIM + own
+    for ref, start, count, at, f_at in (
+        (below_ref, 0, RIM, 0, 0),
+        (warped_ref, 0, own, RIM, RIM),
+        (warped_ref, SIDE - own, own, stack, RIM + SIDE - own),
+        (above_ref, 0, RIM, stack + own, RIM + SIDE),
+    ):
+        m = ref[pl.ds(start * ROW, count * ROW), :]
+        f = fixed_ref[pl.ds(f_at * ROW, count * ROW), :]
+        sums_by_y(m, f, wide, sums, pl.ds(at * ROW, count * ROW), bands)
+
+    def by_z(i, carry):
+        side = jnp.where(i < RIM, 0, 1)
+        j = i - RIM * side
+        force_row(wide, sums, stack * side + j, mean_ref, away_ref, gain_ref, (MID - RIM) * side + j, force, i)
+        return carry
+
+    lax.fori_loop(0, 2 * RIM, by_z, 0)
+    kept = 2 * SMOOTH_RADIUS
+    tall = RIM + kept
+    for c in range(3):
+        for side in range(2):
+            f = force[c, pl.ds(side * RIM * ROW, RIM * ROW), :]
+            new = (side * tall + (kept if side else 0)) * ROW
+            smooth_y[c, pl.ds(new, RIM * ROW), :] = times(jnp.concatenate([f, f, f], axis=1), triple)
+            old = (side * tall + (0 if side else RIM)) * ROW
+            smooth_y[c, pl.ds(old, kept * ROW), :] = edge_ref[c, pl.ds(side * kept * ROW, kept * ROW), :]
+
+    def smooth(i, peak):
+        side = jnp.where(i < RIM, 0, 1)
+        j = i - RIM * side
+        return smooth_row(smooth_y, tall * side + j, out_ref, (SIDE - RIM) * side + j, peak)
+
+    peak = lax.fori_loop(0, 2 * RIM, smooth, first_ref[...])
+    top = jnp.max(jnp.max(peak, axis=0, keepdims=True), axis=1, keepdims=True)
+    peak_ref[...] = jnp.broadcast_to(top.reshape(1, 1, 1), peak_ref.shape)
+
+
+def inner(warped, fixed, mean, away, gain):
+    return pl.pallas_call(
+        inner_kernel,
+        out_shape=[
+            jax.ShapeDtypeStruct((3 * SIDE * SIDE, WIDTH), jnp.float32),
+            jax.ShapeDtypeStruct((3, 4 * SMOOTH_RADIUS * ROW, WIDTH), jnp.float32),
+            jax.ShapeDtypeStruct((SIDE, WIDTH), jnp.float32),
+        ],
+        in_specs=[in_vmem()] * 5,
+        out_specs=[in_vmem()] * 3,
+        scratch_shapes=[
+            pltpu.VMEM((SIDE * ROW, WIDTH), jnp.float32),
+            pltpu.VMEM((3, SIDE * ROW, WIDTH), jnp.float32),
+            pltpu.VMEM((3, INNER * ROW, WIDTH), jnp.bfloat16),
+            pltpu.VMEM((3, INNER * ROW, WIDTH), jnp.float32),
+        ],
+        compiler_params=params(20),
+        cost_estimate=cost(10_000_000_000, 8_000_000),
+        name="inner",
+    )(warped, fixed, mean, away, gain)
+
+
+def rim(below, above, warped, fixed, mean, away, gain, edge, first):
+    stack = 2 * (2 * RIM - 1) * ROW
+    tall = 2 * (RIM + 2 * SMOOTH_RADIUS) * ROW
+    return pl.pallas_call(
+        rim_kernel,
+        out_shape=[
+            jax.ShapeDtypeStruct((3 * SIDE * SIDE, WIDTH), jnp.float32),
+            jax.ShapeDtypeStruct((OWNERS, 1, WIDTH), jnp.float32),
+        ],
+        in_specs=[in_vmem()] * 9,
+        out_specs=[in_vmem()] * 2,
+        scratch_shapes=[
+            pltpu.VMEM((stack, WIDTH), jnp.float32),
+            pltpu.VMEM((3, stack, WIDTH), jnp.float32),
+            pltpu.VMEM((3, 2 * RIM * ROW, WIDTH), jnp.bfloat16),
+            pltpu.VMEM((3, tall, WIDTH), jnp.float32),
+        ],
+        compiler_params=params(20),
+        name="rim",
+    )(below, above, warped, fixed, mean, away, gain, edge, first)
+
+
+def relay_kernel(in_ref, out_ref):
+    a = jnp.max(in_ref[...].reshape(in_ref.shape[0], WIDTH), axis=0, keepdims=True)
+    out_ref[...] = jnp.broadcast_to(a.reshape(1, 1, WIDTH), out_ref.shape)
+
+
+def relay(tiles, count):
+    return pl.pallas_call(
+        relay_kernel,
+        out_shape=jax.ShapeDtypeStruct((count, 1, WIDTH), jnp.float32),
+        in_specs=[in_vmem()],
+        out_specs=in_vmem(),
+        compiler_params=params(1),
+        name="relay",
+    )(tiles)
+
+
+STEP_X = 8
+
+
+def finish_kernel(peaks_ref, core_ref, rim_ref, out_ref):
+    x0 = pl.program_id(0) * STEP_X
+    peak = jnp.sqrt(jnp.max(peaks_ref[...].reshape(peaks_ref.shape[0], WIDTH), axis=0, keepdims=True))
+    scale = step_length / (peak + peak_eps)
+    z = lax.broadcasted_iota(jnp.int32, (SIDE, WIDTH), 0)
+    at_rim = (z < RIM) | (z >= SIDE - RIM)
+    for c in range(3):
+        for x in range(STEP_X):
+            rows = pl.ds(c * SIDE * SIDE + x0 + x, SIDE, stride=SIDE)
+            out_ref[c, x] = jnp.where(at_rim, rim_ref[rows, :], core_ref[rows, :]) * scale
+
+
+def finish(peaks, core, rims):
+    return pl.pallas_call(
+        finish_kernel,
+        out_shape=jax.ShapeDtypeStruct((3, SIDE, SIDE, WIDTH), jnp.float32),
+        grid=(SIDE // STEP_X,),
+        in_specs=[in_vmem()] * 3,
+        out_specs=pl.BlockSpec((3, STEP_X, SIDE, WIDTH), lambda i: (0, i, 0, 0)),
+        compiler_params=params(12),
+        name="finish",
+    )(peaks, core, rims)
+
+
 def per_device(fixed_image, moving_image, fetch_owner, fetch_block, fetch_count, interp_level, block_mask):
-    side = fixed_image.shape[0]
-    width = fixed_image.shape[2]
-    blocks = fetch_count.shape[2]
-    ext = side + 2 * RIM
-    mid = side + 2 * SMOOTH_RADIUS
+    side, width, ext = SIDE, WIDTH, EXT
     sent = pack(fetch_owner, fetch_block, fetch_count, interp_level, moving_image)
     got = lax.all_to_all(sent, "blk", split_axis=0, concat_axis=0, tiled=True)
-    warped = lax.all_to_all(hold(got), "blk", split_axis=0, concat_axis=0, tiled=True)
-
-    mask_row = jnp.repeat(block_mask.reshape(blocks), side).astype(jnp.bfloat16)
+
+    mask_row = jnp.repeat(block_mask.reshape(BLOCKS), side).astype(jnp.bfloat16)
     fixed_t = fixed_image.transpose(1, 0, 2)
     tail = jnp.concatenate([fixed_t[side - RIM :].reshape(-1, width), mask_row[None]], axis=0)
     head = jnp.concatenate([fixed_t[:RIM].reshape(-1, width), mask_row[None]], axis=0)
@@ -229,52 +536,48 @@
         [below[:-1].reshape(RIM, side, width), fixed_t, above[:-1].reshape(RIM, side, width)], axis=0
     )
     masks = jnp.stack([below[-1], mask_row, above[-1]])
+
+    held = hold(got)
+    fixed_z, masks, _ = lax.optimization_barrier((fixed_z, masks, held))
+    warped = lax.all_to_all(held, "blk", split_axis=0, concat_axis=0, tiled=True)
+
     tail = jnp.concatenate([fixed_z[:, side - RIM :].reshape(-1, width), masks], axis=0)
     head = jnp.concatenate([fixed_z[:, :RIM].reshape(-1, width), masks], axis=0)
     left = lax.ppermute(tail, "blk", shift_up("blk"))
     right = lax.ppermute(head, "blk", shift_down("blk"))
     fixed = jnp.concatenate(
-        [left[:-3].reshape(ext, RIM, width), fixed_z, right[:-3].reshape(ext, RIM, width)], axis=1
-    ).astype(jnp.float32)
-    masks = jnp.stack([left[-3:], masks, right[-3:]], axis=1).astype(jnp.float32)
-    mask = jnp.repeat(jnp.repeat(masks, jnp.array([SMOOTH_RADIUS, side, SMOOTH_RADIUS]), axis=0, total_repeat_length=mid),
-                      jnp.array([SMOOTH_RADIUS, side, SMOOTH_RADIUS]), axis=1, total_repeat_length=mid)
+        [
+            left[:-3].reshape(ext, RIM, width),
+            fixed_z,
+            right[:-3].reshape(ext, RIM, width),
+            jnp.zeros((ext, ROW - ext, width), jnp.bfloat16),
+        ],
+        axis=1,
+    ).reshape(ext * ROW, width)
+    spread_x = lambda a, n: jnp.broadcast_to(a[:, None], (3, n, width)).astype(jnp.float32)
+    mask = jnp.concatenate(
+        [
+            jnp.zeros((3, BOX_RADIUS, width), jnp.float32),
+            spread_x(left[-3:], SMOOTH_RADIUS),
+            spread_x(masks, side),
+            spread_x(right[-3:], SMOOTH_RADIUS),
+            jnp.zeros((3, ROW - MID - BOX_RADIUS, width), jnp.float32),
+        ],
+        axis=1,
+    ).reshape(3 * ROW, width)
+    mean, away, gain = fixed_part(fixed, mask)
 
     below = lax.ppermute(warped[side - RIM :], "slab", shift_up("slab"))
     above = lax.ppermute(warped[:RIM], "slab", shift_down("slab"))
-    moving = jnp.concatenate([below, warped, above], axis=0).astype(jnp.float32)
-
-    ones = [1.0] * (2 * BOX_RADIUS + 1)
-    n = float(len(ones) ** 3)
-
-    def box(a):
-        a = window_sum(a, 0, mid, ones)
-        a = window_sum(a, 1, mid, ones)
-        a = jnp.pad(a, ((0, 0), (0, 0), (BOX_RADIUS, BOX_RADIUS)))
-        return window_sum(a, 2, width, ones)
-
-    mean_f = box(fixed) / n
-    mean_m = box(moving) / n
-    var_f = box(fixed * fixed) / n - mean_f * mean_f + var_eps
-    var_m = box(moving * moving) / n - mean_m * mean_m + var_eps
-    cov = box(fixed * moving) / n - mean_f * mean_m
-    r = BOX_RADIUS
-    here = (slice(r, r + mid), slice(r, r + mid))
-    grad_z = (moving[r + 1 : r + 1 + mid, here[1]] - moving[r - 1 : r - 1 + mid, here[1]]) * 0.5
-    grad_x = (moving[here[0], r + 1 : r + 1 + mid] - moving[here[0], r - 1 : r - 1 + mid]) * 0.5
-    padded = jnp.pad(moving[here], ((0, 0), (0, 0), (1, 1)))
-    grad_y = (padded[:, :, 2:] - padded[:, :, :-2]) * 0.5
-    term = mask * 2.0 * cov / (var_f * var_m) * (fixed[here] - mean_f - cov / var_m * (moving[here] - mean_m))
-    force = jnp.stack([term * grad_x, term * grad_z, term * grad_y]).astype(jnp.bfloat16).astype(jnp.float32)
-    taps = smooth_weights(SMOOTH_RADIUS)
-    s = window_sum(force, 2, side, taps)
-    s = window_sum(s, 1, side, taps)
-    s = window_sum(jnp.pad(s, ((0, 0), (0, 0), (0, 0), (SMOOTH_RADIUS, SMOOTH_RADIUS))), 3, width, taps)
-    peak = jnp.max(jnp.sqrt(s[0] * s[0] + s[1] * s[1] + s[2] * s[2]))
-    for axis in ("blk", "slab"):
-        tile = jnp.broadcast_to(peak, (lax.axis_size(axis), 1, 128))
-        peak = jnp.max(lax.all_to_all(tile, axis, split_axis=0, concat_axis=0, tiled=True))
-    return (step_length * s / (peak + peak_eps)).transpose(0, 2, 1, 3)
+    flat = warped.reshape(side * ROW, width)
+    core, edge, first = inner(flat, fixed, mean, away, gain)
+    rims, peak = rim(
+        below.reshape(RIM * ROW, width), above.reshape(RIM * ROW, width), flat, fixed, mean, away, gain, edge, first
+    )
+    peak = lax.all_to_all(peak, "blk", split_axis=0, concat_axis=0, tiled=True)
+    peak = relay(peak, lax.axis_size("slab"))
+    peak = lax.all_to_all(peak, "slab", split_axis=0, concat_axis=0, tiled=True)
+    return finish(peak, core, rims)
 
 
 def solution(mesh):

time: 135 us -> 119 us (0.88)
  other arithmetic: 18.8 us -> 0.33 us
  Pallas kernels: 7.11 us -> 23.2 us
  waiting for transfers between devices: 26.1 us -> 20.8 us
  starting transfers between devices: 38 us -> 33.4 us
    pallas_call x1 -> x6, Pallas kernels: 4.98 us -> 21.3 us  [the longest x1 7.87 us: inner(): pl.pallas_call(inner_kernel, out_shape=[jax.ShapeDtypeStruct((3 * SIDE *...]
    all_to_all x1, waiting for transfers between devices: 0.01 us -> 7.31 us  [per_device(): got = lax.all_to_all(sent, 'blk', split_axis=0, concat_axis=0, tiled=True)]
    add x11 -> x0, other arithmetic: 6.76 us -> none  [window_sum(): result + weights[offset] * lax.slice_in_dim(volume, offset, offset + leng...]
    all_to_all x1, starting transfers between devices: 10.4 us -> 4.97 us  [per_device(): lax.all_to_all(held, 'blk', split_axis=0, concat_axis=0, tiled=True)]
    all_to_all x1, waiting for transfers between devices: 13.1 us -> 7.98 us  [per_device(): lax.all_to_all(held, 'blk', split_axis=0, concat_axis=0, tiled=True)]
    another operation x4 -> x1, other arithmetic: 4.89 us -> 0.01 us  [per_device(): masks = jnp.stack([below[-1], mask_row, above[-1]])]
    ppermute x1, waiting for transfers between devices: 4.04 us -> 0.01 us  [per_device(): above = lax.ppermute(warped[:RIM], 'slab', shift_down('slab'))]
    unnamed x12 -> x17, local copies, waits for them, and re-layouts: 2.26 us -> 5.78 us
  transfers between devices with their start and end apart: 8 -> 8, of which waited for: 5 -> 4; matrix products, arithmetic and copies ran while one was open for 2% -> 1% of each run, Pallas kernels for 0% -> 10%
where the time goes in v2:
time: 119 us
  blocking collectives  33.9 us (28%)
  starting transfers between devices  33.4 us (28%)
  Pallas kernels  23.2 us (19%)
  waiting for transfers between devices  20.8 us (17%)
  local copies, waits for them, and re-layouts  6.67 us (6%)
    all_to_all x1, blocking collectives, per_device(): peak = lax.all_to_all(peak, 'slab', split_axis=0, concat_axis=0, tiled=True)  21.1 us
    all_to_all x1, blocking collectives, per_device(): peak = lax.all_to_all(peak, 'blk', split_axis=0, concat_axis=0, tiled=True)  12.8 us
    all_to_all x1, starting transfers between devices, per_device(): got = lax.all_to_all(sent, 'blk', split_axis=0, concat_axis=0, tiled=True)  10.4 us
    all_to_all x1, waiting for transfers between devices, per_device(): lax.all_to_all(held, 'blk', split_axis=0, concat_axis=0, tiled=True)  7.98 us
    pallas_call x1, Pallas kernels, inner(): pl.pallas_call(inner_kernel, out_shape=[jax.ShapeDtypeStruct((3 * SIDE *...  7.87 us
    all_to_all x1, waiting for transfers between devices, per_device(): got = lax.all_to_all(sent, 'blk', split_axis=0, concat_axis=0, tiled=True)  7.31 us
    unnamed x17, local copies, waits for them, and re-layouts  5.78 us
    ppermute x1, starting transfers between devices, per_device(): below = lax.ppermute(warped[side - RIM:], 'slab', shift_up('slab'))  5.49 us
  transfers between devices with their start and end apart: 8, of which 4 were waited for; matrix products, arithmetic and copies ran while one was open for 1% of the time, Pallas kernels for 10%

profile of v2, /device:TPU:1, one launch (start us, length us, event | category | flops | bytes accessed | tf_op | source)
XLA Modules:
  0.0 118.7 jit_solution(78000931508910369)
XLA Ops:
  0.0 0.7 copy.14.level_ref
  0.7 0.9 copy-done.2
  3.7 1.9 %pack.1 = bf16[32,66,128]{2,1,0:T(8,128)(2,1)} custom-call(s32[1,1,4,4]{3,2,1,0:T(4,128)S(1)} %copy-done.3, s32[1,1,4,4]{3,2,1,0:T(4,128)S(1)} %copy-done.4, s32[1,1,4]{2,1,0:T(1,128)S(1)} %copy-done.5, s32[1,1,4,3,4]{4,3,2,1,0:T(4,128)S(1)} %copy.14.level_ref, bf16[32,32,128]{2,1,0:T(8,128)(2,1)S(1)} %copy-done.2), custom_call_target="tpu_custom_call" | custom-call | tf_op jit(solution)/shard_map/pack/pallas_call | solution.py:99
  5.6 10.4 %all-to-all-start = ((bf16[32,66,128]{2,1,0:T(8,128)(2,1)}), bf16[32,66,128]{2,1,0:T(8,128)(2,1)S(1)}, u32[]{:S(2)}, u32[]{:S(2)}) async-start(bf16[32,66,128]{2,1,0:T(8,128)(2,1)} %pack.1), calls=%async_computation | async-start | bytes 1179648 | tf_op jit(solution)/shard_map/all_to_all | solution.py:527
  16.3 3.6 %collective-permute-start.2 = (bf16[161,128]{1,0:T(8,128)(2,1)S(1)}, bf16[161,128]{1,0:T(8,128)(2,1)S(1)}, u32[]{:S(2)}, u32[]{:S(2)}) collective-permute-start(bf16[161,128]{1,0:T(8,128)(2,1)S(1)} %get-tuple-element.33), channel_id=1, source_target_pairs={{0,32},{32,64},{64,96},{96,128},{128,160},{160,192},{192,224},{224... | collective-permute-start | bytes 123656 | tf_op jit(solution)/shard_map/ppermute | solution.py:533
  19.9 1.3 %collective-permute-start.3 = (bf16[161,128]{1,0:T(8,128)(2,1)S(1)}, bf16[161,128]{1,0:T(8,128)(2,1)S(1)}, u32[]{:S(2)}, u32[]{:S(2)}) collective-permute-start(bf16[161,128]{1,0:T(8,128)(2,1)S(1)} %get-tuple-element.34), channel_id=1, source_target_pairs={{32,0},{64,32},{96,64},{128,96},{160,128},{192,160},{224,192},{256... | collective-permute-start | bytes 123656 | tf_op jit(solution)/shard_map/ppermute | solution.py:534
  21.2 1.4 %collective-permute-done.2 = bf16[161,128]{1,0:T(8,128)(2,1)S(1)} collective-permute-done((bf16[161,128]{1,0:T(8,128)(2,1)S(1)}, bf16[161,128]{1,0:T(8,128)(2,1)S(1)}, u32[]{:S(2)}, u32[]{:S(2)}) %collective-permute-start.2) | collective-permute-done | bytes 41248 | tf_op jit(solution)/shard_map/ppermute | solution.py:533
  22.7 4.1 %collective-permute-done.3 = bf16[161,128]{1,0:T(8,128)(2,1)S(1)} collective-permute-done((bf16[161,128]{1,0:T(8,128)(2,1)S(1)}, bf16[161,128]{1,0:T(8,128)(2,1)S(1)}, u32[]{:S(2)}, u32[]{:S(2)}) %collective-permute-start.3) | collective-permute-done | bytes 41248 | tf_op jit(solution)/shard_map/ppermute | solution.py:534
  27.0 7.3 %all-to-all-done.got_ref = bf16[32,66,128]{2,1,0:T(8,128)(2,1)S(1)} async-done(((bf16[32,66,128]{2,1,0:T(8,128)(2,1)}), bf16[32,66,128]{2,1,0:T(8,128)(2,1)S(1)}, u32[]{:S(2)}, u32[]{:S(2)}) %all-to-all-start) | async-done | bytes 540704 | tf_op jit(solution)/shard_map/all_to_all | solution.py:527
  34.3 3.9 %hold.1 = bf16[32,48,128]{2,1,0:T(8,128)(2,1)} custom-call(bf16[32,66,128]{2,1,0:T(8,128)(2,1)S(1)} %all-to-all-done.got_ref), custom_call_target="tpu_custom_call" | custom-call | tf_op jit(solution)/shard_map/hold/pallas_call | solution.py:208
  38.4 3.3 %collective-permute-start.5 = (bf16[213,128]{1,0:T(8,128)(2,1)S(1)}, bf16[213,128]{1,0:T(8,128)(2,1)S(1)}, u32[]{:S(2)}, u32[]{:S(2)}) collective-permute-start(bf16[213,128]{1,0:T(8,128)(2,1)S(1)} %get-tuple-element.32), channel_id=1, source_target_pairs={{1,0},{2,1},{3,2},{4,3},{5,4},{6,5},{7,6},{8,7},{9,8},{10,9},{11,1... | collective-permute-start | bytes 163592 | tf_op jit(solution)/shard_map/ppermute | solution.py:547
  41.7 3.0 %collective-permute-start.4 = (bf16[213,128]{1,0:T(8,128)(2,1)S(1)}, bf16[213,128]{1,0:T(8,128)(2,1)S(1)}, u32[]{:S(2)}, u32[]{:S(2)}) collective-permute-start(bf16[213,128]{1,0:T(8,128)(2,1)S(1)} %get-tuple-element.31), channel_id=1, source_target_pairs={{0,1},{1,2},{2,3},{3,4},{4,5},{5,6},{6,7},{7,8},{8,9},{9,10},{10,1... | collective-permute-start | bytes 163592 | tf_op jit(solution)/shard_map/ppermute | solution.py:546
  44.8 5.0 %all-to-all-start.1 = ((bf16[32,48,128]{2,1,0:T(8,128)(2,1)}), bf16[32,48,128]{2,1,0:T(8,128)(2,1)S(1)}, u32[]{:S(2)}, u32[]{:S(2)}) async-start(bf16[32,48,128]{2,1,0:T(8,128)(2,1)} %hold.1), calls=%async_computation.1 | async-start | bytes 786432 | tf_op jit(solution)/shard_map/all_to_all | solution.py:542
  50.5 4.2 %fixed_part.1 = (f32[1824,128]{1,0:T(8,128)S(1)}, f32[1824,128]{1,0:T(8,128)S(1)}, f32[1824,128]{1,0:T(8,128)S(1)}) custom-call(bf16[2016,128]{1,0:T(8,128)(2,1)S(1)} %bitcast.16, f32[144,128]{1,0:T(8,128)S(1)} %bitcast.19), custom_call_target="tpu_custom_call" | custom-call | flops 5000000000 | bytes 4000000 | tf_op jit(solution)/shard_map/fixed_part/pallas_call | solution.py:304
  54.6 0.9 copy-done
  55.6 8.0 %all-to-all-done.1 = bf16[32,48,128]{2,1,0:T(8,128)(2,1)S(1)} async-done(((bf16[32,48,128]{2,1,0:T(8,128)(2,1)}), bf16[32,48,128]{2,1,0:T(8,128)(2,1)S(1)}, u32[]{:S(2)}, u32[]{:S(2)}) %all-to-all-start.1) | async-done | bytes 393248 | tf_op jit(solution)/shard_map/all_to_all | solution.py:542
  63.5 1.3 %collective-permute-start.1 = (bf16[5,48,128]{2,1,0:T(8,128)(2,1)S(1)}, bf16[5,48,128]{2,1,0:T(8,128)(2,1)S(1)}, u32[]{:S(2)}, u32[]{:S(2)}) collective-permute-start(bf16[5,48,128]{2,1,0:T(8,128)(2,1)S(1)} %get-tuple-element.27), channel_id=1, source_target_pairs={{32,0},{64,32},{96,64},{128,96},{160,128},{192,160},{224,192},{256... | collective-permute-start | bytes 184328 | tf_op jit(solution)/shard_map/ppermute | solution.py:571
  64.8 5.5 %collective-permute-start = (bf16[5,48,128]{2,1,0:T(8,128)(2,1)S(1)}, bf16[5,48,128]{2,1,0:T(8,128)(2,1)S(1)}, u32[]{:S(2)}, u32[]{:S(2)}) collective-permute-start(bf16[5,48,128]{2,1,0:T(8,128)(2,1)S(1)} %get-tuple-element.28), channel_id=1, source_target_pairs={{0,32},{32,64},{64,96},{96,128},{128,160},{160,192},{192,224},{224... | collective-permute-start | bytes 184328 | tf_op jit(solution)/shard_map/ppermute | solution.py:570
  70.4 1.2 copy-done.1
  71.5 7.9 %inner.1 = (f32[3072,128]{1,0:T(8,128)S(1)}, f32[3,576,128]{2,1,0:T(8,128)S(1)}, f32[32,128]{1,0:T(8,128)S(1)}) custom-call(bf16[1536,128]{1,0:T(8,128)(2,1)S(1)} %bitcast.14, bf16[2016,128]{1,0:T(8,128)(2,1)S(1)} %bitcast.17, f32[1824,128]{1,0:T(8,128)S(1)} %get-tuple-element.17.mean_ref, f32[1824,128]{1,0:T(8,128)S(1)} %get-tuple-element.18.away_ref, ...), custom_call_target="tpu_custom_call" | custom-call | flops 10000000000 | bytes 8000000 | tf_op jit(solution)/shard_map/inner/pallas_call | solution.py:438
  79.4 2.8 %rim.1 = (f32[3072,128]{1,0:T(8,128)S(1)}, f32[32,1,128]{2,1,0:T(1,128)S(1)}) custom-call(bf16[240,128]{1,0:T(8,128)(2,1)S(1)} %bitcast.21, bf16[240,128]{1,0:T(8,128)(2,1)S(1)} %bitcast.20, bf16[1536,128]{1,0:T(8,128)(2,1)S(1)} %bitcast.15, bf16[2016,128]{1,0:T(8,128)(2,1)S(1)} %bitcast.18, f32[1824,128]{1,0:T(8,128)S(1)} %get-tuple-element.17.mean_ref, ...), custom_call_target="tpu_custom_call" | custom-call | tf_op jit(solution)/shard_map/rim/pallas_call | solution.py:462
  82.2 12.8 %all_to_all.20.in_ref = f32[32,1,128]{2,1,0:T(1,128)S(1)} all-to-all(f32[32,1,128]{2,1,0:T(1,128)S(1)} %get-tuple-element.22), channel_id=1, replica_groups=mesh['slab'=16,'blk'=32] {'blk'}, dimensions={0} | all-to-all | bytes 32768 | tf_op jit(solution)/shard_map/all_to_all | solution.py:577
  95.1 21.1 %all_to_all.21.peaks_ref = f32[16,1,128]{2,1,0:T(1,128)S(1)} all-to-all(f32[16,1,128]{2,1,0:T(1,128)S(1)} %relay.1), channel_id=1, replica_groups=mesh['slab'=16,'blk'=32] {'slab'}, dimensions={0} | all-to-all | bytes 16384 | tf_op jit(solution)/shard_map/all_to_all | solution.py:579
  116.1 2.5 %finish.1 = f32[3,32,32,128]{3,2,1,0:T(8,128)} custom-call(f32[16,1,128]{2,1,0:T(1,128)S(1)} %all_to_all.21.peaks_ref, f32[3072,128]{1,0:T(8,128)S(1)} %get-tuple-element.23.core_ref, f32[3072,128]{1,0:T(8,128)S(1)} %get-tuple-element.24.rim_ref), custom_call_target="tpu_custom_call" | custom-call | tf_op jit(solution)/shard_map/finish/pallas_call | solution.py:513
  (56 shorter events, 3.3 us)
Async XLA Ops:
  0.0 16.0 %copy-start.7 = (s32[1,1,4]{2,1,0:T(1,128)S(1)}, s32[1,1,4]{2,1,0:T(1,128)}, u32[]{:S(2)}) copy-start(s32[1,1,4]{2,1,0:T(1,128)} %param.13) | copy-start | bytes 52
  0.7 0.9 copy-start.2
  1.7 0.7 copy-start.3
  2.3 0.7 copy-start.4
  3.0 0.7 copy-start.5
  3.7 12.5 %copy-start.6 = (bf16[32,32,128]{2,1,0:T(8,128)(2,1)S(1)}, bf16[32,32,128]{2,1,0:T(8,128)(2,1)}, u32[]{:S(2)}) copy-start(bf16[32,32,128]{2,1,0:T(8,128)(2,1)} %param.7) | copy-start | bytes 786436
  5.6 28.7 %all-to-all-start = ((bf16[32,66,128]{2,1,0:T(8,128)(2,1)}), bf16[32,66,128]{2,1,0:T(8,128)(2,1)S(1)}, u32[]{:S(2)}, u32[]{:S(2)}) async-start(bf16[32,66,128]{2,1,0:T(8,128)(2,1)} %pack.1), calls=%async_computation | async-start | bytes 1179648 | tf_op jit(solution)/shard_map/all_to_all | solution.py:527
  16.3 6.4 %collective-permute-start.2 = (bf16[161,128]{1,0:T(8,128)(2,1)S(1)}, bf16[161,128]{1,0:T(8,128)(2,1)S(1)}, u32[]{:S(2)}, u32[]{:S(2)}) collective-permute-start(bf16[161,128]{1,0:T(8,128)(2,1)S(1)} %get-tuple-element.33), channel_id=1, source_target_pairs={{0,32},{32,64},{64,96},{96,128},{128,160},{160,192},{192,224},{224... | collective-permute-start | bytes 123656 | tf_op jit(solution)/shard_map/ppermute | solution.py:533
  19.9 6.9 %collective-permute-start.3 = (bf16[161,128]{1,0:T(8,128)(2,1)S(1)}, bf16[161,128]{1,0:T(8,128)(2,1)S(1)}, u32[]{:S(2)}, u32[]{:S(2)}) collective-permute-start(bf16[161,128]{1,0:T(8,128)(2,1)S(1)} %get-tuple-element.34), channel_id=1, source_target_pairs={{32,0},{64,32},{96,64},{128,96},{160,128},{192,160},{224,192},{256... | collective-permute-start | bytes 123656 | tf_op jit(solution)/shard_map/ppermute | solution.py:534
  38.4 11.4 %collective-permute-start.5 = (bf16[213,128]{1,0:T(8,128)(2,1)S(1)}, bf16[213,128]{1,0:T(8,128)(2,1)S(1)}, u32[]{:S(2)}, u32[]{:S(2)}) collective-permute-start(bf16[213,128]{1,0:T(8,128)(2,1)S(1)} %get-tuple-element.32), channel_id=1, source_target_pairs={{1,0},{2,1},{3,2},{4,3},{5,4},{6,5},{7,6},{8,7},{9,8},{10,9},{11,1... | collective-permute-start | bytes 163592 | tf_op jit(solution)/shard_map/ppermute | solution.py:547
  41.7 8.1 %collective-permute-start.4 = (bf16[213,128]{1,0:T(8,128)(2,1)S(1)}, bf16[213,128]{1,0:T(8,128)(2,1)S(1)}, u32[]{:S(2)}, u32[]{:S(2)}) collective-permute-start(bf16[213,128]{1,0:T(8,128)(2,1)S(1)} %get-tuple-element.31), channel_id=1, source_target_pairs={{0,1},{1,2},{2,3},{3,4},{4,5},{5,6},{6,7},{7,8},{8,9},{9,10},{10,1... | collective-permute-start | bytes 163592 | tf_op jit(solution)/shard_map/ppermute | solution.py:546
  44.8 18.7 %all-to-all-start.1 = ((bf16[32,48,128]{2,1,0:T(8,128)(2,1)}), bf16[32,48,128]{2,1,0:T(8,128)(2,1)S(1)}, u32[]{:S(2)}, u32[]{:S(2)}) async-start(bf16[32,48,128]{2,1,0:T(8,128)(2,1)} %hold.1), calls=%async_computation.1 | async-start | bytes 786432 | tf_op jit(solution)/shard_map/all_to_all | solution.py:542
  54.6 0.9 copy-start
  63.5 15.9 %collective-permute-start.1 = (bf16[5,48,128]{2,1,0:T(8,128)(2,1)S(1)}, bf16[5,48,128]{2,1,0:T(8,128)(2,1)S(1)}, u32[]{:S(2)}, u32[]{:S(2)}) collective-permute-start(bf16[5,48,128]{2,1,0:T(8,128)(2,1)S(1)} %get-tuple-element.27), channel_id=1, source_target_pairs={{32,0},{64,32},{96,64},{128,96},{160,128},{192,160},{224,192},{256... | collective-permute-start | bytes 184328 | tf_op jit(solution)/shard_map/ppermute | solution.py:571
  64.8 14.6 %collective-permute-start = (bf16[5,48,128]{2,1,0:T(8,128)(2,1)S(1)}, bf16[5,48,128]{2,1,0:T(8,128)(2,1)S(1)}, u32[]{:S(2)}, u32[]{:S(2)}) collective-permute-start(bf16[5,48,128]{2,1,0:T(8,128)(2,1)S(1)} %get-tuple-element.28), channel_id=1, source_target_pairs={{0,32},{32,64},{64,96},{96,128},{128,160},{160,192},{192,224},{224... | collective-permute-start | bytes 184328 | tf_op jit(solution)/shard_map/ppermute | solution.py:570
  70.3 1.2 %copy-start.1 = (f32[1824,128]{1,0:T(8,128)S(1)}, f32[1824,128]{1,0:T(8,128)}, u32[]{:S(2)}) copy-start(f32[1824,128]{1,0:T(8,128)} %copy-done) | copy-start | bytes 2801668

commit v3 on v2

v3 whole, which is shorter than its diff:
```python
import math

import jax
import jax.numpy as jnp
from jax import lax
from jax.experimental import pallas as pl
from jax.experimental.pallas import tpu as pltpu
from jax.sharding import PartitionSpec as P

LEVELS = 8
BOX_RADIUS = 2
SMOOTH_RADIUS = 3
RIM = BOX_RADIUS + SMOOTH_RADIUS

sigma_smooth = 1.5
step_length = 2.0
var_eps = 1e-05
peak_eps = 1e-06


def smooth_weights(radius):
    raw = [math.exp(-(t * t) / (2.0 * sigma_smooth * sigma_smooth)) for t in range(-radius, radius + 1)]
    total = sum(raw)
    return [one / total for one in raw]


def shift_up(axis):
    n = lax.axis_size(axis)
    return [(i, i + 1) for i in range(n - 1)]


def shift_down(axis):
    n = lax.axis_size(axis)
    return [(i + 1, i) for i in range(n - 1)]


SIDE = 32
WIDTH = 128
BLOCKS = WIDTH // SIDE
SLOTS = 4
OWNERS = 32
DEEP = 2
HALF = SIDE // 2
TAKEN = DEEP + 1
SENT = TAKEN * HALF + TAKEN + 1
PITCH = 56
EXT = SIDE + 2 * RIM
OUT_PITCH = 48
PART = OUT_PITCH // DEEP
MID = SIDE + 2 * SMOOTH_RADIUS
INNER = SIDE - 2 * BOX_RADIUS
CORE = INNER - 2 * SMOOTH_RADIUS
ROW = OUT_PITCH
MIB = 1 << 20


def params(mib):
    return pltpu.CompilerParams(vmem_limit_bytes=mib * MIB)


def cost(flops, nbytes):
    return pl.CostEstimate(flops=flops, bytes_accessed=nbytes, transcendentals=0)


def in_vmem():
    return pl.BlockSpec(memory_space=pltpu.VMEM)


def in_smem():
    return pl.BlockSpec(memory_space=pltpu.SMEM)


def pack_kernel(owner_ref, block_ref, count_ref, level_ref, moving_ref, out_ref, wide):
    lane = lax.broadcasted_iota(jnp.int32, (TAKEN + 1, WIDTH), 1)
    row = jnp.zeros((TAKEN + 1, WIDTH), jnp.int32)
    e = BLOCKS * SLOTS
    for g in range(BLOCKS):
        count = count_ref[0, 0, g]
        row = jnp.where(lane == 4 * e + g, count, row)
        for k in range(SLOTS):
            name = block_ref[0, 0, g, k] * OWNERS + owner_ref[0, 0, g, k]
            row = jnp.where(lane == g * SLOTS + k, jnp.where(k < count, name, -1), row)
            for axis in range(3):
                at = e + (g * 3 + axis) * SLOTS + k
                row = jnp.where(lane == at, level_ref[0, 0, g, axis, k], row)
    row = row.astype(jnp.float32)
    for x in range(SIDE):
        wide[pl.ds(x * SIDE, SIDE), :] = moving_ref[x].astype(jnp.float32)
    place = lax.broadcasted_iota(jnp.int32, (TAKEN + 1, WIDTH), 0)
    for z in range(SIDE):
        plane = wide[pl.ds(z, SIDE, stride=SIDE), :].astype(jnp.bfloat16)
        spots = [(z // DEEP, z % DEEP)]
        if z % DEEP == 0 and z > 0:
            spots.append((z // DEEP - 1, DEEP))
        if z == SIDE - 1:
            spots.append((z // DEEP, DEEP))
        for pair, at in spots:
            for half in range(2):
                out_ref[pair * 2 + half, at * HALF : (at + 1) * HALF, :] = plane[half * HALF : (half + 1) * HALF]
    for pair in range(SIDE // DEEP):
        for half in range(2):
            x = min((half + 1) * HALF, SIDE - 1)
            if pair < SIDE // DEEP - 1:
                extra = wide[pl.ds(x * SIDE + pair * DEEP, TAKEN + 1), :]
            else:
                two = wide[pl.ds(x * SIDE + pair * DEEP, DEEP), :]
                extra = jnp.concatenate([two, two[1:2], two[1:2]], axis=0)
            extra = jnp.where(place == TAKEN, row, extra)
            out_ref[pair * 2 + half, TAKEN * HALF : SENT, :] = extra.astype(jnp.bfloat16)


def pack(owner, block, count, level, moving):
    return pl.pallas_call(
        pack_kernel,
        out_shape=jax.ShapeDtypeStruct((OWNERS, SENT, WIDTH), jnp.bfloat16),
        in_specs=[in_smem()] * 4 + [in_vmem()],
        out_specs=in_vmem(),
        scratch_shapes=[pltpu.VMEM((SIDE * SIDE, WIDTH), jnp.float32)],
        name="pack",
    )(owner, block, count, level, moving)


def exchange_groups(parts, lane):
    turned = [[p] + [pltpu.roll(p, SIDE * s, 1) for s in range(1, BLOCKS)] for p in parts]
    out = []
    for b in range(BLOCKS):
        pick = [turned[a][(a - b) % BLOCKS] for a in range(BLOCKS)]
        out.append(
            jnp.where(
                lane < 2 * SIDE,
                jnp.where(lane < SIDE, pick[0], pick[1]),
                jnp.where(lane < 3 * SIDE, pick[2], pick[3]),
            )
        )
    return out


def hold_kernel(half_ref, got_ref, out_ref, wide, source, coef, mixed, spread):
    strip = HALF // BLOCKS
    rows = OWNERS * BLOCKS
    lane = lax.broadcasted_iota(jnp.int32, (OWNERS, WIDTH), 1)
    last_y = lane % SIDE == SIDE - 1
    for o in range(OWNERS):
        wide[pl.ds(o * PITCH, SENT), :] = got_ref[o].astype(jnp.float32)

    lists = wide[pl.ds(SENT - 1, OWNERS, stride=PITCH), :]
    where_k = lane.astype(jnp.float32)
    e = BLOCKS * SLOTS
    top = float(LEVELS)
    scales = []
    for g in range(BLOCKS):
        total = {}
        for k in range(SLOTS):
            at = g * SLOTS + k
            name = lists[:, at : at + 1]
            base = e + g * 3 * SLOTS + k
            lx, lz, ly = (lists[:, base + a * SLOTS : base + a * SLOTS + 1] for a in range(3))
            hit = jnp.where(where_k == name, 1.0, 0.0)
            for dx in range(2):
                ax = hit * (lx if dx else top - lx)
                for dz in range(2):
                    az = ax * (lz if dz else top - lz)
                    for dy in range(2):
                        ay = az * (ly if dy else top - ly)
                        key = (dx, dz, dy)
                        total[key] = ay if k == 0 else total[key] + ay
        for (dx, dz, dy), c in total.items():
            hi = jnp.floor(c * (1.0 / 16.0)) * 16.0
            col = pl.ds(dy * WIDTH, WIDTH)
            coef[dz * 2 + dx, pl.ds(g * OWNERS, OWNERS), col] = hi.astype(jnp.bfloat16)
            coef[dz * 2 + dx, pl.ds(rows + g * OWNERS, OWNERS), col] = (c - hi).astype(jnp.bfloat16)
        count = lists[:, 4 * e + g : 4 * e + g + 1]
        scales.append((1.0 / count) * (1.0 / LEVELS**3))

    wrap = strip + 1
    for z in range(TAKEN):
        for t in range(wrap):
            at = [strip * q + t for q in range(BLOCKS)]
            parts = [
                wide[pl.ds(z * HALF + x if x < HALF else TAKEN * HALF + z, OWNERS, stride=PITCH), :] for x in at
            ]
            for g, u in enumerate(exchange_groups(parts, lane)):
                v = jnp.where(last_y, u, pltpu.roll(u, WIDTH - 1, 1))
                for dy, a in enumerate((u, v)):
                    source[pl.ds(dy * rows + g * OWNERS, OWNERS), pl.ds((z * wrap + t) * WIDTH, WIDTH)] = a.astype(
                        jnp.bfloat16
                    )

    piece = 2 * WIDTH
    for z in range(DEEP):
        for t in range(0, strip, 2):
            acc = None
            for dz in range(2):
                for dx in range(2):
                    col = ((z + dz) * wrap + t + dx) * WIDTH
                    one = jnp.dot(
                        coef[dz * 2 + dx], source[:, pl.ds(col, piece)], preferred_element_type=jnp.float32
                    )
                    acc = one if acc is None else acc + one
            for g in range(BLOCKS):
                lo = rows + g * OWNERS
                part = acc[g * OWNERS : (g + 1) * OWNERS] + acc[lo : lo + OWNERS]
                mixed[pl.ds(g * OWNERS, OWNERS), pl.ds((z * strip + t) * WIDTH, piece)] = part * scales[g]

    for r in range(OWNERS):
        for z in range(DEEP):
            spread[pl.ds((r + 1) * OUT_PITCH + z * PART + HALF, PART - HALF), :] = jnp.zeros(
                (PART - HALF, WIDTH), jnp.float32
            )
    for z in range(DEEP):
        for t in range(strip):
            parts = [
                mixed[pl.ds(g * OWNERS, OWNERS), pl.ds((z * strip + t) * WIDTH, WIDTH)] for g in range(BLOCKS)
            ]
            for q, w in enumerate(exchange_groups(parts, lane)):
                spread[pl.ds(OUT_PITCH + z * PART + strip * q + t, OWNERS, stride=OUT_PITCH), :] = w
    half = half_ref[0]

    @pl.when(half == 0)
    def _():
        for z in range(DEEP):
            for k in range(RIM):
                w = spread[pl.ds(OUT_PITCH + z * PART + k, OWNERS, stride=OUT_PITCH), :]
                spread[pl.ds(z * PART + HALF + k, OWNERS, stride=OUT_PITCH), :] = w

    @pl.when(half == 1)
    def _():
        for z in range(DEEP):
            for k in range(RIM):
                w = spread[pl.ds(OUT_PITCH + z * PART + HALF - RIM + k, OWNERS, stride=OUT_PITCH), :]
                spread[pl.ds(2 * OUT_PITCH + z * PART + PART - RIM + k, OWNERS, stride=OUT_PITCH), :] = w

    for r in range(OWNERS):
        out_ref[r] = spread[pl.ds((r + 1) * OUT_PITCH, OUT_PITCH), :].astype(jnp.bfloat16)


def hold(half, got):
    strip = HALF // BLOCKS
    rows = OWNERS * BLOCKS
    return pl.pallas_call(
        hold_kernel,
        out_shape=jax.ShapeDtypeStruct((OWNERS, OUT_PITCH, WIDTH), jnp.bfloat16),
        in_specs=[in_smem(), in_vmem()],
        out_specs=in_vmem(),
        scratch_shapes=[
            pltpu.VMEM((OWNERS * PITCH, WIDTH), jnp.float32),
            pltpu.VMEM((2 * rows, TAKEN * (strip + 1) * WIDTH), jnp.bfloat16),
            pltpu.VMEM((4, 2 * rows, 2 * rows), jnp.bfloat16),
            pltpu.VMEM((rows, DEEP * strip * WIDTH), jnp.float32),
            pltpu.VMEM(((OWNERS + 2) * OUT_PITCH, WIDTH), jnp.float32),
        ],
        compiler_params=params(12),
        name="hold",
    )(half, got)


def distance():
    i = lax.broadcasted_iota(jnp.int32, (WIDTH, WIDTH), 0)
    j = lax.broadcasted_iota(jnp.int32, (WIDTH, WIDTH), 1)
    return jnp.abs(i - j)


def box_band():
    one = jnp.where(distance() <= BOX_RADIUS, 1.0, 0.0).astype(jnp.bfloat16)
    return one, jnp.concatenate([one, one], axis=0)


def smooth_band():
    d = distance()
    taps = smooth_weights(SMOOTH_RADIUS)
    left = jnp.zeros((WIDTH, WIDTH), jnp.float32)
    for t in range(SMOOTH_RADIUS + 1):
        left = jnp.where(d == t, taps[SMOOTH_RADIUS + t], left)
    parts = []
    for _ in range(3):
        part = left.astype(jnp.bfloat16)
        parts.append(part)
        left = left - part.astype(jnp.float32)
    return jnp.concatenate(parts, axis=0)


def times(a, band):
    return jnp.dot(a, band, preferred_element_type=jnp.float32)


def halves(product):
    hi = product.astype(jnp.bfloat16)
    return jnp.concatenate([hi, (product - hi.astype(jnp.float32)).astype(jnp.bfloat16)], axis=1)


def rows_at(i):
    if isinstance(i, int):
        return pl.ds(i * ROW, ROW)
    return pl.ds(pl.multiple_of(i * ROW, ROW), ROW)


def along(a, step):
    return pltpu.roll(a, (-step) % ROW, 0)


def box_zx(ref, which, i):
    r = [ref[which, rows_at(i + t), :] for t in range(2 * BOX_RADIUS + 1)]
    a = ((r[0] + r[1]) + (r[2] + r[3])) + r[4]
    two = a + along(a, -1)
    return ((along(two, -1) + a) + along(two, 2)) * (1.0 / (2 * BOX_RADIUS + 1) ** 3)


def mask_rows(ref):
    x = lax.broadcasted_iota(jnp.int32, (ROW, WIDTH), 0)
    m = ref[...].astype(jnp.float32)
    right = jnp.where(x < SIDE + SMOOTH_RADIUS, m[1:2], 0.0)
    return jnp.where(x < SIDE, m[0:1], jnp.where(x >= ROW - SMOOTH_RADIUS, m[2:3], right))


def fixed_sums(f, sums, q, rows, bands):
    sums[q, rows, :] = times(f, bands[0])
    wide = f.astype(jnp.float32)
    sums[q + 1, rows, :] = times(halves(wide * wide), bands[1])


def fixed_row(sums, q, i, here, mask, mean_ref, away_ref, gain_ref, k):
    mean = box_zx(sums, q, i)
    var = box_zx(sums, q + 1, i) - mean * mean + var_eps
    mean_ref[rows_at(k), :] = mean
    away_ref[rows_at(k), :] = here - mean
    gain_ref[rows_at(k), :] = mask / var


def fixed_kernel(fixed_ref, mask_ref, mean_ref, away_ref, gain_ref, sums):
    bands = box_band()
    chunk = 4 * ROW

    def by_y(i, carry):
        rows = pl.ds(pl.multiple_of(i * chunk, chunk), chunk)
        fixed_sums(fixed_ref[rows, :], sums, 0, rows, bands)
        return carry

    lax.fori_loop(0, SIDE // 4, by_y, 0)
    mask = mask_rows(mask_ref)

    def by_z(i, carry):
        here = fixed_ref[rows_at(i + BOX_RADIUS), :].astype(jnp.float32)
        fixed_row(sums, 0, i, here, mask, mean_ref, away_ref, gain_ref, i)
        return carry

    lax.fori_loop(0, INNER, by_z, 0)


def fixed_part(fixed, mask):
    out = jax.ShapeDtypeStruct((INNER * ROW, WIDTH), jnp.float32)
    return pl.pallas_call(
        fixed_kernel,
        out_shape=[out] * 3,
        in_specs=[in_vmem()] * 2,
        out_specs=[in_vmem()] * 3,
        scratch_shapes=[pltpu.VMEM((2, SIDE * ROW, WIDTH), jnp.float32)],
        compiler_params=params(8),
        cost_estimate=cost(5_000_000_000, 4_000_000),
        name="fixed_part",
    )(fixed, mask)


def sums_by_y(f, wide, sums, rows, bands):
    mw = wide[rows, :]
    m = mw.astype(jnp.bfloat16)
    sums[0, rows, :] = times(m, bands[0])
    sums[1, rows, :] = times(halves(mw * mw), bands[1])
    sums[2, rows, :] = times(halves(mw * f.astype(jnp.float32)), bands[1])


def force_row(wide, sums, i, mean_ref, away_ref, gain_ref, j, force, k):
    mean = box_zx(sums, 0, i)
    var = box_zx(sums, 1, i) - mean * mean + var_eps
    cov = box_zx(sums, 2, i) - mean_ref[rows_at(j), :] * mean
    q = cov / var
    m = wide[rows_at(i + BOX_RADIUS), :]
    term = gain_ref[rows_at(j), :] * q * (away_ref[rows_at(j), :] - q * (m - mean))
    lane = lax.broadcasted_iota(jnp.int32, (ROW, WIDTH), 1)
    up = jnp.where(lane == WIDTH - 1, 0.0, pltpu.roll(m, WIDTH - 1, 1))
    down = jnp.where(lane == 0, 0.0, pltpu.roll(m, 1, 1))
    force[0, rows_at(k), :] = (term * (along(m, 1) - along(m, -1))).astype(jnp.bfloat16)
    z_step = wide[rows_at(i + BOX_RADIUS + 1), :] - wide[rows_at(i + BOX_RADIUS - 1), :]
    force[1, rows_at(k), :] = (term * z_step).astype(jnp.bfloat16)
    force[2, rows_at(k), :] = (term * (up - down)).astype(jnp.bfloat16)


def smooth_row(smooth_y, i, out_ref, z, peak):
    taps = smooth_weights(SMOOTH_RADIUS)[SMOOTH_RADIUS:]
    total = None
    for c in range(3):
        g = [smooth_y[c, rows_at(i + t), :] for t in range(2 * SMOOTH_RADIUS + 1)]
        mid = SMOOTH_RADIUS
        s = taps[0] * g[mid]
        for t in range(1, SMOOTH_RADIUS + 1):
            s += taps[t] * (g[mid - t] + g[mid + t])
        a = taps[0] * s
        for t in range(1, SMOOTH_RADIUS + 1):
            a += taps[t] * (along(s, -t) + along(s, t))
        a = a[:SIDE]
        out_ref[pl.ds(c * SIDE * SIDE + z, SIDE, stride=SIDE), :] = a
        total = a * a if total is None else total + a * a
    return jnp.maximum(peak, total)


def inner_kernel(warped_ref, fixed_ref, mean_ref, away_ref, gain_ref, out_ref, edge_ref, peak_ref, wide, sums, force, smooth_y):
    bands = box_band()
    triple = smooth_band()
    chunk = 4 * ROW

    def by_y(i, carry):
        for step in range(2):
            pair = 2 * i + step
            for half in range(2):
                for z in range(DEEP):
                    src = (pair * 2 + half) * OUT_PITCH + z * PART
                    dst = (pair * DEEP + z) * ROW
                    own = warped_ref[pl.ds(pl.multiple_of(src, 8), HALF), :]
                    wide[pl.ds(pl.multiple_of(dst + half * HALF, 8), HALF), :] = own.astype(jnp.float32)
                    side = warped_ref[pl.ds(pl.multiple_of(src + HALF, 8), 8), :]
                    wide[pl.ds(pl.multiple_of(dst + SIDE + 8 * half, 8), 8), :] = side.astype(jnp.float32)
        rows = pl.ds(pl.multiple_of(i * chunk, chunk), chunk)
        sums_by_y(fixed_ref[rows, :], wide, sums, rows, bands)
        return carry

    lax.fori_loop(0, SIDE // 4, by_y, 0)

    def by_z(i, carry):
        force_row(wide, sums, i, mean_ref, away_ref, gain_ref, i, force, i)
        return carry

    lax.fori_loop(0, INNER, by_z, 0)

    def smooth(i, carry):
        rows = pl.ds(pl.multiple_of(i * chunk, chunk), chunk)
        for c in range(3):
            f = force[c, rows, :]
            smooth_y[c, rows, :] = times(jnp.concatenate([f, f, f], axis=1), triple)
        return carry

    lax.fori_loop(0, INNER // 4, smooth, 0)
    kept = 2 * SMOOTH_RADIUS * ROW
    for c in range(3):
        edge_ref[c, 0:kept, :] = smooth_y[c, 0:kept, :]
        edge_ref[c, kept : 2 * kept, :] = smooth_y[c, INNER * ROW - kept : INNER * ROW, :]
    peak_ref[...] = lax.fori_loop(
        0, CORE, lambda i, peak: smooth_row(smooth_y, i, out_ref, i + RIM, peak), jnp.zeros((SIDE, WIDTH), jnp.float32)
    )


def rim_kernel(
    below_ref, above_ref, head_ref, tail_ref, mask_ref, edge_ref, first_ref,
    out_ref, peak_ref, wide, fwide, sums, fmean, faway, fgain, force, smooth_y,
):
    bands = box_band()
    triple = smooth_band()
    own = RIM - 1
    stack = RIM + own
    for ref, start, count, at in (
        (below_ref, 0, RIM, 0),
        (head_ref, 0, own, RIM),
        (tail_ref, RIM - own, own, stack),
        (above_ref, 0, RIM, stack + own),
    ):
        rows = pl.ds(at * ROW, count * ROW)
        f = ref[pl.ds((RIM + start) * ROW, count * ROW), :]
        wide[rows, :] = ref[pl.ds(start * ROW, count * ROW), :].astype(jnp.float32)
        fwide[rows, :] = f.astype(jnp.float32)
        sums_by_y(f, wide, sums, rows, bands)
        fixed_sums(f, sums, 3, rows, bands)
    here = mask_rows(mask_ref)
    last = pl.ds(2 * RIM * ROW, 8)
    masks = [mask_rows(below_ref.at[last, :]), here, mask_rows(above_ref.at[last, :])]

    def by_z(i, carry):
        side = jnp.where(i < RIM, 0, 1)
        first = stack * side + i - RIM * side
        outer = jnp.where(side == 0, masks[0], masks[2])
        mask = jnp.where((i >= SMOOTH_RADIUS) & (i < 2 * RIM - SMOOTH_RADIUS), masks[1], outer)
        fixed_row(sums, 3, first, fwide[rows_at(first + BOX_RADIUS), :], mask, fmean, faway, fgain, i)
        force_row(wide, sums, first, fmean, faway, fgain, i, force, i)
        return carry

    lax.fori_loop(0, 2 * RIM, by_z, 0)
    kept = 2 * SMOOTH_RADIUS
    tall = RIM + kept
    for c in range(3):
        for side in range(2):
            f = force[c, pl.ds(side * RIM * ROW, RIM * ROW), :]
            new = (side * tall + (kept if side else 0)) * ROW
            smooth_y[c, pl.ds(new, RIM * ROW), :] = times(jnp.concatenate([f, f, f], axis=1), triple)
            old = (side * tall + (0 if side else RIM)) * ROW
            smooth_y[c, pl.ds(old, kept * ROW), :] = edge_ref[c, pl.ds(side * kept * ROW, kept * ROW), :]

    def smooth(i, peak):
        side = jnp.where(i < RIM, 0, 1)
        j = i - RIM * side
        return smooth_row(smooth_y, tall * side + j, out_ref, (SIDE - RIM) * side + j, peak)

    peak = lax.fori_loop(0, 2 * RIM, smooth, first_ref[...])
    top = jnp.max(jnp.max(peak, axis=0, keepdims=True), axis=1, keepdims=True)
    peak_ref[...] = jnp.broadcast_to(top.reshape(1, 1, 1), peak_ref.shape)


def inner(warped, fixed, mean, away, gain):
    return pl.pallas_call(
        inner_kernel,
        out_shape=[
            jax.ShapeDtypeStruct((3 * SIDE * SIDE, WIDTH), jnp.float32),
            jax.ShapeDtypeStruct((3, 4 * SMOOTH_RADIUS * ROW, WIDTH), jnp.float32),
            jax.ShapeDtypeStruct((SIDE, WIDTH), jnp.float32),
        ],
        in_specs=[in_vmem()] * 5,
        out_specs=[in_vmem()] * 3,
        scratch_shapes=[
            pltpu.VMEM((SIDE * ROW, WIDTH), jnp.float32),
            pltpu.VMEM((3, SIDE * ROW, WIDTH), jnp.float32),
            pltpu.VMEM((3, INNER * ROW, WIDTH), jnp.bfloat16),
            pltpu.VMEM((3, INNER * ROW, WIDTH), jnp.float32),
        ],
        compiler_params=params(14),
        cost_estimate=cost(10_000_000_000, 8_000_000),
        name="inner",
    )(warped, fixed, mean, away, gain)


def rim(below, above, head, tail, mask, edge, first):
    stack = 2 * (2 * RIM - 1) * ROW
    tall = 2 * (RIM + 2 * SMOOTH_RADIUS) * ROW
    return pl.pallas_call(
        rim_kernel,
        out_shape=[
            jax.ShapeDtypeStruct((3 * SIDE * SIDE, WIDTH), jnp.float32),
            jax.ShapeDtypeStruct((OWNERS, 1, WIDTH), jnp.float32),
        ],
        in_specs=[in_vmem()] * 7,
        out_specs=[in_vmem()] * 2,
        scratch_shapes=[pltpu.VMEM((stack, WIDTH), jnp.float32)] * 2
        + [pltpu.VMEM((5, stack, WIDTH), jnp.float32)]
        + [pltpu.VMEM((2 * RIM * ROW, WIDTH), jnp.float32)] * 3
        + [
            pltpu.VMEM((3, 2 * RIM * ROW, WIDTH), jnp.bfloat16),
            pltpu.VMEM((3, tall, WIDTH), jnp.float32),
        ],
        compiler_params=params(14),
        name="rim",
    )(below, above, head, tail, mask, edge, first)


def relay_kernel(in_ref, out_ref):
    a = jnp.max(in_ref[...].reshape(in_ref.shape[0], WIDTH), axis=0, keepdims=True)
    out_ref[...] = jnp.broadcast_to(a.reshape(1, 1, WIDTH), out_ref.shape)


def relay(tiles, count):
    return pl.pallas_call(
        relay_kernel,
        out_shape=jax.ShapeDtypeStruct((count, 1, WIDTH), jnp.float32),
        in_specs=[in_vmem()],
        out_specs=in_vmem(),
        compiler_params=params(1),
        name="relay",
    )(tiles)


STEP_X = 8


def finish_kernel(peaks_ref, core_ref, rim_ref, out_ref):
    x0 = pl.program_id(0) * STEP_X
    peak = jnp.sqrt(jnp.max(peaks_ref[...].reshape(peaks_ref.shape[0], WIDTH), axis=0, keepdims=True))
    scale = step_length / (peak + peak_eps)
    z = lax.broadcasted_iota(jnp.int32, (SIDE, WIDTH), 0)
    at_rim = (z < RIM) | (z >= SIDE - RIM)
    for c in range(3):
        for x in range(STEP_X):
            rows = pl.ds(pl.multiple_of((c * SIDE + x0 + x) * SIDE, SIDE), SIDE)
            out_ref[c, x] = jnp.where(at_rim, rim_ref[rows, :], core_ref[rows, :]) * scale


def finish(peaks, core, rims):
    return pl.pallas_call(
        finish_kernel,
        out_shape=jax.ShapeDtypeStruct((3, SIDE, SIDE, WIDTH), jnp.float32),
        grid=(SIDE // STEP_X,),
        in_specs=[in_vmem()] * 3,
        out_specs=pl.BlockSpec((3, STEP_X, SIDE, WIDTH), lambda i: (0, i, 0, 0)),
        compiler_params=params(12),
        name="finish",
    )(peaks, core, rims)


def per_device(fixed_image, moving_image, fetch_owner, fetch_block, fetch_count, interp_level, block_mask):
    side, width = SIDE, WIDTH
    sent = pack(fetch_owner, fetch_block, fetch_count, interp_level, moving_image)
    got = lax.all_to_all(sent, "blk", split_axis=0, concat_axis=0, tiled=True)

    mask_row = jnp.repeat(block_mask.reshape(BLOCKS), side).astype(jnp.bfloat16)[None]
    last = jnp.concatenate([fixed_image[side - RIM :].reshape(-1, width), mask_row], axis=0)
    first = jnp.concatenate([fixed_image[:RIM].reshape(-1, width), mask_row], axis=0)
    left = lax.ppermute(last, "blk", shift_up("blk"))
    right = lax.ppermute(first, "blk", shift_down("blk"))
    turn = lambda a: a[:-1].reshape(RIM, side, width)
    fixed = jnp.concatenate(
        [fixed_image, turn(right), jnp.zeros((ROW - EXT, side, width), jnp.bfloat16), turn(left)], axis=0
    ).transpose(1, 0, 2)
    masks = jnp.concatenate([mask_row, right[-1:], left[-1:], jnp.zeros((5, width), jnp.bfloat16)], axis=0)
    mean, away, gain = fixed_part(fixed.reshape(side * ROW, width), masks)

    half = (lax.axis_index("blk") % 2).astype(jnp.int32).reshape(1)
    warped = lax.all_to_all(hold(half, got), "blk", split_axis=0, concat_axis=0, tiled=True)

    def z_rows(pairs):
        part = warped.reshape(side // DEEP, 2, DEEP, PART, width)[pairs]
        rows = [part[:, 0, :, :HALF], part[:, 1, :, :HALF], part[:, 0, :, HALF:], part[:, 1, :, HALF:]]
        return jnp.concatenate(rows, axis=2).reshape(-1, ROW, width)

    def message(moving_rows, fixed_rows):
        return jnp.concatenate([moving_rows.reshape(-1, width), fixed_rows.reshape(-1, width), masks], axis=0)

    tail = message(z_rows(slice(side // DEEP - 3, None))[1:], fixed[side - RIM :])
    head = message(z_rows(slice(0, 3))[:RIM], fixed[:RIM])
    below = lax.ppermute(tail, "slab", shift_up("slab"))
    above = lax.ppermute(head, "slab", shift_down("slab"))
    core, edge, top = inner(warped.reshape(side * ROW, width), fixed.reshape(side * ROW, width), mean, away, gain)
    rims, peak = rim(below, above, head, tail, masks, edge, top)
    peak = lax.all_to_all(peak, "blk", split_axis=0, concat_axis=0, tiled=True)
    peak = relay(peak, lax.axis_size("slab"))
    peak = lax.all_to_all(peak, "slab", split_axis=0, concat_axis=0, tiled=True)
    return finish(peak, core, rims)


def solution(mesh):
    in_specs = (
        P("blk", "slab", None),
        P("blk", "slab", None),
        P("blk", "slab", None, None),
        P("blk", "slab", None, None),
        P("blk", "slab", None),
        P("blk", "slab", None, None, None),
        P("blk", "slab", None),
    )
    return jax.shard_map(
        per_device, mesh=mesh, in_specs=in_specs, out_specs=P(None, "blk", "slab", None), check_vma=False
    )
```

time: 119 us -> 107 us (0.90)
  starting transfers between devices: 33.4 us -> 28 us
  local copies, waits for them, and re-layouts: 6.67 us -> 1.99 us
  Pallas kernels: 23.2 us -> 21.9 us
    ppermute x4 -> x2, starting transfers between devices: 13.1 us -> 5.47 us  [the longest x1 3.55 us: per_device(): left = lax.ppermute(last, 'blk', shift_up('blk'))]
    unnamed x17 -> x5, local copies, waits for them, and re-layouts: 5.78 us -> 1.34 us
    ppermute x1, waiting for transfers between devices: 4.12 us -> 0.01 us  [per_device(): above = lax.ppermute(head, 'slab', shift_down('slab'))]
    ppermute x4 -> x2, waiting for transfers between devices: 0.01 us -> 4.07 us  [the longest x1 4.07 us: per_device(): right = lax.ppermute(first, 'blk', shift_down('blk'))]
    all_to_all x1, waiting for transfers between devices: 7.98 us -> 10.9 us  [per_device(): lax.all_to_all(hold(half, got), 'blk', split_axis=0, concat_axis=0, tiled...]
    all_to_all x1, waiting for transfers between devices: 7.31 us -> 5.07 us  [per_device(): got = lax.all_to_all(sent, 'blk', split_axis=0, concat_axis=0, tiled=True)]
    ppermute x1, starting transfers between devices: 3.65 us -> 5.49 us  [per_device(): below = lax.ppermute(tail, 'slab', shift_up('slab'))]
    pallas_call x1, Pallas kernels: 4.16 us -> 2.68 us  [fixed_part(): pl.pallas_call(fixed_kernel, out_shape=[out] * 3, in_specs=[in_vmem()] *...]
  transfers between devices with their start and end apart: 8 -> 6, of which waited for: 4 -> 3; matrix products, arithmetic and copies ran while one was open for 1% -> 1% of each run, Pallas kernels for 10% -> 10%
where the time goes in v3:
time: 107 us; the launch traced here: 106 us
  blocking collectives  33.9 us (32%)
  starting transfers between devices  28 us (26%)
  Pallas kernels  21.9 us (20%)
  waiting for transfers between devices  20.1 us (19%)
  local copies, waits for them, and re-layouts  1.99 us (2%)
    all_to_all x1, blocking collectives, per_device(): peak = lax.all_to_all(peak, 'slab', split_axis=0, concat_axis=0, tiled=True)  21.1 us
    all_to_all x1, blocking collectives, per_device(): peak = lax.all_to_all(peak, 'blk', split_axis=0, concat_axis=0, tiled=True)  12.9 us
    all_to_all x1, waiting for transfers between devices, per_device(): lax.all_to_all(hold(half, got), 'blk', split_axis=0, concat_axis=0, tiled...  10.9 us
    all_to_all x1, starting transfers between devices, per_device(): got = lax.all_to_all(sent, 'blk', split_axis=0, concat_axis=0, tiled=True)  10.4 us
    pallas_call x1, Pallas kernels, inner(): pl.pallas_call(inner_kernel, out_shape=[jax.ShapeDtypeStruct((3 * SIDE *...  8.31 us
    ppermute x1, starting transfers between devices, per_device(): below = lax.ppermute(tail, 'slab', shift_up('slab'))  5.49 us
    all_to_all x1, starting transfers between devices, per_device(): lax.all_to_all(hold(half, got), 'blk', split_axis=0, concat_axis=0, tiled...  5.37 us
    all_to_all x1, waiting for transfers between devices, per_device(): got = lax.all_to_all(sent, 'blk', split_axis=0, concat_axis=0, tiled=True)  5.07 us
  transfers between devices with their start and end apart: 6, of which 3 were waited for; matrix products, arithmetic and copies ran while one was open for 1% of the time, Pallas kernels for 10%

profile of v3, /device:TPU:1, one launch (start us, length us, event | category | flops | bytes accessed | tf_op | source)
XLA Modules:
  0.0 106.3 jit_solution(5233608847180906244)
XLA Ops:
  0.0 1.3 %copy.8.level_ref = s32[1,1,4,3,4]{4,3,2,1,0:T(4,128)} copy(s32[1,1,4,3,4]{4,2,3,1,0:T(4,128)} %param.12) | data formatting | bytes 384 | tf_op args[5]
  1.3 2.1 %pack.1 = bf16[32,52,128]{2,1,0:T(8,128)(2,1)} custom-call(s32[1,1,4,4]{3,2,1,0:T(4,128)} %owner_ref.1, s32[1,1,4,4]{3,2,1,0:T(4,128)} %block_ref.1, s32[1,1,4]{2,1,0:T(1,128)} %count_ref.1, s32[1,1,4,3,4]{4,3,2,1,0:T(4,128)} %copy.8.level_ref, bf16[32,32,128]{2,1,0:T(8,128)(2,1)} %moving_ref.1), custom_call_target="tpu_custom_call" | custom-call | tf_op jit(solution)/shard_map/pack/pallas_call | solution.py:113
  3.4 10.4 %all-to-all-start = ((bf16[32,52,128]{2,1,0:T(8,128)(2,1)}), bf16[32,52,128]{2,1,0:T(8,128)(2,1)S(1)}, u32[]{:S(2)}, u32[]{:S(2)}) async-start(bf16[32,52,128]{2,1,0:T(8,128)(2,1)} %pack.1), calls=%async_computation | async-start | bytes 917504 | tf_op jit(solution)/shard_map/all_to_all | solution.py:595
  13.8 0.1 broadcast_in_dim.10
  13.9 0.1 convert_element_type.19
  14.0 3.5 %collective-permute-start.1 = (bf16[161,128]{1,0:T(8,128)(2,1)S(1)}, bf16[161,128]{1,0:T(8,128)(2,1)S(1)}, u32[]{:S(2)}, u32[]{:S(2)}) collective-permute-start(bf16[161,128]{1,0:T(8,128)(2,1)S(1)} %get-tuple-element.36), channel_id=1, source_target_pairs={{0,1},{1,2},{2,3},{3,4},{4,5},{5,6},{6,7},{7,8},{8,9},{9,10},{10,1... | collective-permute-start | bytes 123656 | tf_op jit(solution)/shard_map/ppermute | solution.py:600
  17.6 1.9 %collective-permute-start = (bf16[161,128]{1,0:T(8,128)(2,1)S(1)}, bf16[161,128]{1,0:T(8,128)(2,1)S(1)}, u32[]{:S(2)}, u32[]{:S(2)}) collective-permute-start(bf16[161,128]{1,0:T(8,128)(2,1)S(1)} %get-tuple-element.35), channel_id=1, source_target_pairs={{1,0},{2,1},{3,2},{4,3},{5,4},{6,5},{7,6},{8,7},{9,8},{10,9},{11,1... | collective-permute-start | bytes 123656 | tf_op jit(solution)/shard_map/ppermute | solution.py:601
  19.5 0.1 pad.10.clone
  19.6 4.1 %collective-permute-done = bf16[161,128]{1,0:T(8,128)(2,1)S(1)} collective-permute-done((bf16[161,128]{1,0:T(8,128)(2,1)S(1)}, bf16[161,128]{1,0:T(8,128)(2,1)S(1)}, u32[]{:S(2)}, u32[]{:S(2)}) %collective-permute-start) | collective-permute-done | bytes 41248 | tf_op jit(solution)/shard_map/ppermute | solution.py:601
  23.7 0.1 maximum_bitcast_fusion
  23.8 0.2 copy.11
  24.0 5.1 %all-to-all-done.got_ref = bf16[32,52,128]{2,1,0:T(8,128)(2,1)S(1)} async-done(((bf16[32,52,128]{2,1,0:T(8,128)(2,1)}), bf16[32,52,128]{2,1,0:T(8,128)(2,1)S(1)}, u32[]{:S(2)}, u32[]{:S(2)}) %all-to-all-start) | async-done | bytes 426016 | tf_op jit(solution)/shard_map/all_to_all | solution.py:595
  29.0 3.8 %hold.1 = bf16[32,48,128]{2,1,0:T(8,128)(2,1)} custom-call(s32[1]{0:T(128)} %bitcast.half_ref, bf16[32,52,128]{2,1,0:T(8,128)(2,1)S(1)} %all-to-all-done.got_ref), custom_call_target="tpu_custom_call" | custom-call | tf_op jit(solution)/shard_map/hold/pallas_call | solution.py:240
  32.8 5.4 %all-to-all-start.1 = ((bf16[32,48,128]{2,1,0:T(8,128)(2,1)}), bf16[32,48,128]{2,1,0:T(8,128)(2,1)S(1)}, u32[]{:S(2)}, u32[]{:S(2)}) async-start(bf16[32,48,128]{2,1,0:T(8,128)(2,1)} %hold.1), calls=%async_computation.1 | async-start | bytes 786432 | tf_op jit(solution)/shard_map/all_to_all | solution.py:610
  38.3 2.7 %fixed_part.1 = (f32[1344,128]{1,0:T(8,128)S(1)}, f32[1344,128]{1,0:T(8,128)S(1)}, f32[1344,128]{1,0:T(8,128)S(1)}) custom-call(bf16[1536,128]{1,0:T(8,128)(2,1)S(1)} %bitcast.26, bf16[8,128]{1,0:T(8,128)(2,1)S(1)} %pad_maximum_fusion.8.mask_ref), custom_call_target="tpu_custom_call" | custom-call | flops 5000000000 | bytes 4000000 | tf_op jit(solution)/shard_map/fixed_part/pallas_call | solution.py:351
  41.0 10.9 %all-to-all-done.1 = bf16[32,48,128]{2,1,0:T(8,128)(2,1)S(1)} async-done(((bf16[32,48,128]{2,1,0:T(8,128)(2,1)}), bf16[32,48,128]{2,1,0:T(8,128)(2,1)S(1)}, u32[]{:S(2)}, u32[]{:S(2)}) %all-to-all-start.1) | async-done | bytes 393248 | tf_op jit(solution)/shard_map/all_to_all | solution.py:610
  52.0 0.1 concatenate.58.head_ref
  52.1 1.3 %collective-permute-start.3 = (bf16[488,128]{1,0:T(8,128)(2,1)S(1)}, bf16[488,128]{1,0:T(8,128)(2,1)S(1)}, u32[]{:S(2)}, u32[]{:S(2)}) collective-permute-start(bf16[488,128]{1,0:T(8,128)(2,1)S(1)} %concatenate.58.head_ref), channel_id=1, source_target_pairs={{32,0},{64,32},{96,64},{128,96},{160,128},{192,160},{224,192},{256... | collective-permute-start | bytes 374792 | tf_op jit(solution)/shard_map/ppermute | solution.py:623
  53.4 5.5 %collective-permute-start.2 = (bf16[488,128]{1,0:T(8,128)(2,1)S(1)}, bf16[488,128]{1,0:T(8,128)(2,1)S(1)}, u32[]{:S(2)}, u32[]{:S(2)}) collective-permute-start(bf16[488,128]{1,0:T(8,128)(2,1)S(1)} %concatenate.52.tail_ref), channel_id=1, source_target_pairs={{0,32},{32,64},{64,96},{96,128},{128,160},{160,192},{192,224},{224... | collective-permute-start | bytes 374792 | tf_op jit(solution)/shard_map/ppermute | solution.py:622
  58.9 8.3 %inner.1 = (f32[3072,128]{1,0:T(8,128)S(1)}, f32[3,576,128]{2,1,0:T(8,128)S(1)}, f32[32,128]{1,0:T(8,128)S(1)}) custom-call(bf16[1536,128]{1,0:T(8,128)(2,1)S(1)} %bitcast.25, bf16[1536,128]{1,0:T(8,128)(2,1)S(1)} %bitcast.27, f32[1344,128]{1,0:T(8,128)S(1)} %get-tuple-element.13.mean_ref, f32[1344,128]{1,0:T(8,128)S(1)} %get-tuple-element.14.away_ref, ...), custom_call_target="tpu_custom_call" | custom-call | flops 10000000000 | bytes 8000000 | tf_op jit(solution)/shard_map/inner/pallas_call | solution.py:505
  67.3 3.3 %rim.1 = (f32[3072,128]{1,0:T(8,128)S(1)}, f32[32,1,128]{2,1,0:T(1,128)S(1)}) custom-call(bf16[488,128]{1,0:T(8,128)(2,1)S(1)} %collective-permute-done.2.below_ref, bf16[488,128]{1,0:T(8,128)(2,1)S(1)} %collective-permute-done.3.above_ref, bf16[488,128]{1,0:T(8,128)(2,1)S(1)} %concatenate.58.head_ref, bf16[488,128]{1,0:T(8,128)(2,1)S(1)} %concatenate.52.tail_ref, ...), custom_call_target="tpu_custom_call" | custom-call | tf_op jit(solution)/shard_map/rim/pallas_call | solution.py:529
  70.6 12.9 %all_to_all.20.in_ref = f32[32,1,128]{2,1,0:T(1,128)S(1)} all-to-all(f32[32,1,128]{2,1,0:T(1,128)S(1)} %get-tuple-element.18), channel_id=1, replica_groups=mesh['slab'=16,'blk'=32] {'blk'}, dimensions={0} | all-to-all | bytes 32768 | tf_op jit(solution)/shard_map/all_to_all | solution.py:626
  83.5 21.1 %all_to_all.21.peaks_ref = f32[16,1,128]{2,1,0:T(1,128)S(1)} all-to-all(f32[16,1,128]{2,1,0:T(1,128)S(1)} %relay.1), channel_id=1, replica_groups=mesh['slab'=16,'blk'=32] {'slab'}, dimensions={0} | all-to-all | bytes 16384 | tf_op jit(solution)/shard_map/all_to_all | solution.py:628
  104.5 1.7 %finish.1 = f32[3,32,32,128]{3,2,1,0:T(8,128)} custom-call(f32[16,1,128]{2,1,0:T(1,128)S(1)} %all_to_all.21.peaks_ref, f32[3072,128]{1,0:T(8,128)S(1)} %get-tuple-element.19.core_ref, f32[3072,128]{1,0:T(8,128)S(1)} %get-tuple-element.20.rim_ref), custom_call_target="tpu_custom_call" | custom-call | tf_op jit(solution)/shard_map/finish/pallas_call | solution.py:581
  (29 shorter events, 0.3 us)
Async XLA Ops:
  0.0 13.8 %copy-start.1 = (s32[1,1,4]{2,1,0:T(1,128)S(1)}, s32[1,1,4]{2,1,0:T(1,128)}, u32[]{:S(2)}) copy-start(s32[1,1,4]{2,1,0:T(1,128)} %param.13) | copy-start | bytes 52
  0.0 14.0 %copy-start = (bf16[32,32,128]{2,1,0:T(8,128)(2,1)S(1)}, bf16[32,32,128]{2,1,0:T(8,128)(2,1)}, u32[]{:S(2)}) copy-start(bf16[32,32,128]{2,1,0:T(8,128)(2,1)} %param.7) | copy-start | bytes 786436
  3.4 25.6 %all-to-all-start = ((bf16[32,52,128]{2,1,0:T(8,128)(2,1)}), bf16[32,52,128]{2,1,0:T(8,128)(2,1)S(1)}, u32[]{:S(2)}, u32[]{:S(2)}) async-start(bf16[32,52,128]{2,1,0:T(8,128)(2,1)} %pack.1), calls=%async_computation | async-start | bytes 917504 | tf_op jit(solution)/shard_map/all_to_all | solution.py:595
  14.0 5.6 %collective-permute-start.1 = (bf16[161,128]{1,0:T(8,128)(2,1)S(1)}, bf16[161,128]{1,0:T(8,128)(2,1)S(1)}, u32[]{:S(2)}, u32[]{:S(2)}) collective-permute-start(bf16[161,128]{1,0:T(8,128)(2,1)S(1)} %get-tuple-element.36), channel_id=1, source_target_pairs={{0,1},{1,2},{2,3},{3,4},{4,5},{5,6},{6,7},{7,8},{8,9},{9,10},{10,1... | collective-permute-start | bytes 123656 | tf_op jit(solution)/shard_map/ppermute | solution.py:600
  17.6 6.1 %collective-permute-start = (bf16[161,128]{1,0:T(8,128)(2,1)S(1)}, bf16[161,128]{1,0:T(8,128)(2,1)S(1)}, u32[]{:S(2)}, u32[]{:S(2)}) collective-permute-start(bf16[161,128]{1,0:T(8,128)(2,1)S(1)} %get-tuple-element.35), channel_id=1, source_target_pairs={{1,0},{2,1},{3,2},{4,3},{5,4},{6,5},{7,6},{8,7},{9,8},{10,9},{11,1... | collective-permute-start | bytes 123656 | tf_op jit(solution)/shard_map/ppermute | solution.py:601
  32.8 19.1 %all-to-all-start.1 = ((bf16[32,48,128]{2,1,0:T(8,128)(2,1)}), bf16[32,48,128]{2,1,0:T(8,128)(2,1)S(1)}, u32[]{:S(2)}, u32[]{:S(2)}) async-start(bf16[32,48,128]{2,1,0:T(8,128)(2,1)} %hold.1), calls=%async_computation.1 | async-start | bytes 786432 | tf_op jit(solution)/shard_map/all_to_all | solution.py:610
  52.1 15.2 %collective-permute-start.3 = (bf16[488,128]{1,0:T(8,128)(2,1)S(1)}, bf16[488,128]{1,0:T(8,128)(2,1)S(1)}, u32[]{:S(2)}, u32[]{:S(2)}) collective-permute-start(bf16[488,128]{1,0:T(8,128)(2,1)S(1)} %concatenate.58.head_ref), channel_id=1, source_target_pairs={{32,0},{64,32},{96,64},{128,96},{160,128},{192,160},{224,192},{256... | collective-permute-start | bytes 374792 | tf_op jit(solution)/shard_map/ppermute | solution.py:623
  53.4 13.8 %collective-permute-start.2 = (bf16[488,128]{1,0:T(8,128)(2,1)S(1)}, bf16[488,128]{1,0:T(8,128)(2,1)S(1)}, u32[]{:S(2)}, u32[]{:S(2)}) collective-permute-start(bf16[488,128]{1,0:T(8,128)(2,1)S(1)} %concatenate.52.tail_ref), channel_id=1, source_target_pairs={{0,32},{32,64},{64,96},{96,128},{128,160},{160,192},{192,224},{224... | collective-permute-start | bytes 374792 | tf_op jit(solution)/shard_map/ppermute | solution.py:622

commit v4 on v3

--- a/solution.py
+++ b/solution.py
@@ -82,7 +82,7 @@
             row = jnp.where(lane == g * SLOTS + k, jnp.where(k < count, name, -1), row)
             for axis in range(3):
                 at = e + (g * 3 + axis) * SLOTS + k
-                row = jnp.where(lane == at, level_ref[0, 0, g, axis, k], row)
+                row = jnp.where(lane == at, level_ref[0, 0, axis, g, k], row)
     row = row.astype(jnp.float32)
     for x in range(SIDE):
         wide[pl.ds(x * SIDE, SIDE), :] = moving_ref[x].astype(jnp.float32)
@@ -135,6 +135,10 @@
     return out
 
 
+def column(a, i):
+    return jnp.broadcast_to(a[:, i : i + 1], a.shape)
+
+
 def hold_kernel(half_ref, got_ref, out_ref, wide, source, coef, mixed, spread):
     strip = HALF // BLOCKS
     rows = OWNERS * BLOCKS
@@ -152,16 +156,19 @@
         total = {}
         for k in range(SLOTS):
             at = g * SLOTS + k
-            name = lists[:, at : at + 1]
+            name = column(lists, at)
             base = e + g * 3 * SLOTS + k
-            lx, lz, ly = (lists[:, base + a * SLOTS : base + a * SLOTS + 1] for a in range(3))
-            hit = jnp.where(where_k == name, 1.0, 0.0)
+            lx, lz, ly = (column(lists, base + a * SLOTS) for a in range(3))
+            x1 = jnp.where(where_k == name, lx, 0.0)
+            x0 = jnp.where(where_k == name, top - lx, 0.0)
             for dx in range(2):
-                ax = hit * (lx if dx else top - lx)
+                ax = x1 if dx else x0
+                z1 = ax * lz
                 for dz in range(2):
-                    az = ax * (lz if dz else top - lz)
+                    az = z1 if dz else top * ax - z1
+                    y1 = az * ly
                     for dy in range(2):
-                        ay = az * (ly if dy else top - ly)
+                        ay = y1 if dy else top * az - y1
                         key = (dx, dz, dy)
                         total[key] = ay if k == 0 else total[key] + ay
         for (dx, dz, dy), c in total.items():
@@ -169,8 +176,7 @@
             col = pl.ds(dy * WIDTH, WIDTH)
             coef[dz * 2 + dx, pl.ds(g * OWNERS, OWNERS), col] = hi.astype(jnp.bfloat16)
             coef[dz * 2 + dx, pl.ds(rows + g * OWNERS, OWNERS), col] = (c - hi).astype(jnp.bfloat16)
-        count = lists[:, 4 * e + g : 4 * e + g + 1]
-        scales.append((1.0 / count) * (1.0 / LEVELS**3))
+        scales.append((1.0 / column(lists, 4 * e + g)) * (1.0 / LEVELS**3))
 
     wrap = strip + 1
     for z in range(TAKEN):
@@ -200,7 +206,10 @@
             for g in range(BLOCKS):
                 lo = rows + g * OWNERS
                 part = acc[g * OWNERS : (g + 1) * OWNERS] + acc[lo : lo + OWNERS]
-                mixed[pl.ds(g * OWNERS, OWNERS), pl.ds((z * strip + t) * WIDTH, piece)] = part * scales[g]
+                for i in range(2):
+                    mixed[pl.ds(g * OWNERS, OWNERS), pl.ds((z * strip + t + i) * WIDTH, WIDTH)] = (
+                        part[:, i * WIDTH : (i + 1) * WIDTH] * scales[g]
+                    )
 
     for r in range(OWNERS):
         for z in range(DEEP):
@@ -272,7 +281,7 @@
     for t in range(SMOOTH_RADIUS + 1):
         left = jnp.where(d == t, taps[SMOOTH_RADIUS + t], left)
     parts = []
-    for _ in range(3):
+    for _ in range(2):
         part = left.astype(jnp.bfloat16)
         parts.append(part)
         left = left - part.astype(jnp.float32)
@@ -298,11 +307,17 @@
     return pltpu.roll(a, (-step) % ROW, 0)
 
 
-def box_zx(ref, which, i):
-    r = [ref[which, rows_at(i + t), :] for t in range(2 * BOX_RADIUS + 1)]
-    a = ((r[0] + r[1]) + (r[2] + r[3])) + r[4]
+def box_x(a):
     two = a + along(a, -1)
     return ((along(two, -1) + a) + along(two, 2)) * (1.0 / (2 * BOX_RADIUS + 1) ** 3)
+
+
+def box_zx(ref, which, i, count):
+    r = [ref[which, rows_at(i + t), :] for t in range(2 * BOX_RADIUS + count)]
+    if count == 1:
+        return [box_x(((r[0] + r[1]) + (r[2] + r[3])) + r[4])]
+    mid = (r[1] + r[2]) + (r[3] + r[4])
+    return [box_x(r[0] + mid), box_x(mid + r[5])]
 
 
 def mask_rows(ref):
@@ -318,32 +333,37 @@
     sums[q + 1, rows, :] = times(halves(wide * wide), bands[1])
 
 
-def fixed_row(sums, q, i, here, mask, mean_ref, away_ref, gain_ref, k):
-    mean = box_zx(sums, q, i)
-    var = box_zx(sums, q + 1, i) - mean * mean + var_eps
-    mean_ref[rows_at(k), :] = mean
-    away_ref[rows_at(k), :] = here - mean
-    gain_ref[rows_at(k), :] = mask / var
+def fixed_rows(sums, q, i, here, mask):
+    means = box_zx(sums, q, i, len(here))
+    squares = box_zx(sums, q + 1, i, len(here))
+    out = []
+    for h, m, p, sq in zip(here, mask, means, squares):
+        out.append((p, h - p, m / (sq - p * p + var_eps)))
+    return out
 
 
 def fixed_kernel(fixed_ref, mask_ref, mean_ref, away_ref, gain_ref, sums):
     bands = box_band()
-    chunk = 4 * ROW
+    chunk = 8 * ROW
 
     def by_y(i, carry):
         rows = pl.ds(pl.multiple_of(i * chunk, chunk), chunk)
         fixed_sums(fixed_ref[rows, :], sums, 0, rows, bands)
         return carry
 
-    lax.fori_loop(0, SIDE // 4, by_y, 0)
+    lax.fori_loop(0, SIDE // 8, by_y, 0)
     mask = mask_rows(mask_ref)
 
-    def by_z(i, carry):
-        here = fixed_ref[rows_at(i + BOX_RADIUS), :].astype(jnp.float32)
-        fixed_row(sums, 0, i, here, mask, mean_ref, away_ref, gain_ref, i)
+    def by_z(step, carry):
+        i = 2 * step
+        here = [fixed_ref[rows_at(i + BOX_RADIUS + t), :].astype(jnp.float32) for t in range(2)]
+        for t, (mean, away, gain) in enumerate(fixed_rows(sums, 0, i, here, [mask, mask])):
+            mean_ref[rows_at(i + t), :] = mean
+            away_ref[rows_at(i + t), :] = away
+            gain_ref[rows_at(i + t), :] = gain
         return carry
 
-    lax.fori_loop(0, INNER, by_z, 0)
+    lax.fori_loop(0, INNER // 2, by_z, 0)
 
 
 def fixed_part(fixed, mask):
@@ -368,48 +388,54 @@
     sums[2, rows, :] = times(halves(mw * f.astype(jnp.float32)), bands[1])
 
 
-def force_row(wide, sums, i, mean_ref, away_ref, gain_ref, j, force, k):
-    mean = box_zx(sums, 0, i)
-    var = box_zx(sums, 1, i) - mean * mean + var_eps
-    cov = box_zx(sums, 2, i) - mean_ref[rows_at(j), :] * mean
-    q = cov / var
-    m = wide[rows_at(i + BOX_RADIUS), :]
-    term = gain_ref[rows_at(j), :] * q * (away_ref[rows_at(j), :] - q * (m - mean))
+def force_rows(wide, sums, i, fixed, force, k, pitch):
+    count = len(fixed)
+    means = box_zx(sums, 0, i, count)
+    squares = box_zx(sums, 1, i, count)
+    products = box_zx(sums, 2, i, count)
     lane = lax.broadcasted_iota(jnp.int32, (ROW, WIDTH), 1)
-    up = jnp.where(lane == WIDTH - 1, 0.0, pltpu.roll(m, WIDTH - 1, 1))
-    down = jnp.where(lane == 0, 0.0, pltpu.roll(m, 1, 1))
-    force[0, rows_at(k), :] = (term * (along(m, 1) - along(m, -1))).astype(jnp.bfloat16)
-    z_step = wide[rows_at(i + BOX_RADIUS + 1), :] - wide[rows_at(i + BOX_RADIUS - 1), :]
-    force[1, rows_at(k), :] = (term * z_step).astype(jnp.bfloat16)
-    force[2, rows_at(k), :] = (term * (up - down)).astype(jnp.bfloat16)
-
-
-def smooth_row(smooth_y, i, out_ref, z, peak):
+    at = [wide[rows_at(i + BOX_RADIUS - 1 + t), :] for t in range(count + 2)]
+    for t, (mean_f, away, gain) in enumerate(fixed):
+        mean = means[t]
+        q = (products[t] - mean_f * mean) / (squares[t] - mean * mean + var_eps)
+        m = at[t + 1]
+        term = gain * q * (away - q * (m - mean))
+        up = jnp.where(lane == WIDTH - 1, 0.0, pltpu.roll(m, WIDTH - 1, 1))
+        down = jnp.where(lane == 0, 0.0, pltpu.roll(m, 1, 1))
+        steps = (along(m, 1) - along(m, -1), at[t + 2] - at[t], up - down)
+        for c in range(3):
+            force[rows_at(c * pitch + k + t), :] = (term * steps[c]).astype(jnp.bfloat16)
+
+
+def smooth_rows(smooth_y, pitch, i, out_ref, z, count, peak):
     taps = smooth_weights(SMOOTH_RADIUS)[SMOOTH_RADIUS:]
-    total = None
+    mid = SMOOTH_RADIUS
+    total = [None] * count
     for c in range(3):
-        g = [smooth_y[c, rows_at(i + t), :] for t in range(2 * SMOOTH_RADIUS + 1)]
-        mid = SMOOTH_RADIUS
-        s = taps[0] * g[mid]
-        for t in range(1, SMOOTH_RADIUS + 1):
-            s += taps[t] * (g[mid - t] + g[mid + t])
-        a = taps[0] * s
-        for t in range(1, SMOOTH_RADIUS + 1):
-            a += taps[t] * (along(s, -t) + along(s, t))
-        a = a[:SIDE]
-        out_ref[pl.ds(c * SIDE * SIDE + z, SIDE, stride=SIDE), :] = a
-        total = a * a if total is None else total + a * a
-    return jnp.maximum(peak, total)
+        g = [smooth_y[rows_at(c * pitch + i + t), :] for t in range(2 * SMOOTH_RADIUS + count)]
+        for n in range(count):
+            s = taps[0] * g[n + mid]
+            for t in range(1, SMOOTH_RADIUS + 1):
+                s += taps[t] * (g[n + mid - t] + g[n + mid + t])
+            a = taps[0] * s
+            for t in range(1, SMOOTH_RADIUS + 1):
+                a += taps[t] * (along(s, -t) + along(s, t))
+            a = a[:SIDE]
+            out_ref[pl.ds(c * SIDE * SIDE + z + n, SIDE, stride=SIDE), :] = a
+            total[n] = a * a if c == 0 else total[n] + a * a
+    for one in total:
+        peak = jnp.maximum(peak, one)
+    return peak
 
 
 def inner_kernel(warped_ref, fixed_ref, mean_ref, away_ref, gain_ref, out_ref, edge_ref, peak_ref, wide, sums, force, smooth_y):
     bands = box_band()
-    triple = smooth_band()
-    chunk = 4 * ROW
+    double = smooth_band()
+    chunk = 8 * ROW
 
     def by_y(i, carry):
-        for step in range(2):
-            pair = 2 * i + step
+        for step in range(4):
+            pair = 4 * i + step
             for half in range(2):
                 for z in range(DEEP):
                     src = (pair * 2 + half) * OUT_PITCH + z * PART
@@ -422,37 +448,43 @@
         sums_by_y(fixed_ref[rows, :], wide, sums, rows, bands)
         return carry
 
-    lax.fori_loop(0, SIDE // 4, by_y, 0)
-
-    def by_z(i, carry):
-        force_row(wide, sums, i, mean_ref, away_ref, gain_ref, i, force, i)
+    lax.fori_loop(0, SIDE // 8, by_y, 0)
+
+    def by_z(step, carry):
+        i = 2 * step
+        fixed = [(mean_ref[rows_at(i + t), :], away_ref[rows_at(i + t), :], gain_ref[rows_at(i + t), :]) for t in range(2)]
+        force_rows(wide, sums, i, fixed, force, i, INNER)
         return carry
 
-    lax.fori_loop(0, INNER, by_z, 0)
+    lax.fori_loop(0, INNER // 2, by_z, 0)
+    batch = 12 * ROW
 
     def smooth(i, carry):
-        rows = pl.ds(pl.multiple_of(i * chunk, chunk), chunk)
-        for c in range(3):
-            f = force[c, rows, :]
-            smooth_y[c, rows, :] = times(jnp.concatenate([f, f, f], axis=1), triple)
+        rows = pl.ds(pl.multiple_of(i * batch, batch), batch)
+        f = force[rows, :]
+        smooth_y[rows, :] = times(jnp.concatenate([f, f], axis=1), double)
         return carry
 
-    lax.fori_loop(0, INNER // 4, smooth, 0)
+    lax.fori_loop(0, 3 * INNER // 12, smooth, 0)
     kept = 2 * SMOOTH_RADIUS * ROW
     for c in range(3):
-        edge_ref[c, 0:kept, :] = smooth_y[c, 0:kept, :]
-        edge_ref[c, kept : 2 * kept, :] = smooth_y[c, INNER * ROW - kept : INNER * ROW, :]
+        at = c * INNER * ROW
+        edge_ref[c, 0:kept, :] = smooth_y[at : at + kept, :]
+        edge_ref[c, kept : 2 * kept, :] = smooth_y[at + INNER * ROW - kept : at + INNER * ROW, :]
     peak_ref[...] = lax.fori_loop(
-        0, CORE, lambda i, peak: smooth_row(smooth_y, i, out_ref, i + RIM, peak), jnp.zeros((SIDE, WIDTH), jnp.float32)
+        0,
+        CORE // 2,
+        lambda i, peak: smooth_rows(smooth_y, INNER, 2 * i, out_ref, 2 * i + RIM, 2, peak),
+        jnp.zeros((SIDE, WIDTH), jnp.float32),
     )
 
 
 def rim_kernel(
     below_ref, above_ref, head_ref, tail_ref, mask_ref, edge_ref, first_ref,
-    out_ref, peak_ref, wide, fwide, sums, fmean, faway, fgain, force, smooth_y,
+    out_ref, peak_ref, wide, fwide, sums, force, smooth_y,
 ):
     bands = box_band()
-    triple = smooth_band()
+    double = smooth_band()
     own = RIM - 1
     stack = RIM + own
     for ref, start, count, at in (
@@ -462,41 +494,51 @@
         (above_ref, 0, RIM, stack + own),
     ):
         rows = pl.ds(at * ROW, count * ROW)
-        f = ref[pl.ds((RIM + start) * ROW, count * ROW), :]
         wide[rows, :] = ref[pl.ds(start * ROW, count * ROW), :].astype(jnp.float32)
-        fwide[rows, :] = f.astype(jnp.float32)
+        fwide[rows, :] = ref[pl.ds((RIM + start) * ROW, count * ROW), :].astype(jnp.float32)
+    chunk = stack * ROW
+
+    def by_y(i, carry):
+        rows = pl.ds(pl.multiple_of(i * chunk, ROW), chunk)
+        f = fwide[rows, :].astype(jnp.bfloat16)
         sums_by_y(f, wide, sums, rows, bands)
         fixed_sums(f, sums, 3, rows, bands)
-    here = mask_rows(mask_ref)
+        return carry
+
+    lax.fori_loop(0, 2, by_y, 0)
     last = pl.ds(2 * RIM * ROW, 8)
-    masks = [mask_rows(below_ref.at[last, :]), here, mask_rows(above_ref.at[last, :])]
+    masks = [mask_rows(below_ref.at[last, :]), mask_rows(mask_ref), mask_rows(above_ref.at[last, :])]
 
     def by_z(i, carry):
-        side = jnp.where(i < RIM, 0, 1)
-        first = stack * side + i - RIM * side
-        outer = jnp.where(side == 0, masks[0], masks[2])
-        mask = jnp.where((i >= SMOOTH_RADIUS) & (i < 2 * RIM - SMOOTH_RADIUS), masks[1], outer)
-        fixed_row(sums, 3, first, fwide[rows_at(first + BOX_RADIUS), :], mask, fmean, faway, fgain, i)
-        force_row(wide, sums, first, fmean, faway, fgain, i, force, i)
+        for side in range(2):
+            first = stack * side + i
+            if side == 0:
+                mask = jnp.where(i < SMOOTH_RADIUS, masks[0], masks[1])
+            else:
+                mask = jnp.where(i >= RIM - SMOOTH_RADIUS, masks[2], masks[1])
+            fixed = fixed_rows(sums, 3, first, [fwide[rows_at(first + BOX_RADIUS), :]], [mask])
+            force_rows(wide, sums, first, fixed, force, i + RIM * side, 2 * RIM)
         return carry
 
-    lax.fori_loop(0, 2 * RIM, by_z, 0)
+    lax.fori_loop(0, RIM, by_z, 0)
     kept = 2 * SMOOTH_RADIUS
     tall = RIM + kept
     for c in range(3):
+        f = force[pl.ds(c * 2 * RIM * ROW, 2 * RIM * ROW), :]
+        g = times(jnp.concatenate([f, f], axis=1), double)
         for side in range(2):
-            f = force[c, pl.ds(side * RIM * ROW, RIM * ROW), :]
-            new = (side * tall + (kept if side else 0)) * ROW
-            smooth_y[c, pl.ds(new, RIM * ROW), :] = times(jnp.concatenate([f, f, f], axis=1), triple)
-            old = (side * tall + (0 if side else RIM)) * ROW
-            smooth_y[c, pl.ds(old, kept * ROW), :] = edge_ref[c, pl.ds(side * kept * ROW, kept * ROW), :]
+            base = c * 2 * tall + side * tall
+            new = base + (kept if side else 0)
+            smooth_y[pl.ds(new * ROW, RIM * ROW), :] = g[side * RIM * ROW : (side + 1) * RIM * ROW]
+            old = base + (0 if side else RIM)
+            smooth_y[pl.ds(old * ROW, kept * ROW), :] = edge_ref[c, pl.ds(side * kept * ROW, kept * ROW), :]
 
     def smooth(i, peak):
-        side = jnp.where(i < RIM, 0, 1)
-        j = i - RIM * side
-        return smooth_row(smooth_y, tall * side + j, out_ref, (SIDE - RIM) * side + j, peak)
-
-    peak = lax.fori_loop(0, 2 * RIM, smooth, first_ref[...])
+        for side in range(2):
+            peak = smooth_rows(smooth_y, 2 * tall, tall * side + i, out_ref, (SIDE - RIM) * side + i, 1, peak)
+        return peak
+
+    peak = lax.fori_loop(0, RIM, smooth, first_ref[...])
     top = jnp.max(jnp.max(peak, axis=0, keepdims=True), axis=1, keepdims=True)
     peak_ref[...] = jnp.broadcast_to(top.reshape(1, 1, 1), peak_ref.shape)
 
@@ -514,8 +556,8 @@
         scratch_shapes=[
             pltpu.VMEM((SIDE * ROW, WIDTH), jnp.float32),
             pltpu.VMEM((3, SIDE * ROW, WIDTH), jnp.float32),
-            pltpu.VMEM((3, INNER * ROW, WIDTH), jnp.bfloat16),
-            pltpu.VMEM((3, INNER * ROW, WIDTH), jnp.float32),
+            pltpu.VMEM((3 * INNER * ROW, WIDTH), jnp.bfloat16),
+            pltpu.VMEM((3 * INNER * ROW, WIDTH), jnp.float32),
         ],
         compiler_params=params(14),
         cost_estimate=cost(10_000_000_000, 8_000_000),
@@ -536,10 +578,9 @@
         out_specs=[in_vmem()] * 2,
         scratch_shapes=[pltpu.VMEM((stack, WIDTH), jnp.float32)] * 2
         + [pltpu.VMEM((5, stack, WIDTH), jnp.float32)]
-        + [pltpu.VMEM((2 * RIM * ROW, WIDTH), jnp.float32)] * 3
         + [
-            pltpu.VMEM((3, 2 * RIM * ROW, WIDTH), jnp.bfloat16),
-            pltpu.VMEM((3, tall, WIDTH), jnp.float32),
+            pltpu.VMEM((3 * 2 * RIM * ROW, WIDTH), jnp.bfloat16),
+            pltpu.VMEM((3 * tall, WIDTH), jnp.float32),
         ],
         compiler_params=params(14),
         name="rim",
@@ -591,7 +632,7 @@
 
 def per_device(fixed_image, moving_image, fetch_owner, fetch_block, fetch_count, interp_level, block_mask):
     side, width = SIDE, WIDTH
-    sent = pack(fetch_owner, fetch_block, fetch_count, interp_level, moving_image)
+    sent = pack(fetch_owner, fetch_block, fetch_count, interp_level.transpose(0, 1, 3, 2, 4), moving_image)
     got = lax.all_to_all(sent, "blk", split_axis=0, concat_axis=0, tiled=True)
 
     mask_row = jnp.repeat(block_mask.reshape(BLOCKS), side).astype(jnp.bfloat16)[None]

time: 107 us -> 103 us (0.963)
  Pallas kernels: 21.9 us -> 19.1 us
  local copies, waits for them, and re-layouts: 1.99 us -> 0.66 us
    ppermute x1, waiting for transfers between devices: 4.07 us -> 0.11 us  [per_device(): right = lax.ppermute(first, 'blk', shift_down('blk'))]
    all_to_all x1, waiting for transfers between devices: 5.07 us -> 8.05 us  [per_device(): got = lax.all_to_all(sent, 'blk', split_axis=0, concat_axis=0, tiled=True)]
    pallas_call x1, Pallas kernels: 8.31 us -> 6.63 us  [inner(): pl.pallas_call(inner_kernel, out_shape=[jax.ShapeDtypeStruct((3 * SIDE *...]
    unnamed x5 -> x4, local copies, waits for them, and re-layouts: 1.34 us -> 0.01 us
  transfers between devices with their start and end apart: 6 -> 6, of which waited for: 3 -> 4; matrix products, arithmetic and copies ran while one was open for 1% -> 1% of each run, Pallas kernels for 10% -> 8%
where the time goes in v4:
time: 103 us
  blocking collectives  33.9 us (33%)
  starting transfers between devices  28 us (27%)
  waiting for transfers between devices  20.8 us (20%)
  Pallas kernels  19.1 us (19%)
    all_to_all x1, blocking collectives, per_device(): peak = lax.all_to_all(peak, 'slab', split_axis=0, concat_axis=0, tiled=True)  21.1 us
    all_to_all x1, blocking collectives, per_device(): peak = lax.all_to_all(peak, 'blk', split_axis=0, concat_axis=0, tiled=True)  12.8 us
    all_to_all x1, waiting for transfers between devices, per_device(): lax.all_to_all(hold(half, got), 'blk', split_axis=0, concat_axis=0, tiled...  11.8 us
    all_to_all x1, starting transfers between devices, per_device(): got = lax.all_to_all(sent, 'blk', split_axis=0, concat_axis=0, tiled=True)  10.4 us
    all_to_all x1, waiting for transfers between devices, per_device(): got = lax.all_to_all(sent, 'blk', split_axis=0, concat_axis=0, tiled=True)  8.05 us
    pallas_call x1, Pallas kernels, inner(): pl.pallas_call(inner_kernel, out_shape=[jax.ShapeDtypeStruct((3 * SIDE *...  6.63 us
    ppermute x1, starting transfers between devices, per_device(): below = lax.ppermute(tail, 'slab', shift_up('slab'))  5.49 us
    all_to_all x1, starting transfers between devices, per_device(): lax.all_to_all(hold(half, got), 'blk', split_axis=0, concat_axis=0, tiled...  5.33 us
  transfers between devices with their start and end apart: 6, of which 4 were waited for; matrix products, arithmetic and copies ran while one was open for 1% of the time, Pallas kernels for 8%

profile of v4, /device:TPU:1, one launch (start us, length us, event | category | flops | bytes accessed | tf_op | source)
XLA Modules:
  0.0 102.9 jit_solution(9321606133903945932)
XLA Ops:
  0.0 2.1 %pack.1 = bf16[32,52,128]{2,1,0:T(8,128)(2,1)} custom-call(s32[1,1,4,4]{3,2,1,0:T(4,128)} %owner_ref.1, s32[1,1,4,4]{3,2,1,0:T(4,128)} %block_ref.1, s32[1,1,4]{2,1,0:T(1,128)} %count_ref.1, s32[1,1,3,4,4]{4,3,2,1,0:T(4,128)} %bitcast.49, bf16[32,32,128]{2,1,0:T(8,128)(2,1)} %moving_ref.1), custom_call_target="tpu_custom_call" | custom-call | tf_op jit(solution)/shard_map/pack/pallas_call | solution.py:113
  2.1 10.4 %all-to-all-start = ((bf16[32,52,128]{2,1,0:T(8,128)(2,1)}), bf16[32,52,128]{2,1,0:T(8,128)(2,1)S(1)}, u32[]{:S(2)}, u32[]{:S(2)}) async-start(bf16[32,52,128]{2,1,0:T(8,128)(2,1)} %pack.1), calls=%async_computation | async-start | bytes 917504 | tf_op jit(solution)/shard_map/all_to_all | solution.py:636
  12.5 0.1 broadcast_in_dim.10
  12.6 0.1 convert_element_type.19
  12.7 2.3 %collective-permute-start = (bf16[161,128]{1,0:T(8,128)(2,1)S(1)}, bf16[161,128]{1,0:T(8,128)(2,1)S(1)}, u32[]{:S(2)}, u32[]{:S(2)}) collective-permute-start(bf16[161,128]{1,0:T(8,128)(2,1)S(1)} %get-tuple-element.35), channel_id=1, source_target_pairs={{1,0},{2,1},{3,2},{4,3},{5,4},{6,5},{7,6},{8,7},{9,8},{10,9},{11,1... | collective-permute-start | bytes 123656 | tf_op jit(solution)/shard_map/ppermute | solution.py:642
  15.0 3.3 %collective-permute-start.1 = (bf16[161,128]{1,0:T(8,128)(2,1)S(1)}, bf16[161,128]{1,0:T(8,128)(2,1)S(1)}, u32[]{:S(2)}, u32[]{:S(2)}) collective-permute-start(bf16[161,128]{1,0:T(8,128)(2,1)S(1)} %get-tuple-element.36), channel_id=1, source_target_pairs={{0,1},{1,2},{2,3},{3,4},{4,5},{5,6},{6,7},{7,8},{8,9},{9,10},{10,1... | collective-permute-start | bytes 123656 | tf_op jit(solution)/shard_map/ppermute | solution.py:641
  18.3 0.1 pad.10.clone
  18.4 0.1 collective-permute-done
  18.5 0.9 collective-permute-done.1
  19.4 0.1 maximum_bitcast_fusion
  19.5 0.2 copy.10
  19.7 8.1 %all-to-all-done.got_ref = bf16[32,52,128]{2,1,0:T(8,128)(2,1)S(1)} async-done(((bf16[32,52,128]{2,1,0:T(8,128)(2,1)}), bf16[32,52,128]{2,1,0:T(8,128)(2,1)S(1)}, u32[]{:S(2)}, u32[]{:S(2)}) %all-to-all-start) | async-done | bytes 426016 | tf_op jit(solution)/shard_map/all_to_all | solution.py:636
  27.7 3.4 %hold.1 = bf16[32,48,128]{2,1,0:T(8,128)(2,1)} custom-call(s32[1]{0:T(128)} %bitcast.half_ref, bf16[32,52,128]{2,1,0:T(8,128)(2,1)S(1)} %all-to-all-done.got_ref), custom_call_target="tpu_custom_call" | custom-call | tf_op jit(solution)/shard_map/hold/pallas_call | solution.py:249
  31.2 5.3 %all-to-all-start.1 = ((bf16[32,48,128]{2,1,0:T(8,128)(2,1)}), bf16[32,48,128]{2,1,0:T(8,128)(2,1)S(1)}, u32[]{:S(2)}, u32[]{:S(2)}) async-start(bf16[32,48,128]{2,1,0:T(8,128)(2,1)} %hold.1), calls=%async_computation.1 | async-start | bytes 786432 | tf_op jit(solution)/shard_map/all_to_all | solution.py:651
  36.7 1.8 %fixed_part.1 = (f32[1344,128]{1,0:T(8,128)S(1)}, f32[1344,128]{1,0:T(8,128)S(1)}, f32[1344,128]{1,0:T(8,128)S(1)}) custom-call(bf16[1536,128]{1,0:T(8,128)(2,1)S(1)} %bitcast.27, bf16[8,128]{1,0:T(8,128)(2,1)S(1)} %pad_maximum_fusion.8.mask_ref), custom_call_target="tpu_custom_call" | custom-call | flops 5000000000 | bytes 4000000 | tf_op jit(solution)/shard_map/fixed_part/pallas_call | solution.py:371
  38.5 11.8 %all-to-all-done.1 = bf16[32,48,128]{2,1,0:T(8,128)(2,1)S(1)} async-done(((bf16[32,48,128]{2,1,0:T(8,128)(2,1)}), bf16[32,48,128]{2,1,0:T(8,128)(2,1)S(1)}, u32[]{:S(2)}, u32[]{:S(2)}) %all-to-all-start.1) | async-done | bytes 393248 | tf_op jit(solution)/shard_map/all_to_all | solution.py:651
  50.3 0.1 concatenate.58.head_ref
  50.4 1.3 %collective-permute-start.3 = (bf16[488,128]{1,0:T(8,128)(2,1)S(1)}, bf16[488,128]{1,0:T(8,128)(2,1)S(1)}, u32[]{:S(2)}, u32[]{:S(2)}) collective-permute-start(bf16[488,128]{1,0:T(8,128)(2,1)S(1)} %concatenate.58.head_ref), channel_id=1, source_target_pairs={{32,0},{64,32},{96,64},{128,96},{160,128},{192,160},{224,192},{256... | collective-permute-start | bytes 374792 | tf_op jit(solution)/shard_map/ppermute | solution.py:664
  51.8 5.5 %collective-permute-start.2 = (bf16[488,128]{1,0:T(8,128)(2,1)S(1)}, bf16[488,128]{1,0:T(8,128)(2,1)S(1)}, u32[]{:S(2)}, u32[]{:S(2)}) collective-permute-start(bf16[488,128]{1,0:T(8,128)(2,1)S(1)} %concatenate.52.tail_ref), channel_id=1, source_target_pairs={{0,32},{32,64},{64,96},{96,128},{128,160},{160,192},{192,224},{224... | collective-permute-start | bytes 374792 | tf_op jit(solution)/shard_map/ppermute | solution.py:663
  57.3 6.6 %inner.1 = (f32[3072,128]{1,0:T(8,128)S(1)}, f32[3,576,128]{2,1,0:T(8,128)S(1)}, f32[32,128]{1,0:T(8,128)S(1)}) custom-call(bf16[1536,128]{1,0:T(8,128)(2,1)S(1)} %bitcast.26, bf16[1536,128]{1,0:T(8,128)(2,1)S(1)} %bitcast.28, f32[1344,128]{1,0:T(8,128)S(1)} %get-tuple-element.13.mean_ref, f32[1344,128]{1,0:T(8,128)S(1)} %get-tuple-element.14.away_ref, ...), custom_call_target="tpu_custom_call" | custom-call | flops 10000000000 | bytes 8000000 | tf_op jit(solution)/shard_map/inner/pallas_call | solution.py:547
  63.9 3.3 %rim.1 = (f32[3072,128]{1,0:T(8,128)S(1)}, f32[32,1,128]{2,1,0:T(1,128)S(1)}) custom-call(bf16[488,128]{1,0:T(8,128)(2,1)S(1)} %collective-permute-done.2.below_ref, bf16[488,128]{1,0:T(8,128)(2,1)S(1)} %collective-permute-done.3.above_ref, bf16[488,128]{1,0:T(8,128)(2,1)S(1)} %concatenate.58.head_ref, bf16[488,128]{1,0:T(8,128)(2,1)S(1)} %concatenate.52.tail_ref, ...), custom_call_target="tpu_custom_call" | custom-call | tf_op jit(solution)/shard_map/rim/pallas_call | solution.py:571
  67.3 12.8 %all_to_all.20.in_ref = f32[32,1,128]{2,1,0:T(1,128)S(1)} all-to-all(f32[32,1,128]{2,1,0:T(1,128)S(1)} %get-tuple-element.18), channel_id=1, replica_groups=mesh['slab'=16,'blk'=32] {'blk'}, dimensions={0} | all-to-all | bytes 32768 | tf_op jit(solution)/shard_map/all_to_all | solution.py:667
  80.1 21.1 %all_to_all.21.peaks_ref = f32[16,1,128]{2,1,0:T(1,128)S(1)} all-to-all(f32[16,1,128]{2,1,0:T(1,128)S(1)} %relay.1), channel_id=1, replica_groups=mesh['slab'=16,'blk'=32] {'slab'}, dimensions={0} | all-to-all | bytes 16384 | tf_op jit(solution)/shard_map/all_to_all | solution.py:669
  101.2 1.7 %finish.1 = f32[3,32,32,128]{3,2,1,0:T(8,128)} custom-call(f32[16,1,128]{2,1,0:T(1,128)S(1)} %all_to_all.21.peaks_ref, f32[3072,128]{1,0:T(8,128)S(1)} %get-tuple-element.19.core_ref, f32[3072,128]{1,0:T(8,128)S(1)} %get-tuple-element.20.rim_ref), custom_call_target="tpu_custom_call" | custom-call | tf_op jit(solution)/shard_map/finish/pallas_call | solution.py:622
  (28 shorter events, 0.3 us)
Async XLA Ops:
  0.0 12.5 %copy-start.1 = (s32[1,1,4]{2,1,0:T(1,128)S(1)}, s32[1,1,4]{2,1,0:T(1,128)}, u32[]{:S(2)}) copy-start(s32[1,1,4]{2,1,0:T(1,128)} %param.13) | copy-start | bytes 52
  0.0 12.7 %copy-start = (bf16[32,32,128]{2,1,0:T(8,128)(2,1)S(1)}, bf16[32,32,128]{2,1,0:T(8,128)(2,1)}, u32[]{:S(2)}) copy-start(bf16[32,32,128]{2,1,0:T(8,128)(2,1)} %param.7) | copy-start | bytes 786436
  2.1 25.6 %all-to-all-start = ((bf16[32,52,128]{2,1,0:T(8,128)(2,1)}), bf16[32,52,128]{2,1,0:T(8,128)(2,1)S(1)}, u32[]{:S(2)}, u32[]{:S(2)}) async-start(bf16[32,52,128]{2,1,0:T(8,128)(2,1)} %pack.1), calls=%async_computation | async-start | bytes 917504 | tf_op jit(solution)/shard_map/all_to_all | solution.py:636
  12.7 5.8 %collective-permute-start = (bf16[161,128]{1,0:T(8,128)(2,1)S(1)}, bf16[161,128]{1,0:T(8,128)(2,1)S(1)}, u32[]{:S(2)}, u32[]{:S(2)}) collective-permute-start(bf16[161,128]{1,0:T(8,128)(2,1)S(1)} %get-tuple-element.35), channel_id=1, source_target_pairs={{1,0},{2,1},{3,2},{4,3},{5,4},{6,5},{7,6},{8,7},{9,8},{10,9},{11,1... | collective-permute-start | bytes 123656 | tf_op jit(solution)/shard_map/ppermute | solution.py:642
  15.0 4.4 %collective-permute-start.1 = (bf16[161,128]{1,0:T(8,128)(2,1)S(1)}, bf16[161,128]{1,0:T(8,128)(2,1)S(1)}, u32[]{:S(2)}, u32[]{:S(2)}) collective-permute-start(bf16[161,128]{1,0:T(8,128)(2,1)S(1)} %get-tuple-element.36), channel_id=1, source_target_pairs={{0,1},{1,2},{2,3},{3,4},{4,5},{5,6},{6,7},{7,8},{8,9},{9,10},{10,1... | collective-permute-start | bytes 123656 | tf_op jit(solution)/shard_map/ppermute | solution.py:641
  31.2 19.1 %all-to-all-start.1 = ((bf16[32,48,128]{2,1,0:T(8,128)(2,1)}), bf16[32,48,128]{2,1,0:T(8,128)(2,1)S(1)}, u32[]{:S(2)}, u32[]{:S(2)}) async-start(bf16[32,48,128]{2,1,0:T(8,128)(2,1)} %hold.1), calls=%async_computation.1 | async-start | bytes 786432 | tf_op jit(solution)/shard_map/all_to_all | solution.py:651
  50.4 13.5 %collective-permute-start.3 = (bf16[488,128]{1,0:T(8,128)(2,1)S(1)}, bf16[488,128]{1,0:T(8,128)(2,1)S(1)}, u32[]{:S(2)}, u32[]{:S(2)}) collective-permute-start(bf16[488,128]{1,0:T(8,128)(2,1)S(1)} %concatenate.58.head_ref), channel_id=1, source_target_pairs={{32,0},{64,32},{96,64},{128,96},{160,128},{192,160},{224,192},{256... | collective-permute-start | bytes 374792 | tf_op jit(solution)/shard_map/ppermute | solution.py:664
  51.8 12.1 %collective-permute-start.2 = (bf16[488,128]{1,0:T(8,128)(2,1)S(1)}, bf16[488,128]{1,0:T(8,128)(2,1)S(1)}, u32[]{:S(2)}, u32[]{:S(2)}) collective-permute-start(bf16[488,128]{1,0:T(8,128)(2,1)S(1)} %concatenate.52.tail_ref), channel_id=1, source_target_pairs={{0,32},{32,64},{64,96},{96,128},{128,160},{160,192},{192,224},{224... | collective-permute-start | bytes 374792 | tf_op jit(solution)/shard_map/ppermute | solution.py:663

commit v5 on v4

--- a/solution.py
+++ b/solution.py
@@ -51,6 +51,7 @@
 INNER = SIDE - 2 * BOX_RADIUS
 CORE = INNER - 2 * SMOOTH_RADIUS
 ROW = OUT_PITCH
+THIN = 40
 MIB = 1 << 20
 
 
@@ -121,18 +122,18 @@
 
 
 def exchange_groups(parts, lane):
-    turned = [[p] + [pltpu.roll(p, SIDE * s, 1) for s in range(1, BLOCKS)] for p in parts]
-    out = []
-    for b in range(BLOCKS):
-        pick = [turned[a][(a - b) % BLOCKS] for a in range(BLOCKS)]
-        out.append(
-            jnp.where(
-                lane < 2 * SIDE,
-                jnp.where(lane < SIDE, pick[0], pick[1]),
-                jnp.where(lane < 3 * SIDE, pick[2], pick[3]),
-            )
-        )
-    return out
+    parts = list(parts)
+    low = lane < 2 * SIDE
+    for a in range(2):
+        p, q = parts[a], parts[a + 2]
+        r = pltpu.roll(jnp.where(low, q, p), 2 * SIDE, 1)
+        parts[a], parts[a + 2] = jnp.where(low, p, r), jnp.where(low, r, q)
+    even = (lane // SIDE) % 2 == 0
+    for a in (0, 2):
+        p, q = parts[a], parts[a + 1]
+        parts[a] = jnp.where(even, p, pltpu.roll(q, SIDE, 1))
+        parts[a + 1] = jnp.where(even, pltpu.roll(p, WIDTH - SIDE, 1), q)
+    return parts
 
 
 def column(a, i):
@@ -303,13 +304,24 @@
     return pl.ds(pl.multiple_of(i * ROW, ROW), ROW)
 
 
+def thin_at(i):
+    if isinstance(i, int):
+        return pl.ds(i * THIN, THIN)
+    return pl.ds(pl.multiple_of(i * THIN, 8), THIN)
+
+
 def along(a, step):
-    return pltpu.roll(a, (-step) % ROW, 0)
+    return pltpu.roll(a, (-step) % a.shape[0], 0)
+
+
+def thin(a):
+    x = lax.broadcasted_iota(jnp.int32, (8, WIDTH), 0)
+    return jnp.concatenate([a[:SIDE], jnp.where(x < 4, a[SIDE:THIN], a[THIN:])], axis=0)
 
 
 def box_x(a):
     two = a + along(a, -1)
-    return ((along(two, -1) + a) + along(two, 2)) * (1.0 / (2 * BOX_RADIUS + 1) ** 3)
+    return thin((along(two, -1) + a) + along(two, 2)) * (1.0 / (2 * BOX_RADIUS + 1) ** 3)
 
 
 def box_zx(ref, which, i, count):
@@ -321,10 +333,10 @@
 
 
 def mask_rows(ref):
-    x = lax.broadcasted_iota(jnp.int32, (ROW, WIDTH), 0)
+    x = lax.broadcasted_iota(jnp.int32, (THIN, WIDTH), 0)
     m = ref[...].astype(jnp.float32)
     right = jnp.where(x < SIDE + SMOOTH_RADIUS, m[1:2], 0.0)
-    return jnp.where(x < SIDE, m[0:1], jnp.where(x >= ROW - SMOOTH_RADIUS, m[2:3], right))
+    return jnp.where(x < SIDE, m[0:1], jnp.where(x >= THIN - SMOOTH_RADIUS, m[2:3], right))
 
 
 def fixed_sums(f, sums, q, rows, bands):
@@ -356,18 +368,18 @@
 
     def by_z(step, carry):
         i = 2 * step
-        here = [fixed_ref[rows_at(i + BOX_RADIUS + t), :].astype(jnp.float32) for t in range(2)]
+        here = [thin(fixed_ref[rows_at(i + BOX_RADIUS + t), :].astype(jnp.float32)) for t in range(2)]
         for t, (mean, away, gain) in enumerate(fixed_rows(sums, 0, i, here, [mask, mask])):
-            mean_ref[rows_at(i + t), :] = mean
-            away_ref[rows_at(i + t), :] = away
-            gain_ref[rows_at(i + t), :] = gain
+            mean_ref[thin_at(i + t), :] = mean
+            away_ref[thin_at(i + t), :] = away
+            gain_ref[thin_at(i + t), :] = gain
         return carry
 
     lax.fori_loop(0, INNER // 2, by_z, 0)
 
 
 def fixed_part(fixed, mask):
-    out = jax.ShapeDtypeStruct((INNER * ROW, WIDTH), jnp.float32)
+    out = jax.ShapeDtypeStruct((INNER * THIN, WIDTH), jnp.float32)
     return pl.pallas_call(
         fixed_kernel,
         out_shape=[out] * 3,
@@ -380,12 +392,20 @@
     )(fixed, mask)
 
 
-def sums_by_y(f, wide, sums, rows, bands):
+def sums_by_y(f, wide, sums, rows, bands, with_fixed):
     mw = wide[rows, :]
-    m = mw.astype(jnp.bfloat16)
-    sums[0, rows, :] = times(m, bands[0])
-    sums[1, rows, :] = times(halves(mw * mw), bands[1])
-    sums[2, rows, :] = times(halves(mw * f.astype(jnp.float32)), bands[1])
+    fw = f.astype(jnp.float32)
+    n = mw.shape[0]
+    plain = [mw.astype(jnp.bfloat16)] + ([f] if with_fixed else [])
+    pairs = [mw * mw, mw * fw] + ([fw * fw] if with_fixed else [])
+    one = times(jnp.concatenate(plain, axis=0), bands[0])
+    two = times(jnp.concatenate([halves(p) for p in pairs], axis=0), bands[1])
+    sums[0, rows, :] = one[:n]
+    sums[1, rows, :] = two[:n]
+    sums[2, rows, :] = two[n : 2 * n]
+    if with_fixed:
+        sums[3, rows, :] = one[n:]
+        sums[4, rows, :] = two[2 * n :]
 
 
 def force_rows(wide, sums, i, fixed, force, k, pitch):
@@ -393,8 +413,8 @@
     means = box_zx(sums, 0, i, count)
     squares = box_zx(sums, 1, i, count)
     products = box_zx(sums, 2, i, count)
-    lane = lax.broadcasted_iota(jnp.int32, (ROW, WIDTH), 1)
-    at = [wide[rows_at(i + BOX_RADIUS - 1 + t), :] for t in range(count + 2)]
+    lane = lax.broadcasted_iota(jnp.int32, (THIN, WIDTH), 1)
+    at = [thin(wide[rows_at(i + BOX_RADIUS - 1 + t), :]) for t in range(count + 2)]
     for t, (mean_f, away, gain) in enumerate(fixed):
         mean = means[t]
         q = (products[t] - mean_f * mean) / (squares[t] - mean * mean + var_eps)
@@ -404,7 +424,7 @@
         down = jnp.where(lane == 0, 0.0, pltpu.roll(m, 1, 1))
         steps = (along(m, 1) - along(m, -1), at[t + 2] - at[t], up - down)
         for c in range(3):
-            force[rows_at(c * pitch + k + t), :] = (term * steps[c]).astype(jnp.bfloat16)
+            force[thin_at(c * pitch + k + t), :] = term * steps[c]
 
 
 def smooth_rows(smooth_y, pitch, i, out_ref, z, count, peak):
@@ -412,7 +432,7 @@
     mid = SMOOTH_RADIUS
     total = [None] * count
     for c in range(3):
-        g = [smooth_y[rows_at(c * pitch + i + t), :] for t in range(2 * SMOOTH_RADIUS + count)]
+        g = [smooth_y[thin_at(c * pitch + i + t), :] for t in range(2 * SMOOTH_RADIUS + count)]
         for n in range(count):
             s = taps[0] * g[n + mid]
             for t in range(1, SMOOTH_RADIUS + 1):
@@ -428,55 +448,53 @@
     return peak
 
 
+def smooth_along_y(force, i, pitch, count, out, j, out_pitch, double):
+    f = [force[pl.ds((c * pitch + i) * THIN, count * THIN), :].astype(jnp.bfloat16) for c in range(3)]
+    f = jnp.concatenate(f, axis=0)
+    g = times(jnp.concatenate([f, f], axis=1), double)
+    for c in range(3):
+        out[pl.ds((c * out_pitch + j) * THIN, count * THIN), :] = g[c * count * THIN : (c + 1) * count * THIN]
+
+
 def inner_kernel(warped_ref, fixed_ref, mean_ref, away_ref, gain_ref, out_ref, edge_ref, peak_ref, wide, sums, force, smooth_y):
     bands = box_band()
     double = smooth_band()
-    chunk = 8 * ROW
-
-    def by_y(i, carry):
-        for step in range(4):
-            pair = 4 * i + step
+    step = 4
+
+    def by_y(n):
+        for pair in range(n * step // DEEP, (n + 1) * step // DEEP):
             for half in range(2):
                 for z in range(DEEP):
                     src = (pair * 2 + half) * OUT_PITCH + z * PART
                     dst = (pair * DEEP + z) * ROW
-                    own = warped_ref[pl.ds(pl.multiple_of(src, 8), HALF), :]
-                    wide[pl.ds(pl.multiple_of(dst + half * HALF, 8), HALF), :] = own.astype(jnp.float32)
-                    side = warped_ref[pl.ds(pl.multiple_of(src + HALF, 8), 8), :]
-                    wide[pl.ds(pl.multiple_of(dst + SIDE + 8 * half, 8), 8), :] = side.astype(jnp.float32)
-        rows = pl.ds(pl.multiple_of(i * chunk, chunk), chunk)
-        sums_by_y(fixed_ref[rows, :], wide, sums, rows, bands)
-        return carry
-
-    lax.fori_loop(0, SIDE // 8, by_y, 0)
-
-    def by_z(step, carry):
-        i = 2 * step
-        fixed = [(mean_ref[rows_at(i + t), :], away_ref[rows_at(i + t), :], gain_ref[rows_at(i + t), :]) for t in range(2)]
-        force_rows(wide, sums, i, fixed, force, i, INNER)
-        return carry
-
-    lax.fori_loop(0, INNER // 2, by_z, 0)
-    batch = 12 * ROW
-
-    def smooth(i, carry):
-        rows = pl.ds(pl.multiple_of(i * batch, batch), batch)
-        f = force[rows, :]
-        smooth_y[rows, :] = times(jnp.concatenate([f, f], axis=1), double)
-        return carry
-
-    lax.fori_loop(0, 3 * INNER // 12, smooth, 0)
-    kept = 2 * SMOOTH_RADIUS * ROW
+                    own = warped_ref[pl.ds(src, HALF), :]
+                    wide[pl.ds(dst + half * HALF, HALF), :] = own.astype(jnp.float32)
+                    side = warped_ref[pl.ds(src + HALF, 8), :]
+                    wide[pl.ds(dst + SIDE + 8 * half, 8), :] = side.astype(jnp.float32)
+        rows = pl.ds(n * step * ROW, step * ROW)
+        sums_by_y(fixed_ref[rows, :], wide, sums, rows, bands, False)
+
+    by_y(0)
+    peak = jnp.zeros((SIDE, WIDTH), jnp.float32)
+    done = 0
+    for n in range(INNER // step):
+        by_y(n + 1)
+        for i in range(n * step, (n + 1) * step, 2):
+            fixed = [
+                (mean_ref[thin_at(i + t), :], away_ref[thin_at(i + t), :], gain_ref[thin_at(i + t), :])
+                for t in range(2)
+            ]
+            force_rows(wide, sums, i, fixed, force, i, INNER)
+        smooth_along_y(force, n * step, INNER, step, smooth_y, n * step, INNER, double)
+        while done + 1 + 2 * SMOOTH_RADIUS < (n + 1) * step:
+            peak = smooth_rows(smooth_y, INNER, done, out_ref, done + RIM, 2, peak)
+            done += 2
+    kept = 2 * SMOOTH_RADIUS * THIN
     for c in range(3):
-        at = c * INNER * ROW
+        at = c * INNER * THIN
         edge_ref[c, 0:kept, :] = smooth_y[at : at + kept, :]
-        edge_ref[c, kept : 2 * kept, :] = smooth_y[at + INNER * ROW - kept : at + INNER * ROW, :]
-    peak_ref[...] = lax.fori_loop(
-        0,
-        CORE // 2,
-        lambda i, peak: smooth_rows(smooth_y, INNER, 2 * i, out_ref, 2 * i + RIM, 2, peak),
-        jnp.zeros((SIDE, WIDTH), jnp.float32),
-    )
+        edge_ref[c, kept : 2 * kept, :] = smooth_y[at + INNER * THIN - kept : at + INNER * THIN, :]
+    peak_ref[...] = peak
 
 
 def rim_kernel(
@@ -496,49 +514,34 @@
         rows = pl.ds(at * ROW, count * ROW)
         wide[rows, :] = ref[pl.ds(start * ROW, count * ROW), :].astype(jnp.float32)
         fwide[rows, :] = ref[pl.ds((RIM + start) * ROW, count * ROW), :].astype(jnp.float32)
-    chunk = stack * ROW
-
-    def by_y(i, carry):
-        rows = pl.ds(pl.multiple_of(i * chunk, ROW), chunk)
-        f = fwide[rows, :].astype(jnp.bfloat16)
-        sums_by_y(f, wide, sums, rows, bands)
-        fixed_sums(f, sums, 3, rows, bands)
-        return carry
-
-    lax.fori_loop(0, 2, by_y, 0)
     last = pl.ds(2 * RIM * ROW, 8)
     masks = [mask_rows(below_ref.at[last, :]), mask_rows(mask_ref), mask_rows(above_ref.at[last, :])]
-
-    def by_z(i, carry):
+    kept = 2 * SMOOTH_RADIUS
+    tall = RIM + kept
+    for side in range(2):
+        for c in range(3):
+            old = c * 2 * tall + side * tall + (0 if side else RIM)
+            smooth_y[pl.ds(old * THIN, kept * THIN), :] = edge_ref[c, pl.ds(side * kept * THIN, kept * THIN), :]
+        for n in range(stack // 3):
+            rows = pl.ds((side * stack + 3 * n) * ROW, 3 * ROW)
+            sums_by_y(fwide[rows, :].astype(jnp.bfloat16), wide, sums, rows, bands, True)
+    for i, count in ((0, 2), (2, 1), (3, 2)):
         for side in range(2):
             first = stack * side + i
-            if side == 0:
-                mask = jnp.where(i < SMOOTH_RADIUS, masks[0], masks[1])
-            else:
-                mask = jnp.where(i >= RIM - SMOOTH_RADIUS, masks[2], masks[1])
-            fixed = fixed_rows(sums, 3, first, [fwide[rows_at(first + BOX_RADIUS), :]], [mask])
+            mask = []
+            for t in range(i, i + count):
+                outer = t < SMOOTH_RADIUS if side == 0 else t >= RIM - SMOOTH_RADIUS
+                mask.append(masks[2 * side] if outer else masks[1])
+            here = [thin(fwide[rows_at(first + BOX_RADIUS + t), :]) for t in range(count)]
+            fixed = fixed_rows(sums, 3, first, here, mask)
             force_rows(wide, sums, first, fixed, force, i + RIM * side, 2 * RIM)
-        return carry
-
-    lax.fori_loop(0, RIM, by_z, 0)
-    kept = 2 * SMOOTH_RADIUS
-    tall = RIM + kept
-    for c in range(3):
-        f = force[pl.ds(c * 2 * RIM * ROW, 2 * RIM * ROW), :]
-        g = times(jnp.concatenate([f, f], axis=1), double)
+    peak = first_ref[...]
+    for side in range(2):
+        new = side * tall + (kept if side else 0)
+        smooth_along_y(force, side * RIM, 2 * RIM, RIM, smooth_y, new, 2 * tall, double)
+    for i, count in ((0, 2), (2, 2), (4, 1)):
         for side in range(2):
-            base = c * 2 * tall + side * tall
-            new = base + (kept if side else 0)
-            smooth_y[pl.ds(new * ROW, RIM * ROW), :] = g[side * RIM * ROW : (side + 1) * RIM * ROW]
-            old = base + (0 if side else RIM)
-            smooth_y[pl.ds(old * ROW, kept * ROW), :] = edge_ref[c, pl.ds(side * kept * ROW, kept * ROW), :]
-
-    def smooth(i, peak):
-        for side in range(2):
-            peak = smooth_rows(smooth_y, 2 * tall, tall * side + i, out_ref, (SIDE - RIM) * side + i, 1, peak)
-        return peak
-
-    peak = lax.fori_loop(0, RIM, smooth, first_ref[...])
+            peak = smooth_rows(smooth_y, 2 * tall, tall * side + i, out_ref, (SIDE - RIM) * side + i, count, peak)
     top = jnp.max(jnp.max(peak, axis=0, keepdims=True), axis=1, keepdims=True)
     peak_ref[...] = jnp.broadcast_to(top.reshape(1, 1, 1), peak_ref.shape)
 
@@ -548,7 +551,7 @@
         inner_kernel,
         out_shape=[
             jax.ShapeDtypeStruct((3 * SIDE * SIDE, WIDTH), jnp.float32),
-            jax.ShapeDtypeStruct((3, 4 * SMOOTH_RADIUS * ROW, WIDTH), jnp.float32),
+            jax.ShapeDtypeStruct((3, 4 * SMOOTH_RADIUS * THIN, WIDTH), jnp.float32),
             jax.ShapeDtypeStruct((SIDE, WIDTH), jnp.float32),
         ],
         in_specs=[in_vmem()] * 5,
@@ -556,8 +559,8 @@
         scratch_shapes=[
             pltpu.VMEM((SIDE * ROW, WIDTH), jnp.float32),
             pltpu.VMEM((3, SIDE * ROW, WIDTH), jnp.float32),
-            pltpu.VMEM((3 * INNER * ROW, WIDTH), jnp.bfloat16),
-            pltpu.VMEM((3 * INNER * ROW, WIDTH), jnp.float32),
+            pltpu.VMEM((3 * INNER * THIN, WIDTH), jnp.float32),
+            pltpu.VMEM((3 * INNER * THIN, WIDTH), jnp.float32),
         ],
         compiler_params=params(14),
         cost_estimate=cost(10_000_000_000, 8_000_000),
@@ -567,7 +570,7 @@
 
 def rim(below, above, head, tail, mask, edge, first):
     stack = 2 * (2 * RIM - 1) * ROW
-    tall = 2 * (RIM + 2 * SMOOTH_RADIUS) * ROW
+    tall = 2 * (RIM + 2 * SMOOTH_RADIUS) * THIN
     return pl.pallas_call(
         rim_kernel,
         out_shape=[
@@ -579,7 +582,7 @@
         scratch_shapes=[pltpu.VMEM((stack, WIDTH), jnp.float32)] * 2
         + [pltpu.VMEM((5, stack, WIDTH), jnp.float32)]
         + [
-            pltpu.VMEM((3 * 2 * RIM * ROW, WIDTH), jnp.bfloat16),
+            pltpu.VMEM((3 * 2 * RIM * THIN, WIDTH), jnp.float32),
             pltpu.VMEM((3 * tall, WIDTH), jnp.float32),
         ],
         compiler_params=params(14),

time: 103 us -> 99.6 us (0.967)
  Pallas kernels: 19.1 us -> 15.2 us
    pallas_call x1, Pallas kernels: 6.63 us -> 4.22 us  [inner(): pl.pallas_call(inner_kernel, out_shape=[jax.ShapeDtypeStruct((3 * SIDE *...]
  transfers between devices with their start and end apart: 6 -> 6, of which waited for: 4 -> 4; matrix products, arithmetic and copies ran while one was open for 1% -> 1% of each run, Pallas kernels for 8% -> 6%
where the time goes in v5:
time: 99.6 us; the launch traced here: 99.1 us
  blocking collectives  33.9 us (34%)
  starting transfers between devices  28.1 us (28%)
  waiting for transfers between devices  20.8 us (21%)
  Pallas kernels  15.2 us (15%)
    all_to_all x1, blocking collectives, per_device(): peak = lax.all_to_all(peak, 'slab', split_axis=0, concat_axis=0, tiled=True)  21.1 us
    all_to_all x1, blocking collectives, per_device(): peak = lax.all_to_all(peak, 'blk', split_axis=0, concat_axis=0, tiled=True)  12.9 us
    all_to_all x1, waiting for transfers between devices, per_device(): lax.all_to_all(hold(half, got), 'blk', split_axis=0, concat_axis=0, tiled...  11.8 us
    all_to_all x1, starting transfers between devices, per_device(): got = lax.all_to_all(sent, 'blk', split_axis=0, concat_axis=0, tiled=True)  10.4 us
    all_to_all x1, waiting for transfers between devices, per_device(): got = lax.all_to_all(sent, 'blk', split_axis=0, concat_axis=0, tiled=True)  8.05 us
    ppermute x1, starting transfers between devices, per_device(): below = lax.ppermute(tail, 'slab', shift_up('slab'))  5.49 us
    all_to_all x1, starting transfers between devices, per_device(): lax.all_to_all(hold(half, got), 'blk', split_axis=0, concat_axis=0, tiled...  5.35 us
    pallas_call x1, Pallas kernels, inner(): pl.pallas_call(inner_kernel, out_shape=[jax.ShapeDtypeStruct((3 * SIDE *...  4.22 us
  transfers between devices with their start and end apart: 6, of which 4 were waited for; matrix products, arithmetic and copies ran while one was open for 1% of the time, Pallas kernels for 6%

profile of v5, /device:TPU:1, one launch (start us, length us, event | category | flops | bytes accessed | tf_op | source)
XLA Modules:
  0.0 99.1 jit_solution(12915166116970227384)
XLA Ops:
  0.0 2.1 %pack.1 = bf16[32,52,128]{2,1,0:T(8,128)(2,1)} custom-call(s32[1,1,4,4]{3,2,1,0:T(4,128)} %owner_ref.1, s32[1,1,4,4]{3,2,1,0:T(4,128)} %block_ref.1, s32[1,1,4]{2,1,0:T(1,128)} %count_ref.1, s32[1,1,3,4,4]{4,3,2,1,0:T(4,128)} %bitcast.49, bf16[32,32,128]{2,1,0:T(8,128)(2,1)} %moving_ref.1), custom_call_target="tpu_custom_call" | custom-call | tf_op jit(solution)/shard_map/pack/pallas_call | solution.py:114
  2.1 10.4 %all-to-all-start = ((bf16[32,52,128]{2,1,0:T(8,128)(2,1)}), bf16[32,52,128]{2,1,0:T(8,128)(2,1)S(1)}, u32[]{:S(2)}, u32[]{:S(2)}) async-start(bf16[32,52,128]{2,1,0:T(8,128)(2,1)} %pack.1), calls=%async_computation | async-start | bytes 917504 | tf_op jit(solution)/shard_map/all_to_all | solution.py:639
  12.5 0.1 broadcast_in_dim.10
  12.6 0.1 convert_element_type.19
  12.7 2.3 %collective-permute-start = (bf16[161,128]{1,0:T(8,128)(2,1)S(1)}, bf16[161,128]{1,0:T(8,128)(2,1)S(1)}, u32[]{:S(2)}, u32[]{:S(2)}) collective-permute-start(bf16[161,128]{1,0:T(8,128)(2,1)S(1)} %get-tuple-element.35), channel_id=1, source_target_pairs={{1,0},{2,1},{3,2},{4,3},{5,4},{6,5},{7,6},{8,7},{9,8},{10,9},{11,1... | collective-permute-start | bytes 123656 | tf_op jit(solution)/shard_map/ppermute | solution.py:645
  15.0 3.3 %collective-permute-start.1 = (bf16[161,128]{1,0:T(8,128)(2,1)S(1)}, bf16[161,128]{1,0:T(8,128)(2,1)S(1)}, u32[]{:S(2)}, u32[]{:S(2)}) collective-permute-start(bf16[161,128]{1,0:T(8,128)(2,1)S(1)} %get-tuple-element.36), channel_id=1, source_target_pairs={{0,1},{1,2},{2,3},{3,4},{4,5},{5,6},{6,7},{7,8},{8,9},{9,10},{10,1... | collective-permute-start | bytes 123656 | tf_op jit(solution)/shard_map/ppermute | solution.py:644
  18.3 0.1 pad.10.clone
  18.4 0.1 collective-permute-done
  18.5 0.9 collective-permute-done.1
  19.4 0.1 maximum_bitcast_fusion
  19.5 0.2 copy.10
  19.7 8.1 %all-to-all-done.got_ref = bf16[32,52,128]{2,1,0:T(8,128)(2,1)S(1)} async-done(((bf16[32,52,128]{2,1,0:T(8,128)(2,1)}), bf16[32,52,128]{2,1,0:T(8,128)(2,1)S(1)}, u32[]{:S(2)}, u32[]{:S(2)}) %all-to-all-start) | async-done | bytes 426016 | tf_op jit(solution)/shard_map/all_to_all | solution.py:639
  27.7 3.0 %hold.1 = bf16[32,48,128]{2,1,0:T(8,128)(2,1)} custom-call(s32[1]{0:T(128)} %bitcast.half_ref, bf16[32,52,128]{2,1,0:T(8,128)(2,1)S(1)} %all-to-all-done.got_ref), custom_call_target="tpu_custom_call" | custom-call | tf_op jit(solution)/shard_map/hold/pallas_call | solution.py:250
  30.8 5.3 %all-to-all-start.1 = ((bf16[32,48,128]{2,1,0:T(8,128)(2,1)}), bf16[32,48,128]{2,1,0:T(8,128)(2,1)S(1)}, u32[]{:S(2)}, u32[]{:S(2)}) async-start(bf16[32,48,128]{2,1,0:T(8,128)(2,1)} %hold.1), calls=%async_computation.1 | async-start | bytes 786432 | tf_op jit(solution)/shard_map/all_to_all | solution.py:654
  36.3 1.8 %fixed_part.1 = (f32[1120,128]{1,0:T(8,128)S(1)}, f32[1120,128]{1,0:T(8,128)S(1)}, f32[1120,128]{1,0:T(8,128)S(1)}) custom-call(bf16[1536,128]{1,0:T(8,128)(2,1)S(1)} %bitcast.27, bf16[8,128]{1,0:T(8,128)(2,1)S(1)} %pad_maximum_fusion.8.mask_ref), custom_call_target="tpu_custom_call" | custom-call | flops 5000000000 | bytes 4000000 | tf_op jit(solution)/shard_map/fixed_part/pallas_call | solution.py:383
  38.1 11.8 %all-to-all-done.1 = bf16[32,48,128]{2,1,0:T(8,128)(2,1)S(1)} async-done(((bf16[32,48,128]{2,1,0:T(8,128)(2,1)}), bf16[32,48,128]{2,1,0:T(8,128)(2,1)S(1)}, u32[]{:S(2)}, u32[]{:S(2)}) %all-to-all-start.1) | async-done | bytes 393248 | tf_op jit(solution)/shard_map/all_to_all | solution.py:654
  49.9 0.1 concatenate.58.head_ref
  50.0 1.3 %collective-permute-start.3 = (bf16[488,128]{1,0:T(8,128)(2,1)S(1)}, bf16[488,128]{1,0:T(8,128)(2,1)S(1)}, u32[]{:S(2)}, u32[]{:S(2)}) collective-permute-start(bf16[488,128]{1,0:T(8,128)(2,1)S(1)} %concatenate.58.head_ref), channel_id=1, source_target_pairs={{32,0},{64,32},{96,64},{128,96},{160,128},{192,160},{224,192},{256... | collective-permute-start | bytes 374792 | tf_op jit(solution)/shard_map/ppermute | solution.py:667
  51.4 5.5 %collective-permute-start.2 = (bf16[488,128]{1,0:T(8,128)(2,1)S(1)}, bf16[488,128]{1,0:T(8,128)(2,1)S(1)}, u32[]{:S(2)}, u32[]{:S(2)}) collective-permute-start(bf16[488,128]{1,0:T(8,128)(2,1)S(1)} %concatenate.52.tail_ref), channel_id=1, source_target_pairs={{0,32},{32,64},{64,96},{96,128},{128,160},{160,192},{192,224},{224... | collective-permute-start | bytes 374792 | tf_op jit(solution)/shard_map/ppermute | solution.py:666
  56.9 4.2 %inner.1 = (f32[3072,128]{1,0:T(8,128)S(1)}, f32[3,480,128]{2,1,0:T(8,128)S(1)}, f32[32,128]{1,0:T(8,128)S(1)}) custom-call(bf16[1536,128]{1,0:T(8,128)(2,1)S(1)} %bitcast.26, bf16[1536,128]{1,0:T(8,128)(2,1)S(1)} %bitcast.28, f32[1120,128]{1,0:T(8,128)S(1)} %get-tuple-element.13.mean_ref, f32[1120,128]{1,0:T(8,128)S(1)} %get-tuple-element.14.away_ref, ...), custom_call_target="tpu_custom_call" | custom-call | flops 10000000000 | bytes 8000000 | tf_op jit(solution)/shard_map/inner/pallas_call | solution.py:550
  61.1 2.3 %rim.1 = (f32[3072,128]{1,0:T(8,128)S(1)}, f32[32,1,128]{2,1,0:T(1,128)S(1)}) custom-call(bf16[488,128]{1,0:T(8,128)(2,1)S(1)} %collective-permute-done.2.below_ref, bf16[488,128]{1,0:T(8,128)(2,1)S(1)} %collective-permute-done.3.above_ref, bf16[488,128]{1,0:T(8,128)(2,1)S(1)} %concatenate.58.head_ref, bf16[488,128]{1,0:T(8,128)(2,1)S(1)} %concatenate.52.tail_ref, ...), custom_call_target="tpu_custom_call" | custom-call | tf_op jit(solution)/shard_map/rim/pallas_call | solution.py:574
  63.4 12.9 %all_to_all.20.in_ref = f32[32,1,128]{2,1,0:T(1,128)S(1)} all-to-all(f32[32,1,128]{2,1,0:T(1,128)S(1)} %get-tuple-element.18), channel_id=1, replica_groups=mesh['slab'=16,'blk'=32] {'blk'}, dimensions={0} | all-to-all | bytes 32768 | tf_op jit(solution)/shard_map/all_to_all | solution.py:670
  76.3 21.1 %all_to_all.21.peaks_ref = f32[16,1,128]{2,1,0:T(1,128)S(1)} all-to-all(f32[16,1,128]{2,1,0:T(1,128)S(1)} %relay.1), channel_id=1, replica_groups=mesh['slab'=16,'blk'=32] {'slab'}, dimensions={0} | all-to-all | bytes 16384 | tf_op jit(solution)/shard_map/all_to_all | solution.py:672
  97.4 1.7 %finish.1 = f32[3,32,32,128]{3,2,1,0:T(8,128)} custom-call(f32[16,1,128]{2,1,0:T(1,128)S(1)} %all_to_all.21.peaks_ref, f32[3072,128]{1,0:T(8,128)S(1)} %get-tuple-element.19.core_ref, f32[3072,128]{1,0:T(8,128)S(1)} %get-tuple-element.20.rim_ref), custom_call_target="tpu_custom_call" | custom-call | tf_op jit(solution)/shard_map/finish/pallas_call | solution.py:625
  (28 shorter events, 0.3 us)
Async XLA Ops:
  0.0 12.5 %copy-start.1 = (s32[1,1,4]{2,1,0:T(1,128)S(1)}, s32[1,1,4]{2,1,0:T(1,128)}, u32[]{:S(2)}) copy-start(s32[1,1,4]{2,1,0:T(1,128)} %param.13) | copy-start | bytes 52
  0.0 12.7 %copy-start = (bf16[32,32,128]{2,1,0:T(8,128)(2,1)S(1)}, bf16[32,32,128]{2,1,0:T(8,128)(2,1)}, u32[]{:S(2)}) copy-start(bf16[32,32,128]{2,1,0:T(8,128)(2,1)} %param.7) | copy-start | bytes 786436
  2.1 25.6 %all-to-all-start = ((bf16[32,52,128]{2,1,0:T(8,128)(2,1)}), bf16[32,52,128]{2,1,0:T(8,128)(2,1)S(1)}, u32[]{:S(2)}, u32[]{:S(2)}) async-start(bf16[32,52,128]{2,1,0:T(8,128)(2,1)} %pack.1), calls=%async_computation | async-start | bytes 917504 | tf_op jit(solution)/shard_map/all_to_all | solution.py:639
  12.7 5.8 %collective-permute-start = (bf16[161,128]{1,0:T(8,128)(2,1)S(1)}, bf16[161,128]{1,0:T(8,128)(2,1)S(1)}, u32[]{:S(2)}, u32[]{:S(2)}) collective-permute-start(bf16[161,128]{1,0:T(8,128)(2,1)S(1)} %get-tuple-element.35), channel_id=1, source_target_pairs={{1,0},{2,1},{3,2},{4,3},{5,4},{6,5},{7,6},{8,7},{9,8},{10,9},{11,1... | collective-permute-start | bytes 123656 | tf_op jit(solution)/shard_map/ppermute | solution.py:645
  15.0 4.4 %collective-permute-start.1 = (bf16[161,128]{1,0:T(8,128)(2,1)S(1)}, bf16[161,128]{1,0:T(8,128)(2,1)S(1)}, u32[]{:S(2)}, u32[]{:S(2)}) collective-permute-start(bf16[161,128]{1,0:T(8,128)(2,1)S(1)} %get-tuple-element.36), channel_id=1, source_target_pairs={{0,1},{1,2},{2,3},{3,4},{4,5},{5,6},{6,7},{7,8},{8,9},{9,10},{10,1... | collective-permute-start | bytes 123656 | tf_op jit(solution)/shard_map/ppermute | solution.py:644
  30.8 19.1 %all-to-all-start.1 = ((bf16[32,48,128]{2,1,0:T(8,128)(2,1)}), bf16[32,48,128]{2,1,0:T(8,128)(2,1)S(1)}, u32[]{:S(2)}, u32[]{:S(2)}) async-start(bf16[32,48,128]{2,1,0:T(8,128)(2,1)} %hold.1), calls=%async_computation.1 | async-start | bytes 786432 | tf_op jit(solution)/shard_map/all_to_all | solution.py:654
  50.0 11.1 %collective-permute-start.3 = (bf16[488,128]{1,0:T(8,128)(2,1)S(1)}, bf16[488,128]{1,0:T(8,128)(2,1)S(1)}, u32[]{:S(2)}, u32[]{:S(2)}) collective-permute-start(bf16[488,128]{1,0:T(8,128)(2,1)S(1)} %concatenate.58.head_ref), channel_id=1, source_target_pairs={{32,0},{64,32},{96,64},{128,96},{160,128},{192,160},{224,192},{256... | collective-permute-start | bytes 374792 | tf_op jit(solution)/shard_map/ppermute | solution.py:667
  51.4 9.7 %collective-permute-start.2 = (bf16[488,128]{1,0:T(8,128)(2,1)S(1)}, bf16[488,128]{1,0:T(8,128)(2,1)S(1)}, u32[]{:S(2)}, u32[]{:S(2)}) collective-permute-start(bf16[488,128]{1,0:T(8,128)(2,1)S(1)} %concatenate.52.tail_ref), channel_id=1, source_target_pairs={{0,32},{32,64},{64,96},{96,128},{128,160},{160,192},{192,224},{224... | collective-permute-start | bytes 374792 | tf_op jit(solution)/shard_map/ppermute | solution.py:666

commit v6 on v5

--- a/solution.py
+++ b/solution.py
@@ -53,6 +53,7 @@
 ROW = OUT_PITCH
 THIN = 40
 MIB = 1 << 20
+STEP_X = 8
 
 
 def params(mib):
@@ -67,11 +68,15 @@
     return pl.BlockSpec(memory_space=pltpu.VMEM)
 
 
+def in_place():
+    return pl.BlockSpec(memory_space=pl.ANY)
+
+
 def in_smem():
     return pl.BlockSpec(memory_space=pltpu.SMEM)
 
 
-def pack_kernel(owner_ref, block_ref, count_ref, level_ref, moving_ref, out_ref, wide):
+def pack_kernel(owner_ref, block_ref, count_ref, level_ref, moving_ref, out_ref, wide, block, sems):
     lane = lax.broadcasted_iota(jnp.int32, (TAKEN + 1, WIDTH), 1)
     row = jnp.zeros((TAKEN + 1, WIDTH), jnp.int32)
     e = BLOCKS * SLOTS
@@ -88,17 +93,13 @@
     for x in range(SIDE):
         wide[pl.ds(x * SIDE, SIDE), :] = moving_ref[x].astype(jnp.float32)
     place = lax.broadcasted_iota(jnp.int32, (TAKEN + 1, WIDTH), 0)
-    for z in range(SIDE):
-        plane = wide[pl.ds(z, SIDE, stride=SIDE), :].astype(jnp.bfloat16)
-        spots = [(z // DEEP, z % DEEP)]
-        if z % DEEP == 0 and z > 0:
-            spots.append((z // DEEP - 1, DEEP))
-        if z == SIDE - 1:
-            spots.append((z // DEEP, DEEP))
-        for pair, at in spots:
+    copies = []
+    for pair in range(SIDE // DEEP):
+        for at in range(TAKEN):
+            z = min(pair * DEEP + at, SIDE - 1)
+            plane = wide[pl.ds(z, SIDE, stride=SIDE), :].astype(jnp.bfloat16)
             for half in range(2):
-                out_ref[pair * 2 + half, at * HALF : (at + 1) * HALF, :] = plane[half * HALF : (half + 1) * HALF]
-    for pair in range(SIDE // DEEP):
+                block[pair * 2 + half, at * HALF : (at + 1) * HALF, :] = plane[half * HALF : (half + 1) * HALF]
         for half in range(2):
             x = min((half + 1) * HALF, SIDE - 1)
             if pair < SIDE // DEEP - 1:
@@ -107,7 +108,13 @@
                 two = wide[pl.ds(x * SIDE + pair * DEEP, DEEP), :]
                 extra = jnp.concatenate([two, two[1:2], two[1:2]], axis=0)
             extra = jnp.where(place == TAKEN, row, extra)
-            out_ref[pair * 2 + half, TAKEN * HALF : SENT, :] = extra.astype(jnp.bfloat16)
+            block[pair * 2 + half, TAKEN * HALF : SENT, :] = extra.astype(jnp.bfloat16)
+        if pair % 4 == 3:
+            at = pl.ds((pair - 3) * 2, 8)
+            copies.append(pltpu.make_async_copy(block.at[at], out_ref.at[at], sems.at[len(copies)]))
+            copies[-1].start()
+    for copy in copies:
+        copy.wait()
 
 
 def pack(owner, block, count, level, moving):
@@ -115,8 +122,12 @@
         pack_kernel,
         out_shape=jax.ShapeDtypeStruct((OWNERS, SENT, WIDTH), jnp.bfloat16),
         in_specs=[in_smem()] * 4 + [in_vmem()],
-        out_specs=in_vmem(),
-        scratch_shapes=[pltpu.VMEM((SIDE * SIDE, WIDTH), jnp.float32)],
+        out_specs=in_place(),
+        scratch_shapes=[
+            pltpu.VMEM((SIDE * SIDE, WIDTH), jnp.float32),
+            pltpu.VMEM((OWNERS, SENT, WIDTH), jnp.bfloat16),
+            pltpu.SemaphoreType.DMA((4,)),
+        ],
         name="pack",
     )(owner, block, count, level, moving)
 
@@ -140,7 +151,7 @@
     return jnp.broadcast_to(a[:, i : i + 1], a.shape)
 
 
-def hold_kernel(half_ref, got_ref, out_ref, wide, source, coef, mixed, spread):
+def hold_kernel(half_ref, got_ref, out_ref, wide, source, coef, mixed, spread, block, sems):
     strip = HALF // BLOCKS
     rows = OWNERS * BLOCKS
     lane = lax.broadcasted_iota(jnp.int32, (OWNERS, WIDTH), 1)
@@ -240,8 +251,15 @@
                 w = spread[pl.ds(OUT_PITCH + z * PART + HALF - RIM + k, OWNERS, stride=OUT_PITCH), :]
                 spread[pl.ds(2 * OUT_PITCH + z * PART + PART - RIM + k, OWNERS, stride=OUT_PITCH), :] = w
 
+    copies = []
     for r in range(OWNERS):
-        out_ref[r] = spread[pl.ds((r + 1) * OUT_PITCH, OUT_PITCH), :].astype(jnp.bfloat16)
+        block[r] = spread[pl.ds((r + 1) * OUT_PITCH, OUT_PITCH), :].astype(jnp.bfloat16)
+        if r % STEP_X == STEP_X - 1:
+            at = pl.ds(r + 1 - STEP_X, STEP_X)
+            copies.append(pltpu.make_async_copy(block.at[at], out_ref.at[at], sems.at[len(copies)]))
+            copies[-1].start()
+    for copy in copies:
+        copy.wait()
 
 
 def hold(half, got):
@@ -251,13 +269,15 @@
         hold_kernel,
         out_shape=jax.ShapeDtypeStruct((OWNERS, OUT_PITCH, WIDTH), jnp.bfloat16),
         in_specs=[in_smem(), in_vmem()],
-        out_specs=in_vmem(),
+        out_specs=in_place(),
         scratch_shapes=[
             pltpu.VMEM((OWNERS * PITCH, WIDTH), jnp.float32),
             pltpu.VMEM((2 * rows, TAKEN * (strip + 1) * WIDTH), jnp.bfloat16),
             pltpu.VMEM((4, 2 * rows, 2 * rows), jnp.bfloat16),
             pltpu.VMEM((rows, DEEP * strip * WIDTH), jnp.float32),
             pltpu.VMEM(((OWNERS + 2) * OUT_PITCH, WIDTH), jnp.float32),
+            pltpu.VMEM((OWNERS, OUT_PITCH, WIDTH), jnp.bfloat16),
+            pltpu.SemaphoreType.DMA((OWNERS // STEP_X,)),
         ],
         compiler_params=params(12),
         name="hold",
@@ -606,28 +626,34 @@
     )(tiles)
 
 
-STEP_X = 8
-
-
-def finish_kernel(peaks_ref, core_ref, rim_ref, out_ref):
-    x0 = pl.program_id(0) * STEP_X
+def finish_kernel(peaks_ref, core_ref, rim_ref, out_ref, block, sems):
     peak = jnp.sqrt(jnp.max(peaks_ref[...].reshape(peaks_ref.shape[0], WIDTH), axis=0, keepdims=True))
-    scale = step_length / (peak + peak_eps)
+    scale = jnp.broadcast_to(step_length / (peak + peak_eps), (SIDE, WIDTH))
     z = lax.broadcasted_iota(jnp.int32, (SIDE, WIDTH), 0)
     at_rim = (z < RIM) | (z >= SIDE - RIM)
+    copies = []
     for c in range(3):
-        for x in range(STEP_X):
-            rows = pl.ds(pl.multiple_of((c * SIDE + x0 + x) * SIDE, SIDE), SIDE)
-            out_ref[c, x] = jnp.where(at_rim, rim_ref[rows, :], core_ref[rows, :]) * scale
+        for part in range(SIDE // STEP_X):
+            for x in range(part * STEP_X, (part + 1) * STEP_X):
+                rows = pl.ds((c * SIDE + x) * SIDE, SIDE)
+                block[c, x] = jnp.where(at_rim, rim_ref[rows, :], core_ref[rows, :]) * scale
+            at = pl.ds(part * STEP_X, STEP_X)
+            copies.append(pltpu.make_async_copy(block.at[c, at], out_ref.at[c, at], sems.at[len(copies)]))
+            copies[-1].start()
+    for copy in copies:
+        copy.wait()
 
 
 def finish(peaks, core, rims):
     return pl.pallas_call(
         finish_kernel,
         out_shape=jax.ShapeDtypeStruct((3, SIDE, SIDE, WIDTH), jnp.float32),
-        grid=(SIDE // STEP_X,),
         in_specs=[in_vmem()] * 3,
-        out_specs=pl.BlockSpec((3, STEP_X, SIDE, WIDTH), lambda i: (0, i, 0, 0)),
+        out_specs=in_place(),
+        scratch_shapes=[
+            pltpu.VMEM((3, SIDE, SIDE, WIDTH), jnp.float32),
+            pltpu.SemaphoreType.DMA((3 * SIDE // STEP_X,)),
+        ],
         compiler_params=params(12),
         name="finish",
     )(peaks, core, rims)

time: 99.6 us -> 99.1 us (level)
  no operation moved by 1% of the time
where the time goes in v6:
time: 99.1 us; the launch traced here: 98.6 us
  blocking collectives  33.9 us (34%)
  starting transfers between devices  28.1 us (28%)
  waiting for transfers between devices  20.8 us (21%)
  Pallas kernels  14.7 us (15%)
    all_to_all x1, blocking collectives, per_device(): peak = lax.all_to_all(peak, 'slab', split_axis=0, concat_axis=0, tiled=True)  21.1 us
    all_to_all x1, blocking collectives, per_device(): peak = lax.all_to_all(peak, 'blk', split_axis=0, concat_axis=0, tiled=True)  12.9 us
    all_to_all x1, waiting for transfers between devices, per_device(): lax.all_to_all(hold(half, got), 'blk', split_axis=0, concat_axis=0, tiled...  11.8 us
    all_to_all x1, starting transfers between devices, per_device(): got = lax.all_to_all(sent, 'blk', split_axis=0, concat_axis=0, tiled=True)  10.4 us
    all_to_all x1, waiting for transfers between devices, per_device(): got = lax.all_to_all(sent, 'blk', split_axis=0, concat_axis=0, tiled=True)  8.05 us
    ppermute x1, starting transfers between devices, per_device(): below = lax.ppermute(tail, 'slab', shift_up('slab'))  5.49 us
    all_to_all x1, starting transfers between devices, per_device(): lax.all_to_all(hold(half, got), 'blk', split_axis=0, concat_axis=0, tiled...  5.37 us
    pallas_call x1, Pallas kernels, inner(): pl.pallas_call(inner_kernel, out_shape=[jax.ShapeDtypeStruct((3 * SIDE *...  4.22 us
  transfers between devices with their start and end apart: 6, of which 4 were waited for; matrix products, arithmetic and copies ran while one was open for 1% of the time, Pallas kernels for 6%

profile of v6, /device:TPU:1, one launch (start us, length us, event | category | flops | bytes accessed | tf_op | source)
XLA Modules:
  0.0 98.6 jit_solution(14169071105722133531)
XLA Ops:
  0.0 2.1 %pack.1 = bf16[32,52,128]{2,1,0:T(8,128)(2,1)} custom-call(s32[1,1,4,4]{3,2,1,0:T(4,128)} %owner_ref.1, s32[1,1,4,4]{3,2,1,0:T(4,128)} %block_ref.1, s32[1,1,4]{2,1,0:T(1,128)} %count_ref.1, s32[1,1,3,4,4]{4,3,2,1,0:T(4,128)} %bitcast.49, bf16[32,32,128]{2,1,0:T(8,128)(2,1)} %moving_ref.1), custom_call_target="tpu_custom_call" | custom-call | tf_op jit(solution)/shard_map/pack/pallas_call | solution.py:121
  2.1 10.4 %all-to-all-start = ((bf16[32,52,128]{2,1,0:T(8,128)(2,1)}), bf16[32,52,128]{2,1,0:T(8,128)(2,1)S(1)}, u32[]{:S(2)}, u32[]{:S(2)}) async-start(bf16[32,52,128]{2,1,0:T(8,128)(2,1)} %pack.1), calls=%async_computation | async-start | bytes 917504 | tf_op jit(solution)/shard_map/all_to_all | solution.py:665
  12.5 0.1 broadcast_in_dim.10
  12.6 0.1 convert_element_type.19
  12.7 2.3 %collective-permute-start = (bf16[161,128]{1,0:T(8,128)(2,1)S(1)}, bf16[161,128]{1,0:T(8,128)(2,1)S(1)}, u32[]{:S(2)}, u32[]{:S(2)}) collective-permute-start(bf16[161,128]{1,0:T(8,128)(2,1)S(1)} %get-tuple-element.35), channel_id=1, source_target_pairs={{1,0},{2,1},{3,2},{4,3},{5,4},{6,5},{7,6},{8,7},{9,8},{10,9},{11,1... | collective-permute-start | bytes 123656 | tf_op jit(solution)/shard_map/ppermute | solution.py:671
  14.9 3.3 %collective-permute-start.1 = (bf16[161,128]{1,0:T(8,128)(2,1)S(1)}, bf16[161,128]{1,0:T(8,128)(2,1)S(1)}, u32[]{:S(2)}, u32[]{:S(2)}) collective-permute-start(bf16[161,128]{1,0:T(8,128)(2,1)S(1)} %get-tuple-element.36), channel_id=1, source_target_pairs={{0,1},{1,2},{2,3},{3,4},{4,5},{5,6},{6,7},{7,8},{8,9},{9,10},{10,1... | collective-permute-start | bytes 123656 | tf_op jit(solution)/shard_map/ppermute | solution.py:670
  18.3 0.1 pad.10.clone
  18.4 0.1 collective-permute-done
  18.5 0.9 collective-permute-done.1
  19.4 0.1 maximum_bitcast_fusion
  19.5 0.2 copy.10
  19.6 8.1 %all-to-all-done.got_ref = bf16[32,52,128]{2,1,0:T(8,128)(2,1)S(1)} async-done(((bf16[32,52,128]{2,1,0:T(8,128)(2,1)}), bf16[32,52,128]{2,1,0:T(8,128)(2,1)S(1)}, u32[]{:S(2)}, u32[]{:S(2)}) %all-to-all-start) | async-done | bytes 426016 | tf_op jit(solution)/shard_map/all_to_all | solution.py:665
  27.7 3.0 %hold.1 = bf16[32,48,128]{2,1,0:T(8,128)(2,1)} custom-call(s32[1]{0:T(128)} %bitcast.half_ref, bf16[32,52,128]{2,1,0:T(8,128)(2,1)S(1)} %all-to-all-done.got_ref), custom_call_target="tpu_custom_call" | custom-call | tf_op jit(solution)/shard_map/hold/pallas_call | solution.py:268
  30.7 5.4 %all-to-all-start.1 = ((bf16[32,48,128]{2,1,0:T(8,128)(2,1)}), bf16[32,48,128]{2,1,0:T(8,128)(2,1)S(1)}, u32[]{:S(2)}, u32[]{:S(2)}) async-start(bf16[32,48,128]{2,1,0:T(8,128)(2,1)} %hold.1), calls=%async_computation.1 | async-start | bytes 786432 | tf_op jit(solution)/shard_map/all_to_all | solution.py:680
  36.2 1.8 %fixed_part.1 = (f32[1120,128]{1,0:T(8,128)S(1)}, f32[1120,128]{1,0:T(8,128)S(1)}, f32[1120,128]{1,0:T(8,128)S(1)}) custom-call(bf16[1536,128]{1,0:T(8,128)(2,1)S(1)} %bitcast.27, bf16[8,128]{1,0:T(8,128)(2,1)S(1)} %pad_maximum_fusion.8.mask_ref), custom_call_target="tpu_custom_call" | custom-call | flops 5000000000 | bytes 4000000 | tf_op jit(solution)/shard_map/fixed_part/pallas_call | solution.py:403
  38.0 11.8 %all-to-all-done.1 = bf16[32,48,128]{2,1,0:T(8,128)(2,1)S(1)} async-done(((bf16[32,48,128]{2,1,0:T(8,128)(2,1)}), bf16[32,48,128]{2,1,0:T(8,128)(2,1)S(1)}, u32[]{:S(2)}, u32[]{:S(2)}) %all-to-all-start.1) | async-done | bytes 393248 | tf_op jit(solution)/shard_map/all_to_all | solution.py:680
  49.9 0.1 concatenate.58.head_ref
  50.0 1.3 %collective-permute-start.3 = (bf16[488,128]{1,0:T(8,128)(2,1)S(1)}, bf16[488,128]{1,0:T(8,128)(2,1)S(1)}, u32[]{:S(2)}, u32[]{:S(2)}) collective-permute-start(bf16[488,128]{1,0:T(8,128)(2,1)S(1)} %concatenate.58.head_ref), channel_id=1, source_target_pairs={{32,0},{64,32},{96,64},{128,96},{160,128},{192,160},{224,192},{256... | collective-permute-start | bytes 374792 | tf_op jit(solution)/shard_map/ppermute | solution.py:693
  51.4 5.5 %collective-permute-start.2 = (bf16[488,128]{1,0:T(8,128)(2,1)S(1)}, bf16[488,128]{1,0:T(8,128)(2,1)S(1)}, u32[]{:S(2)}, u32[]{:S(2)}) collective-permute-start(bf16[488,128]{1,0:T(8,128)(2,1)S(1)} %concatenate.52.tail_ref), channel_id=1, source_target_pairs={{0,32},{32,64},{64,96},{96,128},{128,160},{160,192},{192,224},{224... | collective-permute-start | bytes 374792 | tf_op jit(solution)/shard_map/ppermute | solution.py:692
  56.9 4.2 %inner.1 = (f32[3072,128]{1,0:T(8,128)S(1)}, f32[3,480,128]{2,1,0:T(8,128)S(1)}, f32[32,128]{1,0:T(8,128)S(1)}) custom-call(bf16[1536,128]{1,0:T(8,128)(2,1)S(1)} %bitcast.26, bf16[1536,128]{1,0:T(8,128)(2,1)S(1)} %bitcast.28, f32[1120,128]{1,0:T(8,128)S(1)} %get-tuple-element.13.mean_ref, f32[1120,128]{1,0:T(8,128)S(1)} %get-tuple-element.14.away_ref, ...), custom_call_target="tpu_custom_call" | custom-call | flops 10000000000 | bytes 8000000 | tf_op jit(solution)/shard_map/inner/pallas_call | solution.py:570
  61.1 2.3 %rim.1 = (f32[3072,128]{1,0:T(8,128)S(1)}, f32[32,1,128]{2,1,0:T(1,128)S(1)}) custom-call(bf16[488,128]{1,0:T(8,128)(2,1)S(1)} %collective-permute-done.2.below_ref, bf16[488,128]{1,0:T(8,128)(2,1)S(1)} %collective-permute-done.3.above_ref, bf16[488,128]{1,0:T(8,128)(2,1)S(1)} %concatenate.58.head_ref, bf16[488,128]{1,0:T(8,128)(2,1)S(1)} %concatenate.52.tail_ref, ...), custom_call_target="tpu_custom_call" | custom-call | tf_op jit(solution)/shard_map/rim/pallas_call | solution.py:594
  63.4 12.9 %all_to_all.20.in_ref = f32[32,1,128]{2,1,0:T(1,128)S(1)} all-to-all(f32[32,1,128]{2,1,0:T(1,128)S(1)} %get-tuple-element.18), channel_id=1, replica_groups=mesh['slab'=16,'blk'=32] {'blk'}, dimensions={0} | all-to-all | bytes 32768 | tf_op jit(solution)/shard_map/all_to_all | solution.py:696
  76.3 21.1 %all_to_all.21.peaks_ref = f32[16,1,128]{2,1,0:T(1,128)S(1)} all-to-all(f32[16,1,128]{2,1,0:T(1,128)S(1)} %relay.1), channel_id=1, replica_groups=mesh['slab'=16,'blk'=32] {'slab'}, dimensions={0} | all-to-all | bytes 16384 | tf_op jit(solution)/shard_map/all_to_all | solution.py:698
  97.4 1.3 %finish.1 = f32[3,32,32,128]{3,2,1,0:T(8,128)} custom-call(f32[16,1,128]{2,1,0:T(1,128)S(1)} %all_to_all.21.peaks_ref, f32[3072,128]{1,0:T(8,128)S(1)} %get-tuple-element.19.core_ref, f32[3072,128]{1,0:T(8,128)S(1)} %get-tuple-element.20.rim_ref), custom_call_target="tpu_custom_call" | custom-call | tf_op jit(solution)/shard_map/finish/pallas_call | solution.py:648
  (28 shorter events, 0.3 us)
Async XLA Ops:
  0.0 12.5 %copy-start.1 = (s32[1,1,4]{2,1,0:T(1,128)S(1)}, s32[1,1,4]{2,1,0:T(1,128)}, u32[]{:S(2)}) copy-start(s32[1,1,4]{2,1,0:T(1,128)} %param.13) | copy-start | bytes 52
  0.0 12.6 %copy-start = (bf16[32,32,128]{2,1,0:T(8,128)(2,1)S(1)}, bf16[32,32,128]{2,1,0:T(8,128)(2,1)}, u32[]{:S(2)}) copy-start(bf16[32,32,128]{2,1,0:T(8,128)(2,1)} %param.7) | copy-start | bytes 786436
  2.1 25.6 %all-to-all-start = ((bf16[32,52,128]{2,1,0:T(8,128)(2,1)}), bf16[32,52,128]{2,1,0:T(8,128)(2,1)S(1)}, u32[]{:S(2)}, u32[]{:S(2)}) async-start(bf16[32,52,128]{2,1,0:T(8,128)(2,1)} %pack.1), calls=%async_computation | async-start | bytes 917504 | tf_op jit(solution)/shard_map/all_to_all | solution.py:665
  12.7 5.8 %collective-permute-start = (bf16[161,128]{1,0:T(8,128)(2,1)S(1)}, bf16[161,128]{1,0:T(8,128)(2,1)S(1)}, u32[]{:S(2)}, u32[]{:S(2)}) collective-permute-start(bf16[161,128]{1,0:T(8,128)(2,1)S(1)} %get-tuple-element.35), channel_id=1, source_target_pairs={{1,0},{2,1},{3,2},{4,3},{5,4},{6,5},{7,6},{8,7},{9,8},{10,9},{11,1... | collective-permute-start | bytes 123656 | tf_op jit(solution)/shard_map/ppermute | solution.py:671
  14.9 4.4 %collective-permute-start.1 = (bf16[161,128]{1,0:T(8,128)(2,1)S(1)}, bf16[161,128]{1,0:T(8,128)(2,1)S(1)}, u32[]{:S(2)}, u32[]{:S(2)}) collective-permute-start(bf16[161,128]{1,0:T(8,128)(2,1)S(1)} %get-tuple-element.36), channel_id=1, source_target_pairs={{0,1},{1,2},{2,3},{3,4},{4,5},{5,6},{6,7},{7,8},{8,9},{9,10},{10,1... | collective-permute-start | bytes 123656 | tf_op jit(solution)/shard_map/ppermute | solution.py:670
  30.7 19.1 %all-to-all-start.1 = ((bf16[32,48,128]{2,1,0:T(8,128)(2,1)}), bf16[32,48,128]{2,1,0:T(8,128)(2,1)S(1)}, u32[]{:S(2)}, u32[]{:S(2)}) async-start(bf16[32,48,128]{2,1,0:T(8,128)(2,1)} %hold.1), calls=%async_computation.1 | async-start | bytes 786432 | tf_op jit(solution)/shard_map/all_to_all | solution.py:680
  50.0 11.1 %collective-permute-start.3 = (bf16[488,128]{1,0:T(8,128)(2,1)S(1)}, bf16[488,128]{1,0:T(8,128)(2,1)S(1)}, u32[]{:S(2)}, u32[]{:S(2)}) collective-permute-start(bf16[488,128]{1,0:T(8,128)(2,1)S(1)} %concatenate.58.head_ref), channel_id=1, source_target_pairs={{32,0},{64,32},{96,64},{128,96},{160,128},{192,160},{224,192},{256... | collective-permute-start | bytes 374792 | tf_op jit(solution)/shard_map/ppermute | solution.py:693
  51.4 9.7 %collective-permute-start.2 = (bf16[488,128]{1,0:T(8,128)(2,1)S(1)}, bf16[488,128]{1,0:T(8,128)(2,1)S(1)}, u32[]{:S(2)}, u32[]{:S(2)}) collective-permute-start(bf16[488,128]{1,0:T(8,128)(2,1)S(1)} %concatenate.52.tail_ref), channel_id=1, source_target_pairs={{0,32},{32,64},{64,96},{96,128},{128,160},{160,192},{192,224},{224... | collective-permute-start | bytes 374792 | tf_op jit(solution)/shard_map/ppermute | solution.py:692

commit v7 on v6

--- a/solution.py
+++ b/solution.py
@@ -5,7 +5,7 @@
 from jax import lax
 from jax.experimental import pallas as pl
 from jax.experimental.pallas import tpu as pltpu
-from jax.sharding import PartitionSpec as P
+from jax.sharding import Mesh, PartitionSpec as P
 
 LEVELS = 8
 BOX_RADIUS = 2
@@ -595,7 +595,7 @@
         rim_kernel,
         out_shape=[
             jax.ShapeDtypeStruct((3 * SIDE * SIDE, WIDTH), jnp.float32),
-            jax.ShapeDtypeStruct((OWNERS, 1, WIDTH), jnp.float32),
+            jax.ShapeDtypeStruct((16, 1, WIDTH), jnp.float32),
         ],
         in_specs=[in_vmem()] * 7,
         out_specs=[in_vmem()] * 2,
@@ -659,16 +659,22 @@
     )(peaks, core, rims)
 
 
+SLAB = ("z", "h")
+BLK = ("y", "l", "c")
+NEAR = ("y", "l")
+FAR = ("z", "h", "c")
+
+
 def per_device(fixed_image, moving_image, fetch_owner, fetch_block, fetch_count, interp_level, block_mask):
     side, width = SIDE, WIDTH
     sent = pack(fetch_owner, fetch_block, fetch_count, interp_level.transpose(0, 1, 3, 2, 4), moving_image)
-    got = lax.all_to_all(sent, "blk", split_axis=0, concat_axis=0, tiled=True)
+    got = lax.all_to_all(sent, BLK, split_axis=0, concat_axis=0, tiled=True)
 
     mask_row = jnp.repeat(block_mask.reshape(BLOCKS), side).astype(jnp.bfloat16)[None]
     last = jnp.concatenate([fixed_image[side - RIM :].reshape(-1, width), mask_row], axis=0)
     first = jnp.concatenate([fixed_image[:RIM].reshape(-1, width), mask_row], axis=0)
-    left = lax.ppermute(last, "blk", shift_up("blk"))
-    right = lax.ppermute(first, "blk", shift_down("blk"))
+    left = lax.ppermute(last, BLK, shift_up(BLK))
+    right = lax.ppermute(first, BLK, shift_down(BLK))
     turn = lambda a: a[:-1].reshape(RIM, side, width)
     fixed = jnp.concatenate(
         [fixed_image, turn(right), jnp.zeros((ROW - EXT, side, width), jnp.bfloat16), turn(left)], axis=0
@@ -676,8 +682,8 @@
     masks = jnp.concatenate([mask_row, right[-1:], left[-1:], jnp.zeros((5, width), jnp.bfloat16)], axis=0)
     mean, away, gain = fixed_part(fixed.reshape(side * ROW, width), masks)
 
-    half = (lax.axis_index("blk") % 2).astype(jnp.int32).reshape(1)
-    warped = lax.all_to_all(hold(half, got), "blk", split_axis=0, concat_axis=0, tiled=True)
+    half = (lax.axis_index(BLK) % 2).astype(jnp.int32).reshape(1)
+    warped = lax.all_to_all(hold(half, got), BLK, split_axis=0, concat_axis=0, tiled=True)
 
     def z_rows(pairs):
         part = warped.reshape(side // DEEP, 2, DEEP, PART, width)[pairs]
@@ -689,26 +695,27 @@
 
     tail = message(z_rows(slice(side // DEEP - 3, None))[1:], fixed[side - RIM :])
     head = message(z_rows(slice(0, 3))[:RIM], fixed[:RIM])
-    below = lax.ppermute(tail, "slab", shift_up("slab"))
-    above = lax.ppermute(head, "slab", shift_down("slab"))
+    below = lax.ppermute(tail, SLAB, shift_up(SLAB))
+    above = lax.ppermute(head, SLAB, shift_down(SLAB))
     core, edge, top = inner(warped.reshape(side * ROW, width), fixed.reshape(side * ROW, width), mean, away, gain)
     rims, peak = rim(below, above, head, tail, masks, edge, top)
-    peak = lax.all_to_all(peak, "blk", split_axis=0, concat_axis=0, tiled=True)
-    peak = relay(peak, lax.axis_size("slab"))
-    peak = lax.all_to_all(peak, "slab", split_axis=0, concat_axis=0, tiled=True)
+    peak = lax.all_to_all(peak, NEAR, split_axis=0, concat_axis=0, tiled=True)
+    peak = relay(peak, 32)
+    peak = lax.all_to_all(peak, FAR, split_axis=0, concat_axis=0, tiled=True)
     return finish(peak, core, rims)
 
 
 def solution(mesh):
+    fine = Mesh(mesh.devices.reshape(8, 2, 8, 2, 2), SLAB + BLK)
     in_specs = (
-        P("blk", "slab", None),
-        P("blk", "slab", None),
-        P("blk", "slab", None, None),
-        P("blk", "slab", None, None),
-        P("blk", "slab", None),
-        P("blk", "slab", None, None, None),
-        P("blk", "slab", None),
+        P(BLK, SLAB, None),
+        P(BLK, SLAB, None),
+        P(BLK, SLAB, None, None),
+        P(BLK, SLAB, None, None),
+        P(BLK, SLAB, None),
+        P(BLK, SLAB, None, None, None),
+        P(BLK, SLAB, None),
     )
     return jax.shard_map(
-        per_device, mesh=mesh, in_specs=in_specs, out_specs=P(None, "blk", "slab", None), check_vma=False
+        per_device, mesh=fine, in_specs=in_specs, out_specs=P(None, BLK, SLAB, None), check_vma=False
     )

time: 99.1 us -> 101 us (1.019)
  blocking collectives: 33.9 us -> 35.4 us
    all_to_all x2, blocking collectives: 33.9 us -> 35.4 us  [the longest x1 24.6 us: per_device(): peak = lax.all_to_all(peak, FAR, split_axis=0, concat_axis=0, tiled=True)]
where the time goes in v7:
time: 101 us; the launch traced here: 100 us
  blocking collectives  35.4 us (35%)
  starting transfers between devices  28.1 us (28%)
  waiting for transfers between devices  20.8 us (21%)
  Pallas kernels  14.8 us (15%)
    all_to_all x1, blocking collectives, per_device(): peak = lax.all_to_all(peak, FAR, split_axis=0, concat_axis=0, tiled=True)  24.6 us
    all_to_all x1, waiting for transfers between devices, per_device(): lax.all_to_all(hold(half, got), BLK, split_axis=0, concat_axis=0, tiled=T...  11.8 us
    all_to_all x1, blocking collectives, per_device(): peak = lax.all_to_all(peak, NEAR, split_axis=0, concat_axis=0, tiled=True)  10.7 us
    all_to_all x1, starting transfers between devices, per_device(): got = lax.all_to_all(sent, BLK, split_axis=0, concat_axis=0, tiled=True)  10.4 us
    all_to_all x1, waiting for transfers between devices, per_device(): got = lax.all_to_all(sent, BLK, split_axis=0, concat_axis=0, tiled=True)  8.05 us
    ppermute x1, starting transfers between devices, per_device(): below = lax.ppermute(tail, SLAB, shift_up(SLAB))  5.49 us
    all_to_all x1, starting transfers between devices, per_device(): lax.all_to_all(hold(half, got), BLK, split_axis=0, concat_axis=0, tiled=T...  5.36 us
    pallas_call x1, Pallas kernels, inner(): pl.pallas_call(inner_kernel, out_shape=[jax.ShapeDtypeStruct((3 * SIDE *...  4.25 us
  transfers between devices with their start and end apart: 6, of which 4 were waited for; matrix products, arithmetic and copies ran while one was open for 1% of the time, Pallas kernels for 6%

profile of v7, /device:TPU:1, one launch (start us, length us, event | category | flops | bytes accessed | tf_op | source)
XLA Modules:
  0.0 100.1 jit_solution(17345394426349776028)
XLA Ops:
  0.0 2.1 %pack.1 = bf16[32,52,128]{2,1,0:T(8,128)(2,1)} custom-call(s32[1,1,4,4]{3,2,1,0:T(4,128)} %owner_ref.1, s32[1,1,4,4]{3,2,1,0:T(4,128)} %block_ref.1, s32[1,1,4]{2,1,0:T(1,128)} %count_ref.1, s32[1,1,3,4,4]{4,3,2,1,0:T(4,128)} %bitcast.49, bf16[32,32,128]{2,1,0:T(8,128)(2,1)} %moving_ref.1), custom_call_target="tpu_custom_call" | custom-call | tf_op jit(solution)/shard_map/pack/pallas_call | solution.py:121
  2.1 10.4 %all-to-all-start = ((bf16[32,52,128]{2,1,0:T(8,128)(2,1)}), bf16[32,52,128]{2,1,0:T(8,128)(2,1)S(1)}, u32[]{:S(2)}, u32[]{:S(2)}) async-start(bf16[32,52,128]{2,1,0:T(8,128)(2,1)} %pack.1), calls=%async_computation | async-start | bytes 917504 | tf_op jit(solution)/shard_map/all_to_all | solution.py:671
  12.5 0.1 broadcast_in_dim.10
  12.6 0.1 convert_element_type.19
  12.7 2.3 %collective-permute-start = (bf16[161,128]{1,0:T(8,128)(2,1)S(1)}, bf16[161,128]{1,0:T(8,128)(2,1)S(1)}, u32[]{:S(2)}, u32[]{:S(2)}) collective-permute-start(bf16[161,128]{1,0:T(8,128)(2,1)S(1)} %get-tuple-element.35), channel_id=1, source_target_pairs={{1,0},{2,1},{3,2},{4,3},{5,4},{6,5},{7,6},{8,7},{9,8},{10,9},{11,1... | collective-permute-start | bytes 123656 | tf_op jit(solution)/shard_map/ppermute | solution.py:677
  14.9 3.3 %collective-permute-start.1 = (bf16[161,128]{1,0:T(8,128)(2,1)S(1)}, bf16[161,128]{1,0:T(8,128)(2,1)S(1)}, u32[]{:S(2)}, u32[]{:S(2)}) collective-permute-start(bf16[161,128]{1,0:T(8,128)(2,1)S(1)} %get-tuple-element.36), channel_id=1, source_target_pairs={{0,1},{1,2},{2,3},{3,4},{4,5},{5,6},{6,7},{7,8},{8,9},{9,10},{10,1... | collective-permute-start | bytes 123656 | tf_op jit(solution)/shard_map/ppermute | solution.py:676
  18.3 0.1 pad.10.clone
  18.4 0.1 collective-permute-done
  18.5 0.9 collective-permute-done.1
  19.4 0.1 maximum_bitcast_fusion
  19.5 0.2 copy.10
  19.6 8.1 %all-to-all-done.got_ref = bf16[32,52,128]{2,1,0:T(8,128)(2,1)S(1)} async-done(((bf16[32,52,128]{2,1,0:T(8,128)(2,1)}), bf16[32,52,128]{2,1,0:T(8,128)(2,1)S(1)}, u32[]{:S(2)}, u32[]{:S(2)}) %all-to-all-start) | async-done | bytes 426016 | tf_op jit(solution)/shard_map/all_to_all | solution.py:671
  27.7 3.0 %hold.1 = bf16[32,48,128]{2,1,0:T(8,128)(2,1)} custom-call(s32[1]{0:T(128)} %bitcast.half_ref, bf16[32,52,128]{2,1,0:T(8,128)(2,1)S(1)} %all-to-all-done.got_ref), custom_call_target="tpu_custom_call" | custom-call | tf_op jit(solution)/shard_map/hold/pallas_call | solution.py:268
  30.7 5.4 %all-to-all-start.1 = ((bf16[32,48,128]{2,1,0:T(8,128)(2,1)}), bf16[32,48,128]{2,1,0:T(8,128)(2,1)S(1)}, u32[]{:S(2)}, u32[]{:S(2)}) async-start(bf16[32,48,128]{2,1,0:T(8,128)(2,1)} %hold.1), calls=%async_computation.1 | async-start | bytes 786432 | tf_op jit(solution)/shard_map/all_to_all | solution.py:686
  36.2 1.8 %fixed_part.1 = (f32[1120,128]{1,0:T(8,128)S(1)}, f32[1120,128]{1,0:T(8,128)S(1)}, f32[1120,128]{1,0:T(8,128)S(1)}) custom-call(bf16[1536,128]{1,0:T(8,128)(2,1)S(1)} %bitcast.27, bf16[8,128]{1,0:T(8,128)(2,1)S(1)} %pad_maximum_fusion.8.mask_ref), custom_call_target="tpu_custom_call" | custom-call | flops 5000000000 | bytes 4000000 | tf_op jit(solution)/shard_map/fixed_part/pallas_call | solution.py:403
  38.0 11.8 %all-to-all-done.1 = bf16[32,48,128]{2,1,0:T(8,128)(2,1)S(1)} async-done(((bf16[32,48,128]{2,1,0:T(8,128)(2,1)}), bf16[32,48,128]{2,1,0:T(8,128)(2,1)S(1)}, u32[]{:S(2)}, u32[]{:S(2)}) %all-to-all-start.1) | async-done | bytes 393248 | tf_op jit(solution)/shard_map/all_to_all | solution.py:686
  49.9 0.1 concatenate.58.head_ref
  50.0 1.3 %collective-permute-start.3 = (bf16[488,128]{1,0:T(8,128)(2,1)S(1)}, bf16[488,128]{1,0:T(8,128)(2,1)S(1)}, u32[]{:S(2)}, u32[]{:S(2)}) collective-permute-start(bf16[488,128]{1,0:T(8,128)(2,1)S(1)} %concatenate.58.head_ref), channel_id=1, source_target_pairs={{32,0},{64,32},{96,64},{128,96},{160,128},{192,160},{224,192},{256... | collective-permute-start | bytes 374792 | tf_op jit(solution)/shard_map/ppermute | solution.py:699
  51.3 5.5 %collective-permute-start.2 = (bf16[488,128]{1,0:T(8,128)(2,1)S(1)}, bf16[488,128]{1,0:T(8,128)(2,1)S(1)}, u32[]{:S(2)}, u32[]{:S(2)}) collective-permute-start(bf16[488,128]{1,0:T(8,128)(2,1)S(1)} %concatenate.52.tail_ref), channel_id=1, source_target_pairs={{0,32},{32,64},{64,96},{96,128},{128,160},{160,192},{192,224},{224... | collective-permute-start | bytes 374792 | tf_op jit(solution)/shard_map/ppermute | solution.py:698
  56.8 4.2 %inner.1 = (f32[3072,128]{1,0:T(8,128)S(1)}, f32[3,480,128]{2,1,0:T(8,128)S(1)}, f32[32,128]{1,0:T(8,128)S(1)}) custom-call(bf16[1536,128]{1,0:T(8,128)(2,1)S(1)} %bitcast.26, bf16[1536,128]{1,0:T(8,128)(2,1)S(1)} %bitcast.28, f32[1120,128]{1,0:T(8,128)S(1)} %get-tuple-element.13.mean_ref, f32[1120,128]{1,0:T(8,128)S(1)} %get-tuple-element.14.away_ref, ...), custom_call_target="tpu_custom_call" | custom-call | flops 10000000000 | bytes 8000000 | tf_op jit(solution)/shard_map/inner/pallas_call | solution.py:570
  61.1 2.3 %rim.1 = (f32[3072,128]{1,0:T(8,128)S(1)}, f32[16,1,128]{2,1,0:T(1,128)S(1)}) custom-call(bf16[488,128]{1,0:T(8,128)(2,1)S(1)} %collective-permute-done.2.below_ref, bf16[488,128]{1,0:T(8,128)(2,1)S(1)} %collective-permute-done.3.above_ref, bf16[488,128]{1,0:T(8,128)(2,1)S(1)} %concatenate.58.head_ref, bf16[488,128]{1,0:T(8,128)(2,1)S(1)} %concatenate.52.tail_ref, ...), custom_call_target="tpu_custom_call" | custom-call | tf_op jit(solution)/shard_map/rim/pallas_call | solution.py:594
  63.5 10.7 %all_to_all.20.in_ref = f32[16,1,128]{2,1,0:T(1,128)S(1)} all-to-all(f32[16,1,128]{2,1,0:T(1,128)S(1)} %get-tuple-element.18), channel_id=1, replica_groups=mesh['z'=8,'h'=2,'y'=8,'l'=2,'c'=2] {'y','l'}, dimensions={0} | all-to-all | bytes 16384 | tf_op jit(solution)/shard_map/all_to_all | solution.py:702
  74.2 24.6 %all_to_all.21.peaks_ref = f32[32,1,128]{2,1,0:T(1,128)S(1)} all-to-all(f32[32,1,128]{2,1,0:T(1,128)S(1)} %relay.1), channel_id=1, replica_groups=mesh['z'=8,'h'=2,'y'=8,'l'=2,'c'=2] {'z','h','c'}, dimensions={0} | all-to-all | bytes 32768 | tf_op jit(solution)/shard_map/all_to_all | solution.py:704
  98.9 1.3 %finish.1 = f32[3,32,32,128]{3,2,1,0:T(8,128)} custom-call(f32[32,1,128]{2,1,0:T(1,128)S(1)} %all_to_all.21.peaks_ref, f32[3072,128]{1,0:T(8,128)S(1)} %get-tuple-element.19.core_ref, f32[3072,128]{1,0:T(8,128)S(1)} %get-tuple-element.20.rim_ref), custom_call_target="tpu_custom_call" | custom-call | tf_op jit(solution)/shard_map/finish/pallas_call | solution.py:648
  (28 shorter events, 0.3 us)
Async XLA Ops:
  0.0 12.5 %copy-start.1 = (s32[1,1,4]{2,1,0:T(1,128)S(1)}, s32[1,1,4]{2,1,0:T(1,128)}, u32[]{:S(2)}) copy-start(s32[1,1,4]{2,1,0:T(1,128)} %param.13) | copy-start | bytes 52
  0.0 12.6 %copy-start = (bf16[32,32,128]{2,1,0:T(8,128)(2,1)S(1)}, bf16[32,32,128]{2,1,0:T(8,128)(2,1)}, u32[]{:S(2)}) copy-start(bf16[32,32,128]{2,1,0:T(8,128)(2,1)} %param.7) | copy-start | bytes 786436
  2.1 25.6 %all-to-all-start = ((bf16[32,52,128]{2,1,0:T(8,128)(2,1)}), bf16[32,52,128]{2,1,0:T(8,128)(2,1)S(1)}, u32[]{:S(2)}, u32[]{:S(2)}) async-start(bf16[32,52,128]{2,1,0:T(8,128)(2,1)} %pack.1), calls=%async_computation | async-start | bytes 917504 | tf_op jit(solution)/shard_map/all_to_all | solution.py:671
  12.7 5.8 %collective-permute-start = (bf16[161,128]{1,0:T(8,128)(2,1)S(1)}, bf16[161,128]{1,0:T(8,128)(2,1)S(1)}, u32[]{:S(2)}, u32[]{:S(2)}) collective-permute-start(bf16[161,128]{1,0:T(8,128)(2,1)S(1)} %get-tuple-element.35), channel_id=1, source_target_pairs={{1,0},{2,1},{3,2},{4,3},{5,4},{6,5},{7,6},{8,7},{9,8},{10,9},{11,1... | collective-permute-start | bytes 123656 | tf_op jit(solution)/shard_map/ppermute | solution.py:677
  14.9 4.4 %collective-permute-start.1 = (bf16[161,128]{1,0:T(8,128)(2,1)S(1)}, bf16[161,128]{1,0:T(8,128)(2,1)S(1)}, u32[]{:S(2)}, u32[]{:S(2)}) collective-permute-start(bf16[161,128]{1,0:T(8,128)(2,1)S(1)} %get-tuple-element.36), channel_id=1, source_target_pairs={{0,1},{1,2},{2,3},{3,4},{4,5},{5,6},{6,7},{7,8},{8,9},{9,10},{10,1... | collective-permute-start | bytes 123656 | tf_op jit(solution)/shard_map/ppermute | solution.py:676
  30.7 19.1 %all-to-all-start.1 = ((bf16[32,48,128]{2,1,0:T(8,128)(2,1)}), bf16[32,48,128]{2,1,0:T(8,128)(2,1)S(1)}, u32[]{:S(2)}, u32[]{:S(2)}) async-start(bf16[32,48,128]{2,1,0:T(8,128)(2,1)} %hold.1), calls=%async_computation.1 | async-start | bytes 786432 | tf_op jit(solution)/shard_map/all_to_all | solution.py:686
  50.0 11.1 %collective-permute-start.3 = (bf16[488,128]{1,0:T(8,128)(2,1)S(1)}, bf16[488,128]{1,0:T(8,128)(2,1)S(1)}, u32[]{:S(2)}, u32[]{:S(2)}) collective-permute-start(bf16[488,128]{1,0:T(8,128)(2,1)S(1)} %concatenate.58.head_ref), channel_id=1, source_target_pairs={{32,0},{64,32},{96,64},{128,96},{160,128},{192,160},{224,192},{256... | collective-permute-start | bytes 374792 | tf_op jit(solution)/shard_map/ppermute | solution.py:699
  51.3 9.8 %collective-permute-start.2 = (bf16[488,128]{1,0:T(8,128)(2,1)S(1)}, bf16[488,128]{1,0:T(8,128)(2,1)S(1)}, u32[]{:S(2)}, u32[]{:S(2)}) collective-permute-start(bf16[488,128]{1,0:T(8,128)(2,1)S(1)} %concatenate.52.tail_ref), channel_id=1, source_target_pairs={{0,32},{32,64},{64,96},{96,128},{128,160},{160,192},{192,224},{224... | collective-permute-start | bytes 374792 | tf_op jit(solution)/shard_map/ppermute | solution.py:698

commit v8 on v6

--- a/solution.py
+++ b/solution.py
@@ -447,12 +447,12 @@
             force[thin_at(c * pitch + k + t), :] = term * steps[c]
 
 
-def smooth_rows(smooth_y, pitch, i, out_ref, z, count, peak):
+def smooth_rows(row, i, out_ref, z, count, peak):
     taps = smooth_weights(SMOOTH_RADIUS)[SMOOTH_RADIUS:]
     mid = SMOOTH_RADIUS
     total = [None] * count
     for c in range(3):
-        g = [smooth_y[thin_at(c * pitch + i + t), :] for t in range(2 * SMOOTH_RADIUS + count)]
+        g = [row(c, i + t) for t in range(2 * SMOOTH_RADIUS + count)]
         for n in range(count):
             s = taps[0] * g[n + mid]
             for t in range(1, SMOOTH_RADIUS + 1):
@@ -507,7 +507,9 @@
             force_rows(wide, sums, i, fixed, force, i, INNER)
         smooth_along_y(force, n * step, INNER, step, smooth_y, n * step, INNER, double)
         while done + 1 + 2 * SMOOTH_RADIUS < (n + 1) * step:
-            peak = smooth_rows(smooth_y, INNER, done, out_ref, done + RIM, 2, peak)
+            peak = smooth_rows(
+                lambda c, i: smooth_y[thin_at(c * INNER + i), :], done, out_ref, done + RIM, 2, peak
+            )
             done += 2
     kept = 2 * SMOOTH_RADIUS * THIN
     for c in range(3):
@@ -539,9 +541,6 @@
     kept = 2 * SMOOTH_RADIUS
     tall = RIM + kept
     for side in range(2):
-        for c in range(3):
-            old = c * 2 * tall + side * tall + (0 if side else RIM)
-            smooth_y[pl.ds(old * THIN, kept * THIN), :] = edge_ref[c, pl.ds(side * kept * THIN, kept * THIN), :]
         for n in range(stack // 3):
             rows = pl.ds((side * stack + 3 * n) * ROW, 3 * ROW)
             sums_by_y(fwide[rows, :].astype(jnp.bfloat16), wide, sums, rows, bands, True)
@@ -557,11 +556,17 @@
             force_rows(wide, sums, first, fixed, force, i + RIM * side, 2 * RIM)
     peak = first_ref[...]
     for side in range(2):
-        new = side * tall + (kept if side else 0)
-        smooth_along_y(force, side * RIM, 2 * RIM, RIM, smooth_y, new, 2 * tall, double)
+        smooth_along_y(force, side * RIM, 2 * RIM, RIM, smooth_y, side * RIM, 2 * RIM, double)
+
+    def row(c, i):
+        side, j = i // tall, i % tall
+        if side == 0 and j >= RIM or side == 1 and j < kept:
+            return edge_ref[c, thin_at(j - RIM if side == 0 else kept + j), :]
+        return smooth_y[thin_at(c * 2 * RIM + (j if side == 0 else RIM + j - kept)), :]
+
     for i, count in ((0, 2), (2, 2), (4, 1)):
         for side in range(2):
-            peak = smooth_rows(smooth_y, 2 * tall, tall * side + i, out_ref, (SIDE - RIM) * side + i, count, peak)
+            peak = smooth_rows(row, tall * side + i, out_ref, (SIDE - RIM) * side + i, count, peak)
     top = jnp.max(jnp.max(peak, axis=0, keepdims=True), axis=1, keepdims=True)
     peak_ref[...] = jnp.broadcast_to(top.reshape(1, 1, 1), peak_ref.shape)
 
@@ -590,7 +595,7 @@
 
 def rim(below, above, head, tail, mask, edge, first):
     stack = 2 * (2 * RIM - 1) * ROW
-    tall = 2 * (RIM + 2 * SMOOTH_RADIUS) * THIN
+    tall = 2 * RIM * THIN
     return pl.pallas_call(
         rim_kernel,
         out_shape=[

time: 99.1 us -> 99.1 us (level)
  no operation moved by 1% of the time
where the time goes in v8:
time: 99.1 us; the launch traced here: 98.6 us
  blocking collectives  33.9 us (34%)
  starting transfers between devices  28.1 us (28%)
  waiting for transfers between devices  20.8 us (21%)
  Pallas kernels  14.7 us (15%)
    all_to_all x1, blocking collectives, per_device(): peak = lax.all_to_all(peak, 'slab', split_axis=0, concat_axis=0, tiled=True)  21.1 us
    all_to_all x1, blocking collectives, per_device(): peak = lax.all_to_all(peak, 'blk', split_axis=0, concat_axis=0, tiled=True)  12.8 us
    all_to_all x1, waiting for transfers between devices, per_device(): lax.all_to_all(hold(half, got), 'blk', split_axis=0, concat_axis=0, tiled...  11.8 us
    all_to_all x1, starting transfers between devices, per_device(): got = lax.all_to_all(sent, 'blk', split_axis=0, concat_axis=0, tiled=True)  10.4 us
    all_to_all x1, waiting for transfers between devices, per_device(): got = lax.all_to_all(sent, 'blk', split_axis=0, concat_axis=0, tiled=True)  8.05 us
    ppermute x1, starting transfers between devices, per_device(): below = lax.ppermute(tail, 'slab', shift_up('slab'))  5.49 us
    all_to_all x1, starting transfers between devices, per_device(): lax.all_to_all(hold(half, got), 'blk', split_axis=0, concat_axis=0, tiled...  5.37 us
    pallas_call x1, Pallas kernels, inner(): pl.pallas_call(inner_kernel, out_shape=[jax.ShapeDtypeStruct((3 * SIDE *...  4.22 us
  transfers between devices with their start and end apart: 6, of which 4 were waited for; matrix products, arithmetic and copies ran while one was open for 1% of the time, Pallas kernels for 6%

profile of v8, /device:TPU:1, one launch (start us, length us, event | category | flops | bytes accessed | tf_op | source)
XLA Modules:
  0.0 98.6 jit_solution(16350436906537882584)
XLA Ops:
  0.0 2.1 %pack.1 = bf16[32,52,128]{2,1,0:T(8,128)(2,1)} custom-call(s32[1,1,4,4]{3,2,1,0:T(4,128)} %owner_ref.1, s32[1,1,4,4]{3,2,1,0:T(4,128)} %block_ref.1, s32[1,1,4]{2,1,0:T(1,128)} %count_ref.1, s32[1,1,3,4,4]{4,3,2,1,0:T(4,128)} %bitcast.49, bf16[32,32,128]{2,1,0:T(8,128)(2,1)} %moving_ref.1), custom_call_target="tpu_custom_call" | custom-call | tf_op jit(solution)/shard_map/pack/pallas_call | solution.py:121
  2.1 10.4 %all-to-all-start = ((bf16[32,52,128]{2,1,0:T(8,128)(2,1)}), bf16[32,52,128]{2,1,0:T(8,128)(2,1)S(1)}, u32[]{:S(2)}, u32[]{:S(2)}) async-start(bf16[32,52,128]{2,1,0:T(8,128)(2,1)} %pack.1), calls=%async_computation | async-start | bytes 917504 | tf_op jit(solution)/shard_map/all_to_all | solution.py:670
  12.5 0.1 broadcast_in_dim.10
  12.6 0.1 convert_element_type.19
  12.7 2.3 %collective-permute-start = (bf16[161,128]{1,0:T(8,128)(2,1)S(1)}, bf16[161,128]{1,0:T(8,128)(2,1)S(1)}, u32[]{:S(2)}, u32[]{:S(2)}) collective-permute-start(bf16[161,128]{1,0:T(8,128)(2,1)S(1)} %get-tuple-element.35), channel_id=1, source_target_pairs={{1,0},{2,1},{3,2},{4,3},{5,4},{6,5},{7,6},{8,7},{9,8},{10,9},{11,1... | collective-permute-start | bytes 123656 | tf_op jit(solution)/shard_map/ppermute | solution.py:676
  14.9 3.3 %collective-permute-start.1 = (bf16[161,128]{1,0:T(8,128)(2,1)S(1)}, bf16[161,128]{1,0:T(8,128)(2,1)S(1)}, u32[]{:S(2)}, u32[]{:S(2)}) collective-permute-start(bf16[161,128]{1,0:T(8,128)(2,1)S(1)} %get-tuple-element.36), channel_id=1, source_target_pairs={{0,1},{1,2},{2,3},{3,4},{4,5},{5,6},{6,7},{7,8},{8,9},{9,10},{10,1... | collective-permute-start | bytes 123656 | tf_op jit(solution)/shard_map/ppermute | solution.py:675
  18.3 0.1 pad.10.clone
  18.4 0.1 collective-permute-done
  18.5 0.9 collective-permute-done.1
  19.4 0.1 maximum_bitcast_fusion
  19.5 0.2 copy.10
  19.6 8.1 %all-to-all-done.got_ref = bf16[32,52,128]{2,1,0:T(8,128)(2,1)S(1)} async-done(((bf16[32,52,128]{2,1,0:T(8,128)(2,1)}), bf16[32,52,128]{2,1,0:T(8,128)(2,1)S(1)}, u32[]{:S(2)}, u32[]{:S(2)}) %all-to-all-start) | async-done | bytes 426016 | tf_op jit(solution)/shard_map/all_to_all | solution.py:670
  27.7 3.0 %hold.1 = bf16[32,48,128]{2,1,0:T(8,128)(2,1)} custom-call(s32[1]{0:T(128)} %bitcast.half_ref, bf16[32,52,128]{2,1,0:T(8,128)(2,1)S(1)} %all-to-all-done.got_ref), custom_call_target="tpu_custom_call" | custom-call | tf_op jit(solution)/shard_map/hold/pallas_call | solution.py:268
  30.7 5.4 %all-to-all-start.1 = ((bf16[32,48,128]{2,1,0:T(8,128)(2,1)}), bf16[32,48,128]{2,1,0:T(8,128)(2,1)S(1)}, u32[]{:S(2)}, u32[]{:S(2)}) async-start(bf16[32,48,128]{2,1,0:T(8,128)(2,1)} %hold.1), calls=%async_computation.1 | async-start | bytes 786432 | tf_op jit(solution)/shard_map/all_to_all | solution.py:685
  36.2 1.8 %fixed_part.1 = (f32[1120,128]{1,0:T(8,128)S(1)}, f32[1120,128]{1,0:T(8,128)S(1)}, f32[1120,128]{1,0:T(8,128)S(1)}) custom-call(bf16[1536,128]{1,0:T(8,128)(2,1)S(1)} %bitcast.27, bf16[8,128]{1,0:T(8,128)(2,1)S(1)} %pad_maximum_fusion.8.mask_ref), custom_call_target="tpu_custom_call" | custom-call | flops 5000000000 | bytes 4000000 | tf_op jit(solution)/shard_map/fixed_part/pallas_call | solution.py:403
  38.0 11.8 %all-to-all-done.1 = bf16[32,48,128]{2,1,0:T(8,128)(2,1)S(1)} async-done(((bf16[32,48,128]{2,1,0:T(8,128)(2,1)}), bf16[32,48,128]{2,1,0:T(8,128)(2,1)S(1)}, u32[]{:S(2)}, u32[]{:S(2)}) %all-to-all-start.1) | async-done | bytes 393248 | tf_op jit(solution)/shard_map/all_to_all | solution.py:685
  49.9 0.1 concatenate.58.head_ref
  50.0 1.3 %collective-permute-start.3 = (bf16[488,128]{1,0:T(8,128)(2,1)S(1)}, bf16[488,128]{1,0:T(8,128)(2,1)S(1)}, u32[]{:S(2)}, u32[]{:S(2)}) collective-permute-start(bf16[488,128]{1,0:T(8,128)(2,1)S(1)} %concatenate.58.head_ref), channel_id=1, source_target_pairs={{32,0},{64,32},{96,64},{128,96},{160,128},{192,160},{224,192},{256... | collective-permute-start | bytes 374792 | tf_op jit(solution)/shard_map/ppermute | solution.py:698
  51.4 5.5 %collective-permute-start.2 = (bf16[488,128]{1,0:T(8,128)(2,1)S(1)}, bf16[488,128]{1,0:T(8,128)(2,1)S(1)}, u32[]{:S(2)}, u32[]{:S(2)}) collective-permute-start(bf16[488,128]{1,0:T(8,128)(2,1)S(1)} %concatenate.52.tail_ref), channel_id=1, source_target_pairs={{0,32},{32,64},{64,96},{96,128},{128,160},{160,192},{192,224},{224... | collective-permute-start | bytes 374792 | tf_op jit(solution)/shard_map/ppermute | solution.py:697
  56.9 4.2 %inner.1 = (f32[3072,128]{1,0:T(8,128)S(1)}, f32[3,480,128]{2,1,0:T(8,128)S(1)}, f32[32,128]{1,0:T(8,128)S(1)}) custom-call(bf16[1536,128]{1,0:T(8,128)(2,1)S(1)} %bitcast.26, bf16[1536,128]{1,0:T(8,128)(2,1)S(1)} %bitcast.28, f32[1120,128]{1,0:T(8,128)S(1)} %get-tuple-element.13.mean_ref, f32[1120,128]{1,0:T(8,128)S(1)} %get-tuple-element.14.away_ref, ...), custom_call_target="tpu_custom_call" | custom-call | flops 10000000000 | bytes 8000000 | tf_op jit(solution)/shard_map/inner/pallas_call | solution.py:575
  61.1 2.3 %rim.1 = (f32[3072,128]{1,0:T(8,128)S(1)}, f32[32,1,128]{2,1,0:T(1,128)S(1)}) custom-call(bf16[488,128]{1,0:T(8,128)(2,1)S(1)} %collective-permute-done.2.below_ref, bf16[488,128]{1,0:T(8,128)(2,1)S(1)} %collective-permute-done.3.above_ref, bf16[488,128]{1,0:T(8,128)(2,1)S(1)} %concatenate.58.head_ref, bf16[488,128]{1,0:T(8,128)(2,1)S(1)} %concatenate.52.tail_ref, ...), custom_call_target="tpu_custom_call" | custom-call | tf_op jit(solution)/shard_map/rim/pallas_call | solution.py:599
  63.4 12.8 %all_to_all.20.in_ref = f32[32,1,128]{2,1,0:T(1,128)S(1)} all-to-all(f32[32,1,128]{2,1,0:T(1,128)S(1)} %get-tuple-element.18), channel_id=1, replica_groups=mesh['slab'=16,'blk'=32] {'blk'}, dimensions={0} | all-to-all | bytes 32768 | tf_op jit(solution)/shard_map/all_to_all | solution.py:701
  76.3 21.1 %all_to_all.21.peaks_ref = f32[16,1,128]{2,1,0:T(1,128)S(1)} all-to-all(f32[16,1,128]{2,1,0:T(1,128)S(1)} %relay.1), channel_id=1, replica_groups=mesh['slab'=16,'blk'=32] {'slab'}, dimensions={0} | all-to-all | bytes 16384 | tf_op jit(solution)/shard_map/all_to_all | solution.py:703
  97.4 1.3 %finish.1 = f32[3,32,32,128]{3,2,1,0:T(8,128)} custom-call(f32[16,1,128]{2,1,0:T(1,128)S(1)} %all_to_all.21.peaks_ref, f32[3072,128]{1,0:T(8,128)S(1)} %get-tuple-element.19.core_ref, f32[3072,128]{1,0:T(8,128)S(1)} %get-tuple-element.20.rim_ref), custom_call_target="tpu_custom_call" | custom-call | tf_op jit(solution)/shard_map/finish/pallas_call | solution.py:653
  (28 shorter events, 0.3 us)
Async XLA Ops:
  0.0 12.5 %copy-start.1 = (s32[1,1,4]{2,1,0:T(1,128)S(1)}, s32[1,1,4]{2,1,0:T(1,128)}, u32[]{:S(2)}) copy-start(s32[1,1,4]{2,1,0:T(1,128)} %param.13) | copy-start | bytes 52
  0.0 12.6 %copy-start = (bf16[32,32,128]{2,1,0:T(8,128)(2,1)S(1)}, bf16[32,32,128]{2,1,0:T(8,128)(2,1)}, u32[]{:S(2)}) copy-start(bf16[32,32,128]{2,1,0:T(8,128)(2,1)} %param.7) | copy-start | bytes 786436
  2.1 25.6 %all-to-all-start = ((bf16[32,52,128]{2,1,0:T(8,128)(2,1)}), bf16[32,52,128]{2,1,0:T(8,128)(2,1)S(1)}, u32[]{:S(2)}, u32[]{:S(2)}) async-start(bf16[32,52,128]{2,1,0:T(8,128)(2,1)} %pack.1), calls=%async_computation | async-start | bytes 917504 | tf_op jit(solution)/shard_map/all_to_all | solution.py:670
  12.7 5.8 %collective-permute-start = (bf16[161,128]{1,0:T(8,128)(2,1)S(1)}, bf16[161,128]{1,0:T(8,128)(2,1)S(1)}, u32[]{:S(2)}, u32[]{:S(2)}) collective-permute-start(bf16[161,128]{1,0:T(8,128)(2,1)S(1)} %get-tuple-element.35), channel_id=1, source_target_pairs={{1,0},{2,1},{3,2},{4,3},{5,4},{6,5},{7,6},{8,7},{9,8},{10,9},{11,1... | collective-permute-start | bytes 123656 | tf_op jit(solution)/shard_map/ppermute | solution.py:676
  14.9 4.4 %collective-permute-start.1 = (bf16[161,128]{1,0:T(8,128)(2,1)S(1)}, bf16[161,128]{1,0:T(8,128)(2,1)S(1)}, u32[]{:S(2)}, u32[]{:S(2)}) collective-permute-start(bf16[161,128]{1,0:T(8,128)(2,1)S(1)} %get-tuple-element.36), channel_id=1, source_target_pairs={{0,1},{1,2},{2,3},{3,4},{4,5},{5,6},{6,7},{7,8},{8,9},{9,10},{10,1... | collective-permute-start | bytes 123656 | tf_op jit(solution)/shard_map/ppermute | solution.py:675
  30.7 19.1 %all-to-all-start.1 = ((bf16[32,48,128]{2,1,0:T(8,128)(2,1)}), bf16[32,48,128]{2,1,0:T(8,128)(2,1)S(1)}, u32[]{:S(2)}, u32[]{:S(2)}) async-start(bf16[32,48,128]{2,1,0:T(8,128)(2,1)} %hold.1), calls=%async_computation.1 | async-start | bytes 786432 | tf_op jit(solution)/shard_map/all_to_all | solution.py:685
  50.0 11.1 %collective-permute-start.3 = (bf16[488,128]{1,0:T(8,128)(2,1)S(1)}, bf16[488,128]{1,0:T(8,128)(2,1)S(1)}, u32[]{:S(2)}, u32[]{:S(2)}) collective-permute-start(bf16[488,128]{1,0:T(8,128)(2,1)S(1)} %concatenate.58.head_ref), channel_id=1, source_target_pairs={{32,0},{64,32},{96,64},{128,96},{160,128},{192,160},{224,192},{256... | collective-permute-start | bytes 374792 | tf_op jit(solution)/shard_map/ppermute | solution.py:698
  51.4 9.7 %collective-permute-start.2 = (bf16[488,128]{1,0:T(8,128)(2,1)S(1)}, bf16[488,128]{1,0:T(8,128)(2,1)S(1)}, u32[]{:S(2)}, u32[]{:S(2)}) collective-permute-start(bf16[488,128]{1,0:T(8,128)(2,1)S(1)} %concatenate.52.tail_ref), channel_id=1, source_target_pairs={{0,32},{32,64},{64,96},{96,128},{128,160},{160,192},{192,224},{224... | collective-permute-start | bytes 374792 | tf_op jit(solution)/shard_map/ppermute | solution.py:697
